TPU v7x, 128 devices: a whole 4x4x4 slice. The times are simulated.
128 devices in a mesh: arc: 16 (over z, y_lo, core), col: 8 (over x, y_hi).
Axes of the slice: x: 4, y: 4 (y_hi: 2, y_lo: 2; y = y_hi * 2 + y_lo), z: 4, core: 2. Of those that a mesh axis runs over, the one named last changes fastest.
Arguments:
- design: bfloat16 [24576, 5120], P('arc', 'col'), may hold values from -0.109375 to 0.109375
- local_design: float32 [16, 24576], P(None, 'arc'), may hold values from -6 to 6
- observed: float32 [24576], P('arc'), may hold values from -6 to 6
- valid_mask: int32 [24576], P('arc'), may hold values 0 or 1
- counts: int32 [128], P('arc'), may hold values from 1 to 192, 15360 in all
Outputs:
- normal: float32 [5120, 5120], P('arc', 'col')
- rhs: float32 [5120], P('col')
Inputs may be any that keep to these rules, and one draw needn't show every extreme that they name: Arc a holds counts[a] recorded slots at its start; the rest are padding.
All inputs are finite; a program needn't handle non-finite values. No bound on the sum of `valid_mask` or of `counts` on one device may be relied on, other than what follows from the above.
Results may differ from a plain program's by a relative error of at most 0.0028.
Values may be sent and summed in bfloat16 or wider, within the bound.
No kernel may reach another device: no remote copies, remote signals or barrier semaphores. Data moves between devices by JAX's collectives and lax.ppermute only.
A program may use at most 128 MiB of HBM per device.

v0:
```python
import jax
import jax.numpy as jnp
from jax import lax

COEFS = 5120
LOCAL = 16
SLOTS = 192
ARCS = 128
ROWS = 24576


def eliminate(block_design, block_local, block_observed, block_live):
    highest = lax.Precision.HIGHEST
    masked = block_local * block_live[None, :]
    gram_matrix = jnp.dot(masked, block_local.T, precision=highest) + jnp.eye(
        block_local.shape[0], dtype=jnp.float32
    )
    factor = jnp.linalg.cholesky(gram_matrix)
    inverse = jax.scipy.linalg.cho_solve(
        (factor, True), jnp.eye(block_local.shape[0], dtype=jnp.float32)
    )
    dense = block_design.astype(jnp.float32)
    cross_terms = jnp.dot(masked, dense, precision=highest)
    cross_obs = jnp.dot(masked, block_observed, precision=highest)
    projector = jnp.dot(inverse, cross_terms, precision=highest)
    projected = block_live[:, None] * (dense - jnp.dot(block_local.T, projector, precision=highest))
    solved_obs = jnp.dot(inverse, cross_obs, precision=highest)
    residual = block_live * (block_observed - jnp.dot(block_local.T, solved_obs, precision=highest))
    return (projected.astype(jnp.bfloat16), residual)


def live_rows(counts, valid_mask):
    slot_count = valid_mask.shape[0] // counts.shape[0]
    inside = jnp.arange(slot_count, dtype=jnp.int32)[None, :] < counts[:, None]
    return inside.reshape(-1).astype(jnp.float32) * valid_mask.astype(jnp.float32)


def reference(design, local_design, observed, valid_mask, counts):
    live_mask = live_rows(counts, valid_mask)
    blocks_design = design.reshape(ARCS, SLOTS, COEFS)
    blocks_local = local_design.reshape(LOCAL, ARCS, SLOTS).transpose(1, 0, 2)
    projected, residual = jax.vmap(eliminate)(
        blocks_design, blocks_local, observed.reshape(ARCS, SLOTS), live_mask.reshape(ARCS, SLOTS)
    )
    dense = projected.reshape(ROWS, COEFS).astype(jnp.float32)
    normal = jnp.dot(dense.T, dense, preferred_element_type=jnp.float32)
    rhs = jnp.dot(residual.reshape(ROWS), dense, precision=lax.Precision.HIGHEST)
    return (normal, rhs)


def solution(mesh):
    return reference
```

profile of v0, /device:TPU:14, one launch (start us, length us, event | category | flops | bytes accessed | tf_op | source)
XLA Modules:
  0.0 376.0 jit_solution(1108685858874650687)
XLA Ops:
  7.2 0.0 all-gather.3.cloned.1.call-start
  7.3 0.9 iota_compare_fusion.3
  8.1 0.1 lt.22
  8.2 0.7 convert_select_fusion
  8.9 0.1 mul.30
  9.0 1.0 reshape.57
  10.0 0.3 fusion.5
  10.2 0.1 copy.9
  10.3 11.7 %custom-call.12 = f32[8,16,16]{2,1,0:T(8,128)S(1)} custom-call(f32[8,16,16]{2,1,0:T(8,128)S(1)} %fusion.20), custom_call_target="Cholesky" | custom-call | tf_op jit(solution)/vmap(jit(cholesky))/cholesky | solution.py:18
  22.1 0.1 copy.10
  22.2 0.1 select_reduce_fusion
  22.3 0.1 select_bitcast_fusion
  22.4 2.7 custom-call.13
  25.2 0.1 copy.12
  25.3 0.3 fusion.24
  25.6 0.2 fusion.31
  25.8 1.0 fusion.7
  26.8 0.4 fusion.32
  27.2 4.8 %fusion.1 = bf16[8,192,640]{2,1,0:T(8,128)(2,1)} fusion(bf16[8,192,640]{2,1,0:T(8,128)(2,1)S(1)} %bitcast.68, f32[8,16,640]{2,1,0:T(8,128)S(1)} %fusion.32, f32[8,192]{1,0:T(8,128)S(1)} %mul.30, f32[16,8,192]{2,1,0:T(8,128)S(1)} %reshape.57), kind=kOutput, calls=%fused_computation.3 | convolution fusion | flops 192675840 | bytes 4364288 | tf_op jit(solution)/vmap()/dot_general | solution.py:26
  32.0 0.0 all-gather.3.cloned.1.call-update
  32.0 0.0 reduce-scatter.4.cloned.1.call-start
  32.0 174.8 %all-gather.3.cloned.1.call-done = bf16[8,192,5120]{2,1,0:T(8,128)(2,1)} async-done(((bf16[8,192,640]{2,1,0:T(8,128)(2,1)}), bf16[8,192,5120]{2,1,0:T(8,128)(2,1)}) %all-gather.3.cloned.1.call-update) | async-done | bytes 15728656 | tf_op jit(solution)/vmap()/convert_element_type | solution.py:29
  206.8 18.7 %convolution_bitcast_fusion = f32[5120,640]{1,0:T(8,128)} fusion(bf16[8,192,5120]{2,1,0:T(8,128)(2,1)} %all-gather.3.cloned.1.call-done, bf16[8,192,640]{2,1,0:T(8,128)(2,1)S(1)} %copy-done), kind=kOutput, calls=%fused_computation | convolution fusion | flops 10066329600 | bytes 30801920 | tf_op jit(solution)/dot_general | solution.py:46
  225.6 0.7 copy-done.2
  226.2 0.1 reshape.89
  226.3 0.1 reshape.73
  226.4 0.3 convolution_bitcast_fusion.2
  226.7 0.2 convolution_bitcast_fusion.1
  226.9 0.2 fusion.3
  227.1 0.9 convolution_reduce_fusion
  228.1 27.7 %all-reduce.1 = f32[640]{0:T(1024)} all-reduce(f32[640]{0:T(1024)S(1)} %convolution_reduce_fusion), channel_id=3, replica_groups=[8,16]<=[16,8]T(1,0), use_global_device_ids=true, to_apply=%add.1.clone | all-reduce | flops 640 | bytes 5120 | tf_op jit(solution)/dot_general | solution.py:47
  255.7 113.4 %reduce-scatter.4.cloned.1.call-done = f32[320,640]{1,0:T(8,128)} async-done(((f32[5120,640]{1,0:T(8,128)}), f32[320,640]{1,0:T(8,128)}) %reduce-scatter.4.cloned.1.call-update) | async-done | bytes 819216
  (12 shorter events, 0.1 us)
Async XLA Ops:
  7.2 18.6 %copy-start.1 = (bf16[1536,640]{1,0:T(8,128)(2,1)S(1)}, bf16[1536,640]{1,0:T(8,128)(2,1)}, u32[]{:S(2)}) copy-start(bf16[1536,640]{1,0:T(8,128)(2,1)} %param.2) | copy-start | bytes 5898244
  7.2 199.7 %all-gather.3.cloned.1.call-start = ((), (), s32[]{:S(2)}) async-start(), calls=%async_computation.1 | async-start | bytes 17694720 | tf_op jit(solution)/vmap()/convert_element_type | solution.py:29
  32.0 174.9 %copy-start = (bf16[8,192,640]{2,1,0:T(8,128)(2,1)S(1)}, bf16[8,192,640]{2,1,0:T(8,128)(2,1)}, u32[]{:S(2)}) copy-start(bf16[8,192,640]{2,1,0:T(8,128)(2,1)} %fusion.1) | copy-start | bytes 5898244
  32.0 337.2 %reduce-scatter.4.cloned.1.call-start = ((), (), s32[]{:S(2)}) async-start(), calls=%async_computation.2 | async-start | bytes 13926400
  225.5 0.7 copy-start.2
Sparse Core Ops, SparseCore 0:
  32.1 174.6 all-gather.2
  225.7 143.4 reduce-scatter.3
where the time goes:
time: 380 us; the launch traced here: 376 us
  waiting for transfers between devices  288 us (76%)
  blocking collectives  27.7 us (7%)
  matrix products  27.3 us (7%)
  other arithmetic  16.3 us (4%)
  between operations  14.2 us (4%)
    convert_element_type x1, waiting for transfers between devices, eliminate(): return (projected.astype(jnp.bfloat16), residual)  175 us
    unnamed x3, waiting for transfers between devices  113 us
    dot_general x1, blocking collectives, reference(): jnp.dot(residual.reshape(ROWS), dense, precision=lax.Precision.HIGHEST)  27.7 us
    dot_general x1, matrix products, reference(): normal = jnp.dot(dense.T, dense, preferred_element_type=jnp.float32)  18.7 us
    another operation x4, other arithmetic, eliminate(): factor = jnp.linalg.cholesky(gram_matrix)  11.9 us
  transfers between devices with their start and end apart: 2, of which 2 were waited for; matrix products, arithmetic and copies ran while one was open for 0% of the time, Pallas kernels for 0%

commit v1 on v0

v1 whole, which is shorter than its diff:
```python
import functools

import jax
import jax.numpy as jnp
from jax import lax
from jax.experimental import pallas as pl
from jax.experimental.pallas import tpu as pltpu
from jax.sharding import Mesh, PartitionSpec as P

LOCAL = 16
SLOTS = 192
AXES = ("z", "yl", "core", "x", "yh")
HIGHEST = lax.Precision.HIGHEST
F32 = jnp.float32
BF16 = jnp.bfloat16
VMEM = pl.BlockSpec(memory_space=pltpu.VMEM)
SMEM = pl.BlockSpec(memory_space=pltpu.SMEM)
PARAMS = pltpu.CompilerParams(vmem_limit_bytes=48 << 20)
CHEAP = pl.CostEstimate(flops=1, transcendentals=0, bytes_accessed=1)


def shape(dims, dtype):
    return jax.ShapeDtypeStruct(dims, dtype)


def inner(a, b, contract, precision=None):
    return lax.dot_general(a, b, ((contract[:1], contract[1:]), ((), ())), precision=precision, preferred_element_type=F32)


def iota(dims, axis):
    return lax.broadcasted_iota(jnp.int32, dims, axis)


def eliminate_kernel(counts, block, observed, valid, high, low, residual):
    arcs = block.shape[0]
    eye = (iota((LOCAL, LOCAL), 0) == iota((LOCAL, LOCAL), 1)).astype(F32)
    live, masked, grams = [], [], []
    for a in range(arcs):
        inside = (iota((1, SLOTS), 1) < counts[a]).astype(F32)
        live.append(inside * valid[a : a + 1, :].astype(F32))
        masked.append(block[a] * live[a])
        grams.append((inner(masked[a], block[a], (1, 1), HIGHEST) + eye)[None])
    gram = jnp.concatenate(grams, 0)
    rows, cols = iota(gram.shape, 1), iota(gram.shape, 2)
    for p in range(LOCAL):
        column = gram[:, :, p : p + 1]
        pivot = 1.0 / gram[:, p : p + 1, p : p + 1]
        row = gram[:, p : p + 1, :] * pivot
        swept = jnp.where(rows == p, row, gram - column * row)
        edge = jnp.where(rows == p, pivot, -column * pivot)
        gram = jnp.where(cols == p, edge, swept)
    diagonal = iota((SLOTS, SLOTS), 0) == iota((SLOTS, SLOTS), 1)
    for a in range(arcs):
        weights = jnp.dot(gram[a], masked[a], precision=HIGHEST, preferred_element_type=F32)
        fitted = inner(masked[a], weights, (0, 0), HIGHEST)
        elim = jnp.where(diagonal, live[a], 0.0) - fitted
        top = elim.astype(BF16)
        high[a * SLOTS : (a + 1) * SLOTS, :] = top
        low[a * SLOTS : (a + 1) * SLOTS, :] = (elim - top.astype(F32)).astype(BF16)
        y = observed[a : a + 1, :]
        solved = jnp.sum(weights * y, axis=1, keepdims=True)
        residual[a : a + 1, :] = live[a] * (y - jnp.sum(block[a] * solved, axis=0, keepdims=True))


def eliminate(local, observed, valid, counts):
    arcs = counts.shape[0]
    block = local.reshape(LOCAL, arcs, SLOTS).transpose(1, 0, 2)
    return pl.pallas_call(
        eliminate_kernel,
        out_shape=(
            shape((arcs * SLOTS, SLOTS), BF16),
            shape((arcs * SLOTS, SLOTS), BF16),
            shape((arcs, SLOTS), F32),
        ),
        in_specs=[SMEM, VMEM, VMEM, VMEM],
        out_specs=(VMEM, VMEM, VMEM),
        compiler_params=PARAMS,
        cost_estimate=CHEAP,
        name="eliminate",
    )(counts, block, observed.reshape(arcs, SLOTS), valid.reshape(arcs, SLOTS))


def rounded(high, low, rows):
    first = jnp.dot(high, rows, preferred_element_type=F32)
    return (first + jnp.dot(low, rows, preferred_element_type=F32)).astype(BF16)


def project_into(out, high, low, rows, begin, count, source):
    for i in range(count):
        to = slice((begin + i) * SLOTS, (begin + i + 1) * SLOTS)
        at = slice((source + i) * SLOTS, (source + i + 1) * SLOTS)
        out[to, :] = rounded(high[to, :], low[to, :], rows[at, :])


def own_kernel(high, low, residual, rows, out, product, rhs):
    arcs = residual.shape[0]
    half = product.shape[1]
    project_into(out, high, low, rows, 0, arcs, 0)
    total = jnp.zeros((1, rows.shape[1]), F32)
    parts = iota((16, SLOTS), 0)
    for a in range(arcs):
        r = residual[a : a + 1, :]
        one = r.astype(BF16).astype(F32)
        two = (r - one).astype(BF16).astype(F32)
        three = r - one - two
        stack = jnp.where(parts == 0, one, jnp.where(parts == 1, two, jnp.where(parts == 2, three, 0.0)))
        part = jnp.dot(stack.astype(BF16), out[a * SLOTS : (a + 1) * SLOTS, :], preferred_element_type=F32)
        total = total + jnp.sum(part, axis=0, keepdims=True)
    rhs[...] = total
    result = tdot(out[...], out[...])
    product[0] = result[:half]
    product[1] = result[half:]


def near_kernel(where, high, low, own, product, above, below, out, both, send):
    arcs, half = high.shape[0] // SLOTS, product.shape[1]
    top = above.shape[0]
    project_into(out, high, low, above, 0, arcs // 2, 0)
    project_into(out, high, low, below, arcs // 2, arcs // 2, 0)
    for piece, rows in enumerate((slice(0, top), slice(top, 2 * top))):
        result = tdot(out[rows, :], own[rows, :])
        both[0, piece] = result[:half]
        both[1, piece] = result[half:]
    other = 1 - where[0]
    send[0] = product[other].astype(BF16)
    send[1] = both[other, 0].astype(BF16)
    send[2] = both[other, 1].astype(BF16)


def far_kernel(where, high, low, own, near, flip_top, flip_bottom, above, below, both, send, flip, two):
    arcs, half = high.shape[0] // SLOTS, both.shape[2]
    top = above.shape[0]
    project_into(flip, high, low, flip_top, 0, arcs // 2, 0)
    project_into(flip, high, low, flip_bottom, arcs // 2, arcs // 2, 0)
    project_into(two, high, low, above, 0, arcs // 2, 0)
    project_into(two, high, low, below, arcs // 2, arcs // 2, 0)
    for slot, rows in ((1, slice(0, top)), (3, slice(top, 2 * top))):
        result = tdot(near[rows, :], flip[rows, :])
        both[0, slot] = result[:half]
        both[1, slot] = result[half:]
    cut_flip, cut_two = where[2], where[3]

    def quadrants(a, b, cut, slot, columns):
        result = tdot(a[...], b[...])
        for r in range(2):
            rows = result[r * half : (r + 1) * half]
            both[r, slot, :, columns] = jnp.where(cut == r, rows[:, :half], rows[:, half:])

    for r in range(2):
        both[r, 0, :, half:] = jnp.zeros((half, half), F32)
    quadrants(flip, own, cut_flip, 0, slice(0, half))
    quadrants(two, own, cut_two, 2, slice(0, half))
    quadrants(two, flip, cut_two, 2, slice(half, 2 * half))
    send[...] = both[1 - where[0]].astype(BF16)


def tdot(a, b):
    return inner(a, b, (0, 0))


def spread(where, sums, mine, ups):
    delta = where[1]
    mine[...] = sums[delta]
    for k, up in enumerate(ups, 1):
        up[...] = sums[(delta + k) % 4].astype(BF16)


def near_spread_kernel(where, product, both, got, mine, up1, up2, up3, sums):
    core = where[0]
    sums[0] = product[core] + got[0].astype(F32)
    sums[1] = both[core, 0] + got[1].astype(F32)
    sums[2] = jnp.zeros(sums.shape[1:], F32)
    sums[3] = both[core, 1] + got[2].astype(F32)
    spread(where, sums, mine, (up1, up2, up3))


def far_spread_kernel(where, both, got, mine, up1, up2, up3, sums):
    sums[...] = both[where[0]] + got[...].astype(F32)
    spread(where, sums, mine, (up1, up2, up3))


def near_total_kernel(mine, one, two, three, total, send):
    total[...] = ((mine[...] + one[...].astype(F32)) + two[...].astype(F32)) + three[...].astype(F32)
    send[...] = total[...].astype(BF16)


def far_total_kernel(where, mine, one, two, three, keep, send):
    total = ((mine[...] + one[...].astype(F32)) + two[...].astype(F32)) + three[...].astype(F32)
    half = total.shape[0]
    opposite, same = where[1] == 2, where[4] == 1
    turned = jnp.concatenate([total[:, half:], total[:, :half]], 1)
    send[...] = jnp.where(jnp.logical_and(opposite, same), turned, total).astype(BF16)
    keep[...] = jnp.where(jnp.logical_and(opposite, jnp.logical_not(same)), turned, total)


def place_kernel(where, near, near_got, keep, got, placed, first, second, across):
    half = placed.shape[0]
    core, delta, same, right = where[0], where[1], where[4] == 1, where[5] == 1
    late = keep[...] + got[...].astype(F32)
    early = near[...] + near_got[...].astype(F32)
    total = jnp.where(jnp.logical_and(same, delta != 2), early, late)
    quad = jnp.logical_or(delta == 2, jnp.logical_and(delta == 0, jnp.logical_not(same)))
    left_side = jnp.where(jnp.logical_and(quad, right), 0.0, total[:, :half])
    right_side = jnp.where(quad, jnp.where(right, total[:, :half], 0.0), total[:, half:])
    placed[:, :half] = left_side
    placed[:, half:] = right_side
    low, high = left_side.astype(BF16), right_side.astype(BF16)
    first[...] = jnp.where(core == 0, low, high)
    second[...] = jnp.where(core == 0, high, low)
    diagonal = delta == 0
    across[:, :half] = jnp.where(diagonal, total[:, :half].astype(BF16), low)
    across[:, half:] = high


def finish_kernel(where, placed, first, second, across, out):
    half = out.shape[0]
    core, delta, same, right = where[0], where[1], where[4] == 1, where[5] == 1
    one, two = first[...].astype(F32), second[...].astype(F32)
    quad = across[:, :half].astype(F32)
    diagonal = delta == 0
    left = jnp.where(diagonal, jnp.where(right, quad, 0.0), jnp.where(core == 0, one, two))
    rest = jnp.where(diagonal, jnp.where(right, 0.0, quad), jnp.where(core == 0, two, one))
    keep = jnp.logical_or(diagonal, same)
    out[:, :half] = jnp.where(keep, placed[:, :half], quad) + left.T
    out[:, half:] = jnp.where(keep, placed[:, half:], across[:, half:].astype(F32)) + rest.T


def call(kernel, outs, *args, scalars=True, scratch=()):
    return pl.pallas_call(
        kernel,
        out_shape=outs,
        in_specs=[SMEM if scalars and i == 0 else VMEM for i in range(len(args))],
        out_specs=jax.tree.map(lambda _: VMEM, outs),
        scratch_shapes=scratch,
        compiler_params=PARAMS,
        cost_estimate=CHEAP,
        name=kernel.__name__,
    )(*args)


def body(sizes, design, local, observed, valid, counts):
    nz, nyl, ncore, nx, nyh = sizes
    z, yl, core, x, yh = (lax.axis_index(name) for name in AXES)
    delta = (z - x) % nx
    rows, width = design.shape
    half, top = width // 2, rows // 2
    down = [(i, (i - 1) % nx) for i in range(nx)]
    up = [(i, (i + 1) % nx) for i in range(nx)]
    swap = [(0, 1), (1, 0)]
    turn = lambda k: [(i, (i + k) % nz) for i in range(nz)]
    high_x = (x >= nx // 2).astype(jnp.int32)
    same = (yl == yh).astype(jnp.int32)
    right = core ^ jnp.where(delta == 2, high_x, yh)
    where = jnp.stack([core, delta, yh, high_x, same, right]).astype(jnp.int32)

    upper, lower = design[:top], design[top:]
    above = lax.ppermute(upper, "x", down)
    below = lax.ppermute(lower, "x", up)
    flip_top = lax.ppermute(upper, "yh", swap)

    a_high, a_low, residual = eliminate(local, observed, valid, counts)
    own, product, rhs = call(
        own_kernel,
        (shape((rows, width), BF16), shape((2, half, width), F32), shape((1, width), F32)),
        a_high, a_low, residual, design,
        scalars=False,
    )
    rhs = rhs[0]
    rhs = rhs + lax.ppermute(rhs, "core", swap)
    rhs = rhs + lax.ppermute(rhs, "yl", swap)
    around = [lax.ppermute(rhs, "z", turn(k)) for k in range(1, nz)]
    rhs = (rhs + around[1]) + (around[0] + around[2])

    above, below, flip_top, own, lower, rhs = lax.optimization_barrier((above, below, flip_top, own, lower, rhs))
    flip_bottom = lax.ppermute(lower, "yh", swap)
    above2 = lax.ppermute(above, "x", down)
    below2 = lax.ppermute(below, "x", up)

    wide, sent = shape((half, width), F32), shape((half, width), BF16)
    sums = (pltpu.VMEM((nz, half, width), F32),)

    near, both, send = call(
        near_kernel,
        (shape((rows, width), BF16), shape((2, 2, half, width), F32), shape((3, half, width), BF16)),
        where, a_high, a_low, own, product, above, below,
    )
    got = lax.ppermute(send, "core", swap)
    mine, *ups = call(near_spread_kernel, (wide, sent, sent, sent), where, product, both, got, scratch=sums)
    ups = [lax.ppermute(v, "z", turn(k)) for k, v in enumerate(ups, 1)]
    early, send = call(near_total_kernel, (wide, sent), mine, *ups, scalars=False)

    flip_top, flip_bottom, above2, below2, early, send = lax.optimization_barrier(
        (flip_top, flip_bottom, above2, below2, early, send)
    )
    early_got = lax.ppermute(send, ("yl", "yh"), [(1, 3), (2, 0)])
    both, send = call(
        far_kernel,
        (shape((2, nz, half, width), F32), shape((nz, half, width), BF16)),
        where, a_high, a_low, own, near, flip_top, flip_bottom, above2, below2,
        scratch=(pltpu.VMEM((rows, width), BF16), pltpu.VMEM((rows, width), BF16)),
    )
    got = lax.ppermute(send, "core", swap)
    mine, *ups = call(far_spread_kernel, (wide, sent, sent, sent), where, both, got, scratch=sums)
    ups = [lax.ppermute(v, "z", turn(k)) for k, v in enumerate(ups, 1)]
    keep, send = call(far_total_kernel, (wide, sent), where, mine, *ups)
    got = lax.ppermute(send, "yl", swap)

    quad = shape((half, half), BF16)
    placed, first, second, across = call(
        place_kernel, (wide, quad, quad, sent), where, early, early_got, keep, got
    )

    def index(a, k, b):
        return (a * ncore + k) * nx + b

    turned = []
    for j, send in enumerate((first, second)):
        pairs = [
            (index(a, k, b), index(b, k ^ j, a))
            for a in range(nz)
            for k in range(ncore)
            for b in range(nx)
            if a != b and ((a - b) % nx != 2 or (b >= nx // 2) == (j == 1))
        ]
        turned.append(lax.ppermute(send, ("z", "core", "x"), pairs))

    def device(a, b, k, c, d):
        return (((a * nyl + b) * ncore + k) * nx + c) * nyh + d

    pairs = []
    for a in range(nz):
        for b in range(nyl):
            for k in range(ncore):
                for c in range(nx):
                    d = 1 - b
                    to = k ^ d if a == c else k
                    pairs.append((device(a, b, k, c, d), device(a, d, to, c, b)))
    across = lax.ppermute(across, AXES, pairs)
    out = call(finish_kernel, wide, where, placed, *turned, across)
    return out, rhs


def solution(mesh):
    sizes = (4, 2, 2, 4, 2)
    grid = Mesh(mesh.devices.reshape(sizes), AXES)
    arc, col = ("z", "yl", "core"), ("x", "yh")

    def run(design, local_design, observed, valid_mask, counts):
        return jax.shard_map(
            functools.partial(body, sizes),
            mesh=grid,
            in_specs=(P(arc, col), P(None, arc), P(arc), P(arc), P(arc)),
            out_specs=(P(arc, col), P(col)),
            check_vma=False,
        )(design, local_design, observed, valid_mask, counts)

    return run
```

time: 380 us -> 163 us (0.43)
  waiting for transfers between devices: 288 us -> 66.5 us
  starting transfers between devices: 0.08 us -> 43.5 us
  Pallas kernels: 0 us -> 42 us
  blocking collectives: 27.7 us -> 0 us
  matrix products: 27.3 us -> 0 us
  other arithmetic: 16.3 us -> 1.3 us
  between operations: 14.2 us -> 0.83 us
  local copies, waits for them, and re-layouts: 2.27 us -> 6.58 us
    convert_element_type x1 -> x0, waiting for transfers between devices: 175 us -> none  [eliminate(): return (projected.astype(jnp.bfloat16), residual)]
    unnamed x3 -> x0, waiting for transfers between devices: 113 us -> none
    ppermute x0 -> x24, waiting for transfers between devices: none -> 66.5 us  [the longest x6 30.2 us: body(): ups = [lax.ppermute(v, 'z', turn(k)) for k, v in enumerate(ups, 1)]]
    ppermute x0 -> x24, starting transfers between devices: none -> 43.5 us  [the longest x6 12 us: body(): ups = [lax.ppermute(v, 'z', turn(k)) for k, v in enumerate(ups, 1)]]
    pallas_call x0 -> x10, Pallas kernels: none -> 42 us  [the longest x9 36.4 us: call(): pl.pallas_call(kernel, out_shape=outs, in_specs=[SMEM if scalars and i ==...]
    dot_general x1 -> x0, blocking collectives: 27.7 us -> none  [reference(): jnp.dot(residual.reshape(ROWS), dense, precision=lax.Precision.HIGHEST)]
    dot_general x9 -> x0, matrix products: 26.8 us -> none  [the longest x1 18.7 us: reference(): normal = jnp.dot(dense.T, dense, preferred_element_type=jnp.float32)]
    another operation x7 -> x0, other arithmetic: 14.7 us -> none  [the longest x4 11.9 us: eliminate(): factor = jnp.linalg.cholesky(gram_matrix)]
  transfers between devices with their start and end apart: 2 -> 24, of which waited for: 2 -> 14; matrix products, arithmetic and copies ran while one was open for 0% -> 1% of each run, Pallas kernels for 0% -> 9%
where the time goes in v1:
time: 163 us; the launch traced here: 161 us
  waiting for transfers between devices  66.5 us (41%)
  starting transfers between devices  43.5 us (27%)
  Pallas kernels  42 us (26%)
  local copies, waits for them, and re-layouts  6.58 us (4%)
    pallas_call x9, Pallas kernels, call(): pl.pallas_call(kernel, out_shape=outs, in_specs=[SMEM if scalars and i ==...  36.4 us
    ppermute x6, waiting for transfers between devices, body(): ups = [lax.ppermute(v, 'z', turn(k)) for k, v in enumerate(ups, 1)]  30.2 us
    ppermute x2, waiting for transfers between devices, body(): turned.append(lax.ppermute(send, ('z', 'core', 'x'), pairs))  13.4 us
    ppermute x6, starting transfers between devices, body(): ups = [lax.ppermute(v, 'z', turn(k)) for k, v in enumerate(ups, 1)]  12 us
    ppermute x1, waiting for transfers between devices, body(): got = lax.ppermute(send, 'yl', swap)  8.94 us
    ppermute x2, starting transfers between devices, body(): turned.append(lax.ppermute(send, ('z', 'core', 'x'), pairs))  6.79 us
    ppermute x3, starting transfers between devices, body(): around = [lax.ppermute(rhs, 'z', turn(k)) for k in range(1, nz)]  6.16 us
    pallas_call x1, Pallas kernels, eliminate(): pl.pallas_call(eliminate_kernel, out_shape=(shape((arcs * SLOTS, SLOTS),...  5.62 us
  transfers between devices with their start and end apart: 24, of which 14 were waited for; matrix products, arithmetic and copies ran while one was open for 1% of the time, Pallas kernels for 9%

profile of v1, /device:TPU:14, one launch (start us, length us, event | category | flops | bytes accessed | tf_op | source)
XLA Modules:
  0.0 160.8 jit_solution(12287778395273299053)
XLA Ops:
  0.7 3.0 %fusion = (bf16[768,640]{1,0:T(8,128)(2,1)}, bf16[768,640]{1,0:T(8,128)(2,1)}) fusion(bf16[1536,640]{1,0:T(8,128)(2,1)} %rows.1), kind=kLoop, calls=%fused_computation.2 | loop fusion | bytes 3932160 | tf_op jit(solution)/shard_map/slice | solution.py:256
  4.2 2.3 %collective-permute-start.2 = (bf16[768,640]{1,0:T(8,128)(2,1)}, bf16[768,640]{1,0:T(8,128)(2,1)}, u32[]{:S(2)}, u32[]{:S(2)}) collective-permute-start(bf16[768,640]{1,0:T(8,128)(2,1)} %get-tuple-element.81), channel_id=1, source_target_pairs={{0,1},{1,0},{2,3},{3,2},{4,5},{5,4},{6,7},{7,6},{8,9},{9,8},{10,11... | collective-permute-start | bytes 2949128 | tf_op jit(solution)/shard_map/ppermute | solution.py:259
  6.5 1.5 collective-permute-start
  9.0 5.6 %eliminate.1 = (bf16[1536,192]{1,0:T(8,128)(2,1)S(1)}, bf16[1536,192]{1,0:T(8,128)(2,1)S(1)}, f32[8,192]{1,0:T(8,128)S(1)}) custom-call(s32[8]{0:T(128)S(1)} %copy-done.3, f32[8,16,192]{2,1,0:T(8,128)S(1)} %bitcast.9, f32[8,192]{1,0:T(8,128)S(1)} %reshape.14.observed, s32[8,192]{1,0:T(8,128)S(1)} %reshape.15.valid), custom_call_target="tpu_custom_call" | custom-call | flops 1 | bytes 1 | tf_op jit(solution)/shard_map/eliminate/pallas_call | solution.py:68
  14.6 4.9 %own_kernel.1 = (bf16[1536,640]{1,0:T(8,128)(2,1)S(1)}, f32[2,320,640]{2,1,0:T(8,128)S(1)}, f32[1,640]{1,0:T(1,128)S(1)}) custom-call(bf16[1536,192]{1,0:T(8,128)(2,1)S(1)} %get-tuple-element.41.high, bf16[1536,192]{1,0:T(8,128)(2,1)S(1)} %get-tuple-element.42.low, f32[8,192]{1,0:T(8,128)S(1)} %get-tuple-element.43.residual, bf16[1536,640]{1,0:T(8,128)(2,1)} %rows.1), custom_call_target="tpu_custom_call" | custom-call | flops 1 | bytes 1 | tf_op jit(solution)/shard_map/own_kernel/pallas_call | solution.py:229
  24.6 4.7 %collective-permute-done.4 = f32[640]{0:T(1024)S(1)} collective-permute-done((f32[640]{0:T(1024)S(1)}, f32[640]{0:T(1024)S(1)}, u32[]{:S(2)}, u32[]{:S(2)}) %collective-permute-start.4) | collective-permute-done | bytes 2592 | tf_op jit(solution)/shard_map/ppermute | solution.py:270
  29.3 4.0 %collective-permute-start.7 = (f32[640]{0:T(1024)S(1)}, f32[640]{0:T(1024)S(1)}, u32[]{:S(2)}, u32[]{:S(2)}) collective-permute-start(f32[640]{0:T(1024)S(1)} %add.21), channel_id=1, source_target_pairs={{0,96},{32,0},{64,32},{96,64},{1,97},{33,1},{65,33},{97,65},{2,98}... | collective-permute-start | bytes 7688 | tf_op jit(solution)/shard_map/ppermute | solution.py:271
  34.7 2.1 %collective-permute-start.5 = (f32[640]{0:T(1024)S(1)}, f32[640]{0:T(1024)}, u32[]{:S(2)}, u32[]{:S(2)}) collective-permute-start(f32[640]{0:T(1024)S(1)} %add.21), channel_id=1, source_target_pairs={{0,64},{32,96},{64,0},{96,32},{1,65},{33,97},{65,1},{97,33},{2,66}... | collective-permute-start | bytes 7688 | tf_op jit(solution)/shard_map/ppermute | solution.py:271
  38.2 1.7 %collective-permute-done.5 = f32[640]{0:T(1024)} collective-permute-done((f32[640]{0:T(1024)S(1)}, f32[640]{0:T(1024)}, u32[]{:S(2)}, u32[]{:S(2)}) %collective-permute-start.5) | collective-permute-done | bytes 2592 | tf_op jit(solution)/shard_map/ppermute | solution.py:271
  41.2 6.7 %near_kernel.1 = (bf16[1536,640]{1,0:T(8,128)(2,1)}, f32[2,2,320,640]{3,2,1,0:T(8,128)}, bf16[3,320,640]{2,1,0:T(8,128)(2,1)S(1)}) custom-call(s32[6]{0:T(128)S(1)} %stack.31.where, bf16[1536,192]{1,0:T(8,128)(2,1)S(1)} %get-tuple-element.41.high, bf16[1536,192]{1,0:T(8,128)(2,1)S(1)} %get-tuple-element.42.low, bf16[1536,640]{1,0:T(8,128)(2,1)} %copy-done, ...), custom_call_target="tpu_custom_call" | custom-call | flops 1 | bytes 1 | tf_op jit(solution)/shard_map/near_kernel/pallas_call | solution.py:229
  47.9 1.6 %collective-permute-start.9 = (bf16[768,640]{1,0:T(8,128)(2,1)S(1)}, bf16[768,640]{1,0:T(8,128)(2,1)S(1)}, u32[]{:S(2)}, u32[]{:S(2)}) collective-permute-start(bf16[768,640]{1,0:T(8,128)(2,1)S(1)} %collective-permute-done.above), channel_id=1, source_target_pairs={{0,6},{2,0},{4,2},{6,4},{1,7},{3,1},{5,3},{7,5},{8,14},{10,8},{12,... | collective-permute-start | bytes 2949128 | tf_op jit(solution)/shard_map/ppermute | solution.py:276
  49.6 1.7 %collective-permute-start.10 = (bf16[768,640]{1,0:T(8,128)(2,1)S(1)}, bf16[768,640]{1,0:T(8,128)(2,1)S(1)}, u32[]{:S(2)}, u32[]{:S(2)}) collective-permute-start(bf16[768,640]{1,0:T(8,128)(2,1)S(1)} %collective-permute-done.1.below), channel_id=1, source_target_pairs={{0,2},{2,4},{4,6},{6,0},{1,3},{3,5},{5,7},{7,1},{8,10},{10,12},{12... | collective-permute-start | bytes 2949128 | tf_op jit(solution)/shard_map/ppermute | solution.py:277
  51.3 2.4 %near_spread_kernel.1 = (f32[320,640]{1,0:T(8,128)S(1)}, bf16[320,640]{1,0:T(8,128)(2,1)S(1)}, bf16[320,640]{1,0:T(8,128)(2,1)S(1)}, bf16[320,640]{1,0:T(8,128)(2,1)S(1)}) custom-call(s32[6]{0:T(128)S(1)} %stack.31.where, f32[2,320,640]{2,1,0:T(8,128)S(1)} %copy-done.2, f32[2,2,320,640]{3,2,1,0:T(8,128)} %get-tuple-element.52.both, ...), custom_call_target="tpu_custom_call" | custom-call | flops 1 | bytes 1 | tf_op jit(solution)/shard_map/near_spread_kernel/pallas_call | solution.py:229
  54.6 4.1 %collective-permute-start.13 = (bf16[320,640]{1,0:T(8,128)(2,1)S(1)}, bf16[320,640]{1,0:T(8,128)(2,1)S(1)}, u32[]{:S(2)}, u32[]{:S(2)}) collective-permute-start(bf16[320,640]{1,0:T(8,128)(2,1)S(1)} %get-tuple-element.56), channel_id=1, source_target_pairs={{0,64},{32,96},{64,0},{96,32},{1,65},{33,97},{65,1},{97,33},{2,66}... | collective-permute-start | bytes 1228808 | tf_op jit(solution)/shard_map/ppermute | solution.py:289
  58.7 8.0 %collective-permute-done.12.one = bf16[320,640]{1,0:T(8,128)(2,1)S(1)} collective-permute-done((bf16[320,640]{1,0:T(8,128)(2,1)S(1)}, bf16[320,640]{1,0:T(8,128)(2,1)S(1)}, u32[]{:S(2)}, u32[]{:S(2)}) %collective-permute-start.12) | collective-permute-done | bytes 409632 | tf_op jit(solution)/shard_map/ppermute | solution.py:289
  66.8 2.8 %collective-permute-start.14 = (bf16[320,640]{1,0:T(8,128)(2,1)S(1)}, bf16[320,640]{1,0:T(8,128)(2,1)S(1)}, u32[]{:S(2)}, u32[]{:S(2)}) collective-permute-start(bf16[320,640]{1,0:T(8,128)(2,1)S(1)} %get-tuple-element.57), channel_id=1, source_target_pairs={{0,96},{32,0},{64,32},{96,64},{1,97},{33,1},{65,33},{97,65},{2,98}... | collective-permute-start | bytes 1228808 | tf_op jit(solution)/shard_map/ppermute | solution.py:289
  69.6 7.1 %collective-permute-done.13.two = bf16[320,640]{1,0:T(8,128)(2,1)S(1)} collective-permute-done((bf16[320,640]{1,0:T(8,128)(2,1)S(1)}, bf16[320,640]{1,0:T(8,128)(2,1)S(1)}, u32[]{:S(2)}, u32[]{:S(2)}) %collective-permute-start.13) | collective-permute-done | bytes 409632 | tf_op jit(solution)/shard_map/ppermute | solution.py:289
  77.9 14.9 %far_kernel.1 = (f32[2,4,320,640]{3,2,1,0:T(8,128)}, bf16[4,320,640]{2,1,0:T(8,128)(2,1)}) custom-call(s32[6]{0:T(128)S(1)} %stack.31.where, bf16[1536,192]{1,0:T(8,128)(2,1)S(1)} %get-tuple-element.41.high, bf16[1536,192]{1,0:T(8,128)(2,1)S(1)} %get-tuple-element.42.low, bf16[1536,640]{1,0:T(8,128)(2,1)} %copy-done, ...), custom_call_target="tpu_custom_call" | custom-call | flops 1 | bytes 1 | tf_op jit(solution)/shard_map/far_kernel/pallas_call | solution.py:229
  92.7 3.7 %collective-permute-done.16.got = bf16[4,320,640]{2,1,0:T(8,128)(2,1)S(1)} collective-permute-done((bf16[4,320,640]{2,1,0:T(8,128)(2,1)}, bf16[4,320,640]{2,1,0:T(8,128)(2,1)S(1)}, u32[]{:S(2)}, u32[]{:S(2)}) %collective-permute-start.16) | collective-permute-done | bytes 1638432 | tf_op jit(solution)/shard_map/ppermute | solution.py:302
  96.4 3.4 %far_spread_kernel.1 = (f32[320,640]{1,0:T(8,128)S(1)}, bf16[320,640]{1,0:T(8,128)(2,1)S(1)}, bf16[320,640]{1,0:T(8,128)(2,1)S(1)}, bf16[320,640]{1,0:T(8,128)(2,1)S(1)}) custom-call(s32[6]{0:T(128)S(1)} %stack.31.where, f32[2,4,320,640]{3,2,1,0:T(8,128)} %get-tuple-element.67.both, bf16[4,320,640]{2,1,0:T(8,128)(2,1)S(1)} %collective-permute-done.16.got), custom_call_target="tpu_custom_call" | custom-call | flops 1 | bytes 1 | tf_op jit(solution)/shard_map/far_spread_kernel/pallas_call | solution.py:229
  100.0 4.1 %collective-permute-start.18 = (bf16[320,640]{1,0:T(8,128)(2,1)S(1)}, bf16[320,640]{1,0:T(8,128)(2,1)S(1)}, u32[]{:S(2)}, u32[]{:S(2)}) collective-permute-start(bf16[320,640]{1,0:T(8,128)(2,1)S(1)} %get-tuple-element.71), channel_id=1, source_target_pairs={{0,64},{32,96},{64,0},{96,32},{1,65},{33,97},{65,1},{97,33},{2,66}... | collective-permute-start | bytes 1228808 | tf_op jit(solution)/shard_map/ppermute | solution.py:304
  104.1 3.9 %collective-permute-start.15 = (bf16[320,640]{1,0:T(8,128)(2,1)S(1)}, bf16[320,640]{1,0:T(8,128)(2,1)S(1)}, u32[]{:S(2)}, u32[]{:S(2)}) collective-permute-start(bf16[320,640]{1,0:T(8,128)(2,1)S(1)} %get-tuple-element.61), channel_id=1, source_target_pairs={{1,17},{16,0},{3,19},{18,2},{5,21},{20,4},{7,23},{22,6},{9,25},{24... | collective-permute-start | bytes 1228808 | tf_op jit(solution)/shard_map/ppermute | solution.py:295
  108.0 4.7 %collective-permute-done.17.one = bf16[320,640]{1,0:T(8,128)(2,1)S(1)} collective-permute-done((bf16[320,640]{1,0:T(8,128)(2,1)S(1)}, bf16[320,640]{1,0:T(8,128)(2,1)S(1)}, u32[]{:S(2)}, u32[]{:S(2)}) %collective-permute-start.17) | collective-permute-done | bytes 409632 | tf_op jit(solution)/shard_map/ppermute | solution.py:304
  112.7 9.6 %collective-permute-done.18.two = bf16[320,640]{1,0:T(8,128)(2,1)S(1)} collective-permute-done((bf16[320,640]{1,0:T(8,128)(2,1)S(1)}, bf16[320,640]{1,0:T(8,128)(2,1)S(1)}, u32[]{:S(2)}, u32[]{:S(2)}) %collective-permute-start.18) | collective-permute-done | bytes 409632 | tf_op jit(solution)/shard_map/ppermute | solution.py:304
  123.2 2.1 %collective-permute-start.20 = (bf16[320,640]{1,0:T(8,128)(2,1)S(1)}, bf16[320,640]{1,0:T(8,128)(2,1)S(1)}, u32[]{:S(2)}, u32[]{:S(2)}) collective-permute-start(bf16[320,640]{1,0:T(8,128)(2,1)S(1)} %get-tuple-element.74), channel_id=1, source_target_pairs={{0,16},{16,0},{1,17},{17,1},{2,18},{18,2},{3,19},{19,3},{4,20},{20... | collective-permute-start | bytes 1228808 | tf_op jit(solution)/shard_map/ppermute | solution.py:306
  125.2 8.9 %collective-permute-done.20.got = bf16[320,640]{1,0:T(8,128)(2,1)S(1)} collective-permute-done((bf16[320,640]{1,0:T(8,128)(2,1)S(1)}, bf16[320,640]{1,0:T(8,128)(2,1)S(1)}, u32[]{:S(2)}, u32[]{:S(2)}) %collective-permute-start.20) | collective-permute-done | bytes 409632 | tf_op jit(solution)/shard_map/ppermute | solution.py:306
  135.2 3.5 %collective-permute-start.23 = (bf16[320,640]{1,0:T(8,128)(2,1)S(1)}, bf16[320,640]{1,0:T(8,128)(2,1)S(1)}, u32[]{:S(2)}, u32[]{:S(2)}) collective-permute-start(bf16[320,640]{1,0:T(8,128)(2,1)S(1)} %get-tuple-element.78), channel_id=1, source_target_pairs={{1,24},{3,18},{5,20},{7,22},{9,16},{11,26},{13,28},{15,30},{16,1},... | collective-permute-start | bytes 1228808 | tf_op jit(solution)/shard_map/ppermute | solution.py:338
  138.7 4.7 %collective-permute-start.21 = (bf16[320,320]{1,0:T(8,128)(2,1)S(1)}, bf16[320,320]{1,0:T(8,128)(2,1)S(1)}, u32[]{:S(2)}, u32[]{:S(2)}) collective-permute-start(bf16[320,320]{1,0:T(8,128)(2,1)S(1)} %get-tuple-element.76), channel_id=1, source_target_pairs={{2,32},{6,96},{10,40},{14,104},{32,2},{36,66},{40,10},{44,74},{64,... | collective-permute-start | bytes 614408 | tf_op jit(solution)/shard_map/ppermute | solution.py:325
  143.4 2.1 %collective-permute-start.22 = (bf16[320,320]{1,0:T(8,128)(2,1)S(1)}, bf16[320,320]{1,0:T(8,128)(2,1)S(1)}, u32[]{:S(2)}, u32[]{:S(2)}) collective-permute-start(bf16[320,320]{1,0:T(8,128)(2,1)S(1)} %get-tuple-element.77), channel_id=1, source_target_pairs={{2,40},{4,72},{6,104},{10,32},{12,64},{14,96},{32,10},{36,74},{38,... | collective-permute-start | bytes 614408 | tf_op jit(solution)/shard_map/ppermute | solution.py:325
  145.5 11.5 %collective-permute-done.21.first = bf16[320,320]{1,0:T(8,128)(2,1)S(1)} collective-permute-done((bf16[320,320]{1,0:T(8,128)(2,1)S(1)}, bf16[320,320]{1,0:T(8,128)(2,1)S(1)}, u32[]{:S(2)}, u32[]{:S(2)}) %collective-permute-start.21) | collective-permute-done | bytes 204832 | tf_op jit(solution)/shard_map/ppermute | solution.py:325
  157.0 1.9 %collective-permute-done.22.second = bf16[320,320]{1,0:T(8,128)(2,1)S(1)} collective-permute-done((bf16[320,320]{1,0:T(8,128)(2,1)S(1)}, bf16[320,320]{1,0:T(8,128)(2,1)S(1)}, u32[]{:S(2)}, u32[]{:S(2)}) %collective-permute-start.22) | collective-permute-done | bytes 204832 | tf_op jit(solution)/shard_map/ppermute | solution.py:325
  158.9 1.9 %finish_kernel.1 = f32[320,640]{1,0:T(8,128)} custom-call(s32[6]{0:T(128)S(1)} %stack.31.where, f32[320,640]{1,0:T(8,128)S(1)} %get-tuple-element.75.placed, bf16[320,320]{1,0:T(8,128)(2,1)S(1)} %collective-permute-done.21.first, bf16[320,320]{1,0:T(8,128)(2,1)S(1)} %collective-permute-done.22.second, bf16[320,640]{1,0:T(8,128)(2,1)S(1)} %collective-permute-done.23.across), custom_call_target="tpu_custom_call" | custom-call | flops 1 | bytes 1 | tf_op jit(solution)/shard_map/finish_kernel/pallas_call | solution.py:229
  (50 shorter events, 14.5 us)
Async XLA Ops:
  0.6 7.4 %copy-start.5 = (f32[1536]{0:T(1024)S(1)}, f32[1536]{0:T(1024)}, u32[]{:S(2)}) copy-start(f32[1536]{0:T(1024)} %param.7) | copy-start | bytes 18436
  0.6 7.4 %copy-start.6 = (s32[1536]{0:T(1024)S(1)}, s32[1536]{0:T(1024)}, u32[]{:S(2)}) copy-start(s32[1536]{0:T(1024)} %param.8) | copy-start | bytes 18436
  0.7 7.5 %copy-start.4 = (f32[16,1536]{1,0:T(8,128)S(1)}, f32[16,1536]{1,0:T(8,128)}, u32[]{:S(2)}) copy-start(f32[16,1536]{1,0:T(8,128)} %param.6) | copy-start | bytes 294916
  3.7 37.5 %collective-permute-start.1 = (bf16[768,640]{1,0:T(8,128)(2,1)}, bf16[768,640]{1,0:T(8,128)(2,1)S(1)}, u32[]{:S(2)}, u32[]{:S(2)}) collective-permute-start(bf16[768,640]{1,0:T(8,128)(2,1)} %get-tuple-element.47), channel_id=1, source_target_pairs={{0,2},{2,4},{4,6},{6,0},{1,3},{3,5},{5,7},{7,1},{8,10},{10,12},{12... | collective-permute-start | bytes 2949128 | tf_op jit(solution)/shard_map/ppermute | solution.py:258
  4.2 37.0 %collective-permute-start.2 = (bf16[768,640]{1,0:T(8,128)(2,1)}, bf16[768,640]{1,0:T(8,128)(2,1)}, u32[]{:S(2)}, u32[]{:S(2)}) collective-permute-start(bf16[768,640]{1,0:T(8,128)(2,1)} %get-tuple-element.81), channel_id=1, source_target_pairs={{0,1},{1,0},{2,3},{3,2},{4,5},{5,4},{6,7},{7,6},{8,9},{9,8},{10,11... | collective-permute-start | bytes 2949128 | tf_op jit(solution)/shard_map/ppermute | solution.py:259
  6.5 34.7 %collective-permute-start = (bf16[768,640]{1,0:T(8,128)(2,1)}, bf16[768,640]{1,0:T(8,128)(2,1)S(1)}, u32[]{:S(2)}, u32[]{:S(2)}) collective-permute-start(bf16[768,640]{1,0:T(8,128)(2,1)} %get-tuple-element.81), channel_id=1, source_target_pairs={{0,6},{2,0},{4,2},{6,4},{1,7},{3,1},{5,3},{7,5},{8,14},{10,8},{12,... | collective-permute-start | bytes 2949128 | tf_op jit(solution)/shard_map/ppermute | solution.py:257
  8.3 0.7 copy-start.3
  19.5 1.4 copy-start
  20.8 1.2 copy-start.1
  22.0 1.2 collective-permute-start.3
  23.3 6.0 %collective-permute-start.4 = (f32[640]{0:T(1024)S(1)}, f32[640]{0:T(1024)S(1)}, u32[]{:S(2)}, u32[]{:S(2)}) collective-permute-start(f32[640]{0:T(1024)S(1)} %add.20), channel_id=1, source_target_pairs={{0,16},{16,0},{1,17},{17,1},{2,18},{18,2},{3,19},{19,3},{4,20},{20... | collective-permute-start | bytes 7688 | tf_op jit(solution)/shard_map/ppermute | solution.py:270
  29.3 5.4 %collective-permute-start.7 = (f32[640]{0:T(1024)S(1)}, f32[640]{0:T(1024)S(1)}, u32[]{:S(2)}, u32[]{:S(2)}) collective-permute-start(f32[640]{0:T(1024)S(1)} %add.21), channel_id=1, source_target_pairs={{0,96},{32,0},{64,32},{96,64},{1,97},{33,1},{65,33},{97,65},{2,98}... | collective-permute-start | bytes 7688 | tf_op jit(solution)/shard_map/ppermute | solution.py:271
  33.3 4.8 %collective-permute-start.6 = (f32[640]{0:T(1024)S(1)}, f32[640]{0:T(1024)S(1)}, u32[]{:S(2)}, u32[]{:S(2)}) collective-permute-start(f32[640]{0:T(1024)S(1)} %add.21), channel_id=1, source_target_pairs={{0,32},{32,64},{64,96},{96,0},{1,33},{33,65},{65,97},{97,1},{2,34}... | collective-permute-start | bytes 7688 | tf_op jit(solution)/shard_map/ppermute | solution.py:271
  34.7 5.2 %collective-permute-start.5 = (f32[640]{0:T(1024)S(1)}, f32[640]{0:T(1024)}, u32[]{:S(2)}, u32[]{:S(2)}) collective-permute-start(f32[640]{0:T(1024)S(1)} %add.21), channel_id=1, source_target_pairs={{0,64},{32,96},{64,0},{96,32},{1,65},{33,97},{65,1},{97,33},{2,66}... | collective-permute-start | bytes 7688 | tf_op jit(solution)/shard_map/ppermute | solution.py:271
  41.2 10.1 %copy-start.2 = (f32[2,320,640]{2,1,0:T(8,128)S(1)}, f32[2,320,640]{2,1,0:T(8,128)}, u32[]{:S(2)}) copy-start(f32[2,320,640]{2,1,0:T(8,128)} %copy-done.1) | copy-start | bytes 4915204
  47.9 3.3 %collective-permute-start.11 = (bf16[3,320,640]{2,1,0:T(8,128)(2,1)S(1)}, bf16[3,320,640]{2,1,0:T(8,128)(2,1)S(1)}, u32[]{:S(2)}, u32[]{:S(2)}) collective-permute-start(bf16[3,320,640]{2,1,0:T(8,128)(2,1)S(1)} %get-tuple-element.53), channel_id=1, source_target_pairs={{0,8},{8,0},{1,9},{9,1},{2,10},{10,2},{3,11},{11,3},{4,12},{12,4},... | collective-permute-start | bytes 3686408 | tf_op jit(solution)/shard_map/ppermute | solution.py:287
  47.9 29.9 %collective-permute-start.8 = (bf16[768,640]{1,0:T(8,128)(2,1)}, bf16[768,640]{1,0:T(8,128)(2,1)S(1)}, u32[]{:S(2)}, u32[]{:S(2)}) collective-permute-start(bf16[768,640]{1,0:T(8,128)(2,1)} %get-tuple-element.47), channel_id=1, source_target_pairs={{0,1},{1,0},{2,3},{3,2},{4,5},{5,4},{6,7},{7,6},{8,9},{9,8},{10,11... | collective-permute-start | bytes 2949128 | tf_op jit(solution)/shard_map/ppermute | solution.py:275
  47.9 29.9 %collective-permute-start.9 = (bf16[768,640]{1,0:T(8,128)(2,1)S(1)}, bf16[768,640]{1,0:T(8,128)(2,1)S(1)}, u32[]{:S(2)}, u32[]{:S(2)}) collective-permute-start(bf16[768,640]{1,0:T(8,128)(2,1)S(1)} %collective-permute-done.above), channel_id=1, source_target_pairs={{0,6},{2,0},{4,2},{6,4},{1,7},{3,1},{5,3},{7,5},{8,14},{10,8},{12,... | collective-permute-start | bytes 2949128 | tf_op jit(solution)/shard_map/ppermute | solution.py:276
  49.6 28.3 %collective-permute-start.10 = (bf16[768,640]{1,0:T(8,128)(2,1)S(1)}, bf16[768,640]{1,0:T(8,128)(2,1)S(1)}, u32[]{:S(2)}, u32[]{:S(2)}) collective-permute-start(bf16[768,640]{1,0:T(8,128)(2,1)S(1)} %collective-permute-done.1.below), channel_id=1, source_target_pairs={{0,2},{2,4},{4,6},{6,0},{1,3},{3,5},{5,7},{7,1},{8,10},{10,12},{12... | collective-permute-start | bytes 2949128 | tf_op jit(solution)/shard_map/ppermute | solution.py:277
  53.7 13.1 %collective-permute-start.12 = (bf16[320,640]{1,0:T(8,128)(2,1)S(1)}, bf16[320,640]{1,0:T(8,128)(2,1)S(1)}, u32[]{:S(2)}, u32[]{:S(2)}) collective-permute-start(bf16[320,640]{1,0:T(8,128)(2,1)S(1)} %get-tuple-element.55), channel_id=1, source_target_pairs={{0,32},{32,64},{64,96},{96,0},{1,33},{33,65},{65,97},{97,1},{2,34}... | collective-permute-start | bytes 1228808 | tf_op jit(solution)/shard_map/ppermute | solution.py:289
  54.6 22.1 %collective-permute-start.13 = (bf16[320,640]{1,0:T(8,128)(2,1)S(1)}, bf16[320,640]{1,0:T(8,128)(2,1)S(1)}, u32[]{:S(2)}, u32[]{:S(2)}) collective-permute-start(bf16[320,640]{1,0:T(8,128)(2,1)S(1)} %get-tuple-element.56), channel_id=1, source_target_pairs={{0,64},{32,96},{64,0},{96,32},{1,65},{33,97},{65,1},{97,33},{2,66}... | collective-permute-start | bytes 1228808 | tf_op jit(solution)/shard_map/ppermute | solution.py:289
  66.8 10.7 %collective-permute-start.14 = (bf16[320,640]{1,0:T(8,128)(2,1)S(1)}, bf16[320,640]{1,0:T(8,128)(2,1)S(1)}, u32[]{:S(2)}, u32[]{:S(2)}) collective-permute-start(bf16[320,640]{1,0:T(8,128)(2,1)S(1)} %get-tuple-element.57), channel_id=1, source_target_pairs={{0,96},{32,0},{64,32},{96,64},{1,97},{33,1},{65,33},{97,65},{2,98}... | collective-permute-start | bytes 1228808 | tf_op jit(solution)/shard_map/ppermute | solution.py:289
  92.7 3.7 %collective-permute-start.16 = (bf16[4,320,640]{2,1,0:T(8,128)(2,1)}, bf16[4,320,640]{2,1,0:T(8,128)(2,1)S(1)}, u32[]{:S(2)}, u32[]{:S(2)}) collective-permute-start(bf16[4,320,640]{2,1,0:T(8,128)(2,1)} %get-tuple-element.68), channel_id=1, source_target_pairs={{0,8},{8,0},{1,9},{9,1},{2,10},{10,2},{3,11},{11,3},{4,12},{12,4},... | collective-permute-start | bytes 4915208 | tf_op jit(solution)/shard_map/ppermute | solution.py:302
  99.9 12.8 %collective-permute-start.17 = (bf16[320,640]{1,0:T(8,128)(2,1)S(1)}, bf16[320,640]{1,0:T(8,128)(2,1)S(1)}, u32[]{:S(2)}, u32[]{:S(2)}) collective-permute-start(bf16[320,640]{1,0:T(8,128)(2,1)S(1)} %get-tuple-element.70), channel_id=1, source_target_pairs={{0,32},{32,64},{64,96},{96,0},{1,33},{33,65},{65,97},{97,1},{2,34}... | collective-permute-start | bytes 1228808 | tf_op jit(solution)/shard_map/ppermute | solution.py:304
  100.0 22.4 %collective-permute-start.18 = (bf16[320,640]{1,0:T(8,128)(2,1)S(1)}, bf16[320,640]{1,0:T(8,128)(2,1)S(1)}, u32[]{:S(2)}, u32[]{:S(2)}) collective-permute-start(bf16[320,640]{1,0:T(8,128)(2,1)S(1)} %get-tuple-element.71), channel_id=1, source_target_pairs={{0,64},{32,96},{64,0},{96,32},{1,65},{33,97},{65,1},{97,33},{2,66}... | collective-permute-start | bytes 1228808 | tf_op jit(solution)/shard_map/ppermute | solution.py:304
  104.1 18.3 %collective-permute-start.19 = (bf16[320,640]{1,0:T(8,128)(2,1)S(1)}, bf16[320,640]{1,0:T(8,128)(2,1)S(1)}, u32[]{:S(2)}, u32[]{:S(2)}) collective-permute-start(bf16[320,640]{1,0:T(8,128)(2,1)S(1)} %get-tuple-element.72), channel_id=1, source_target_pairs={{0,96},{32,0},{64,32},{96,64},{1,97},{33,1},{65,33},{97,65},{2,98}... | collective-permute-start | bytes 1228808 | tf_op jit(solution)/shard_map/ppermute | solution.py:304
  104.1 21.2 %collective-permute-start.15 = (bf16[320,640]{1,0:T(8,128)(2,1)S(1)}, bf16[320,640]{1,0:T(8,128)(2,1)S(1)}, u32[]{:S(2)}, u32[]{:S(2)}) collective-permute-start(bf16[320,640]{1,0:T(8,128)(2,1)S(1)} %get-tuple-element.61), channel_id=1, source_target_pairs={{1,17},{16,0},{3,19},{18,2},{5,21},{20,4},{7,23},{22,6},{9,25},{24... | collective-permute-start | bytes 1228808 | tf_op jit(solution)/shard_map/ppermute | solution.py:295
  123.2 11.0 %collective-permute-start.20 = (bf16[320,640]{1,0:T(8,128)(2,1)S(1)}, bf16[320,640]{1,0:T(8,128)(2,1)S(1)}, u32[]{:S(2)}, u32[]{:S(2)}) collective-permute-start(bf16[320,640]{1,0:T(8,128)(2,1)S(1)} %get-tuple-element.74), channel_id=1, source_target_pairs={{0,16},{16,0},{1,17},{17,1},{2,18},{18,2},{3,19},{19,3},{4,20},{20... | collective-permute-start | bytes 1228808 | tf_op jit(solution)/shard_map/ppermute | solution.py:306
  135.2 23.7 %collective-permute-start.23 = (bf16[320,640]{1,0:T(8,128)(2,1)S(1)}, bf16[320,640]{1,0:T(8,128)(2,1)S(1)}, u32[]{:S(2)}, u32[]{:S(2)}) collective-permute-start(bf16[320,640]{1,0:T(8,128)(2,1)S(1)} %get-tuple-element.78), channel_id=1, source_target_pairs={{1,24},{3,18},{5,20},{7,22},{9,16},{11,26},{13,28},{15,30},{16,1},... | collective-permute-start | bytes 1228808 | tf_op jit(solution)/shard_map/ppermute | solution.py:338
  138.7 18.3 %collective-permute-start.21 = (bf16[320,320]{1,0:T(8,128)(2,1)S(1)}, bf16[320,320]{1,0:T(8,128)(2,1)S(1)}, u32[]{:S(2)}, u32[]{:S(2)}) collective-permute-start(bf16[320,320]{1,0:T(8,128)(2,1)S(1)} %get-tuple-element.76), channel_id=1, source_target_pairs={{2,32},{6,96},{10,40},{14,104},{32,2},{36,66},{40,10},{44,74},{64,... | collective-permute-start | bytes 614408 | tf_op jit(solution)/shard_map/ppermute | solution.py:325
  143.4 15.5 %collective-permute-start.22 = (bf16[320,320]{1,0:T(8,128)(2,1)S(1)}, bf16[320,320]{1,0:T(8,128)(2,1)S(1)}, u32[]{:S(2)}, u32[]{:S(2)}) collective-permute-start(bf16[320,320]{1,0:T(8,128)(2,1)S(1)} %get-tuple-element.77), channel_id=1, source_target_pairs={{2,40},{4,72},{6,104},{10,32},{12,64},{14,96},{32,10},{36,74},{38,... | collective-permute-start | bytes 614408 | tf_op jit(solution)/shard_map/ppermute | solution.py:325

commit v2 on v1

v2 whole, which is shorter than its diff:
```python
import functools

import jax
import jax.numpy as jnp
from jax import lax
from jax.experimental import pallas as pl
from jax.experimental.pallas import tpu as pltpu
from jax.sharding import Mesh, PartitionSpec as P

LOCAL = 16
SLOTS = 192
AXES = ("z", "yl", "core", "x", "yh")
HIGHEST = lax.Precision.HIGHEST
F32 = jnp.float32
BF16 = jnp.bfloat16
VMEM = pl.BlockSpec(memory_space=pltpu.VMEM)
SMEM = pl.BlockSpec(memory_space=pltpu.SMEM)
PARAMS = pltpu.CompilerParams(vmem_limit_bytes=16 << 20)
CHEAP = pl.CostEstimate(flops=1, transcendentals=0, bytes_accessed=1)


def shape(dims, dtype):
    return jax.ShapeDtypeStruct(dims, dtype)


def inner(a, b, contract, precision=None):
    return lax.dot_general(a, b, ((contract[:1], contract[1:]), ((), ())), precision=precision, preferred_element_type=F32)


def iota(dims, axis):
    return lax.broadcasted_iota(jnp.int32, dims, axis)


def eliminate_kernel(counts, block, observed, valid, high, low, residual):
    arcs = block.shape[0]
    eye = (iota((LOCAL, LOCAL), 0) == iota((LOCAL, LOCAL), 1)).astype(F32)
    live, masked, grams = [], [], []
    for a in range(arcs):
        inside = (iota((1, SLOTS), 1) < counts[a]).astype(F32)
        live.append(inside * valid[a : a + 1, :].astype(F32))
        masked.append(block[a] * live[a])
        grams.append((inner(masked[a], block[a], (1, 1), HIGHEST) + eye)[None])
    gram = jnp.concatenate(grams, 0)
    rows, cols = iota(gram.shape, 1), iota(gram.shape, 2)
    for p in range(LOCAL):
        column = gram[:, :, p : p + 1]
        pivot = 1.0 / gram[:, p : p + 1, p : p + 1]
        row = gram[:, p : p + 1, :] * pivot
        swept = jnp.where(rows == p, row, gram - column * row)
        edge = jnp.where(rows == p, pivot, -column * pivot)
        gram = jnp.where(cols == p, edge, swept)
    diagonal = iota((SLOTS, SLOTS), 0) == iota((SLOTS, SLOTS), 1)
    for a in range(arcs):
        weights = jnp.dot(gram[a], masked[a], precision=HIGHEST, preferred_element_type=F32)
        fitted = inner(masked[a], weights, (0, 0), HIGHEST)
        elim = jnp.where(diagonal, live[a], 0.0) - fitted
        top = elim.astype(BF16)
        high[a * SLOTS : (a + 1) * SLOTS, :] = top
        low[a * SLOTS : (a + 1) * SLOTS, :] = (elim - top.astype(F32)).astype(BF16)
        y = observed[a : a + 1, :]
        solved = jnp.sum(weights * y, axis=1, keepdims=True)
        residual[a : a + 1, :] = live[a] * (y - jnp.sum(block[a] * solved, axis=0, keepdims=True))


def eliminate(local, observed, valid, counts):
    arcs = counts.shape[0]
    block = local.reshape(LOCAL, arcs, SLOTS).transpose(1, 0, 2)
    return pl.pallas_call(
        eliminate_kernel,
        out_shape=(
            shape((arcs * SLOTS, SLOTS), BF16),
            shape((arcs * SLOTS, SLOTS), BF16),
            shape((arcs, SLOTS), F32),
        ),
        in_specs=[SMEM, VMEM, VMEM, VMEM],
        out_specs=(VMEM, VMEM, VMEM),
        compiler_params=PARAMS,
        cost_estimate=CHEAP,
        name="eliminate",
    )(counts, block, observed.reshape(arcs, SLOTS), valid.reshape(arcs, SLOTS))


def rounded(high, low, rows):
    first = jnp.dot(high, rows, preferred_element_type=F32)
    return (first + jnp.dot(low, rows, preferred_element_type=F32)).astype(BF16)


def project_into(out, high, low, rows, begin, count, source):
    for i in range(count):
        to = slice((begin + i) * SLOTS, (begin + i + 1) * SLOTS)
        at = slice((source + i) * SLOTS, (source + i + 1) * SLOTS)
        out[to, :] = rounded(high[to, :], low[to, :], rows[at, :])


def project_half(out, high, low, rows, first, count):
    for i in range(count):
        at = slice(i * SLOTS, (i + 1) * SLOTS)
        arc = slice((first + i) * SLOTS, (first + i + 1) * SLOTS)
        out[at, :] = rounded(high[arc, :], low[arc, :], rows[at, :])


def split(core, result, keep, send):
    half = result.shape[0] // 2
    keep[...] = jnp.where(core == 0, result[:half], result[half:])
    send[...] = jnp.where(core == 0, result[half:], result[:half]).astype(BF16)


def parts_of(value):
    one = value.astype(BF16).astype(F32)
    two = (value - one).astype(BF16).astype(F32)
    three = value - one - two
    line = iota((16, value.shape[1]), 0)
    stack = jnp.where(line == 0, one, jnp.where(line == 1, two, jnp.where(line == 2, three, 0.0)))
    return stack.astype(BF16)


def whole_of(block):
    parts = block.astype(F32)
    return (parts[0:1] + parts[1:2]) + parts[2:3]


def own_kernel(where, high, low, residual, rows, out, turned, keep, send, rhs):
    arcs, half = residual.shape[0], keep.shape[0]
    project_into(out, high, low, rows, 0, arcs, 0)
    total = jnp.zeros((1, rows.shape[1]), F32)
    for a in range(arcs):
        stack = parts_of(residual[a : a + 1, :])
        part = jnp.dot(stack, out[a * SLOTS : (a + 1) * SLOTS, :], preferred_element_type=F32)
        total = total + jnp.sum(part, axis=0, keepdims=True)
    rhs[...] = total
    send[half:, :] = parts_of(total)
    turned[...] = out[...].T
    result = jnp.dot(turned[...], out[...], preferred_element_type=F32)
    split(where[0], result, keep, send.at[pl.ds(0, half), :])


def near_kernel(where, high, low, own, above, below, near_top, near_bottom, keep, send):
    arcs = high.shape[0] // SLOTS
    top = above.shape[0]
    project_half(near_top, high, low, above, 0, arcs // 2)
    project_half(near_bottom, high, low, below, arcs // 2, arcs // 2)
    for piece, near in enumerate((near_top, near_bottom)):
        result = jnp.dot(own[:, piece * top : (piece + 1) * top], near[...], preferred_element_type=F32)
        split(where[0], result, keep.at[piece], send.at[piece])


def middle_kernel(where, high, low, near, rows, flip, turned, keep, send):
    top = rows.shape[0]
    project_into(flip, high, low, rows, 0, top // SLOTS, 0)
    turned[...] = flip[...].T
    split(where[0], jnp.dot(turned[...], near[...], preferred_element_type=F32), keep, send)


def far_rows(where, chunk, own, near, done, done_send, flips, turned, two, keep, send):
    size, half = keep.shape[1], own.shape[0] // 2
    top = two.shape[0] // 2
    core, cut_flip, cut_two = where[0], where[2], where[3]
    upper, lower = slice(0, top), slice(top, 2 * top)
    rows = slice(chunk * size, (chunk + 1) * size)

    def lines(ref):
        return jnp.concatenate([ref[rows, :], ref[half + chunk * size : half + (chunk + 1) * size, :]], 0)

    def times(a, b):
        return jnp.dot(a, b, preferred_element_type=F32)

    own_lines, flip_top, flip_bottom = lines(own), lines(turned[0]), lines(turned[1])
    keep[1] = done[rows, :]
    send[1] = done_send[rows, :]
    split(core, times(flip_bottom, near[...]), keep.at[3], send.at[3])

    def quadrants(result, cut, slot, columns):
        first = jnp.where(cut == 0, result[:size, :half], result[:size, half:])
        second = jnp.where(cut == 1, result[size:, :half], result[size:, half:])
        keep[slot, :, columns] = jnp.where(core == 0, first, second)
        send[slot, :, columns] = jnp.where(core == 0, second, first).astype(BF16)

    quadrants(
        times(own_lines[:, upper], flips[0][...]) + times(own_lines[:, lower], flips[1][...]),
        cut_flip, 0, slice(0, half),
    )
    keep[0, :, half:] = jnp.zeros((size, half), F32)
    send[0, :, half:] = jnp.zeros((size, half), BF16)
    quadrants(times(own_lines, two[...]), cut_two, 2, slice(0, half))
    quadrants(
        times(flip_top, two[upper, :]) + times(flip_bottom, two[lower, :]),
        cut_two, 2, slice(half, 2 * half),
    )


def far_kernel(
    where, high, low, own, near, done, done_send, flip_top, top_turned, rows, above, below,
    keep, send, flip_bottom, bottom_turned, two,
):
    arcs = high.shape[0] // SLOTS
    project_half(flip_bottom, high, low, rows, arcs // 2, arcs // 2)
    bottom_turned[...] = flip_bottom[...].T
    project_into(two, high, low, above, 0, arcs // 2, 0)
    project_into(two, high, low, below, arcs // 2, arcs // 2, 0)
    flips, turned = (flip_top, flip_bottom), (top_turned, bottom_turned)
    far_rows(where, 0, own, near, done, done_send, flips, turned, two, keep, send)


def far_rest_kernel(
    where, own, near, done, done_send, flip_top, top_turned, flip_bottom, bottom_turned, two, keep, send
):
    flips, turned = (flip_top, flip_bottom), (top_turned, bottom_turned)
    far_rows(where, 1, own, near, done, done_send, flips, turned, two, keep, send)


def tdot(a, b):
    return inner(a, b, (0, 0))


def spread(where, sums, mine, ups):
    delta = where[1]
    mine[...] = sums[delta]
    for k, up in enumerate(ups, 1):
        up[...] = sums[(delta + k) % 4].astype(BF16)


def near_spread_kernel(where, own, keep, rhs, own_got, got, mine, up1, up2, up3, rhs_sum, sums):
    half = own.shape[0]
    sums[0] = own[...] + own_got[:half, :].astype(F32)
    sums[1] = keep[0] + got[0].astype(F32)
    sums[2] = jnp.zeros(sums.shape[1:], F32)
    sums[3] = keep[1] + got[1].astype(F32)
    spread(where, sums, mine, (up1, up2, up3))
    rhs_sum[...] = rhs[...] + whole_of(own_got[half:, :])


def far_spread_kernel(where, keep, got, rhs, mine, up1, up2, up3):
    delta, size = where[1], keep.shape[1]
    mine[...] = keep[delta] + got[delta].astype(F32)
    for k, up in enumerate((up1, up2, up3), 1):
        slot = (delta + k) % 4
        up[:size, :] = (keep[slot] + got[slot].astype(F32)).astype(BF16)
        if up.shape[0] > size:
            up[size:, :] = parts_of(rhs[...])


def near_total_kernel(mine, one, two, three, total, send):
    total[...] = ((mine[...] + one[...].astype(F32)) + two[...].astype(F32)) + three[...].astype(F32)
    send[...] = total[...].astype(BF16)


def far_total_kernel(where, rhs, *refs):
    keep, send, rhs_sum = refs[-3:]
    half = keep.shape[0]
    opposite, same = where[1] == 2, where[4] == 1
    first = 0
    for chunk in range(len(refs) // 4):
        mine, one, two, three = refs[4 * chunk : 4 * chunk + 4]
        size = mine.shape[0]
        one, two, three = (up[:size, :].astype(F32) for up in (one, two, three))
        total = ((mine[...] + one) + two) + three
        rows = slice(first, first + size)
        first += size
        turned = jnp.concatenate([total[:, half:], total[:, :half]], 1)
        send[rows, :] = jnp.where(jnp.logical_and(opposite, same), turned, total).astype(BF16)
        keep[rows, :] = jnp.where(jnp.logical_and(opposite, jnp.logical_not(same)), turned, total)
    one, two, three = (whole_of(up[refs[0].shape[0] :, :]) for up in refs[1:4])
    total = (rhs[...] + two) + (one + three)
    rhs_sum[...] = total
    send[half:, :] = parts_of(total)


def place_kernel(where, near, near_got, keep, got, rhs, placed, mirror, mirror_quad, quad_send, rhs_sum):
    half = placed.shape[0]
    core, delta, same, right = where[0], where[1], where[4] == 1, where[5] == 1
    late = keep[...] + got[:half, :].astype(F32)
    early = near[...] + near_got[...].astype(F32)
    total = jnp.where(jnp.logical_and(same, delta != 2), early, late)
    quad = jnp.logical_or(delta == 2, jnp.logical_and(delta == 0, jnp.logical_not(same)))
    left_side = jnp.where(jnp.logical_and(quad, right), 0.0, total[:, :half])
    right_side = jnp.where(quad, jnp.where(right, total[:, :half], 0.0), total[:, half:])
    placed[:, :half] = left_side
    placed[:, half:] = right_side
    mirror[...] = placed[...].astype(BF16)
    mirror_quad[...] = total[:, :half].astype(BF16)
    quad_send[...] = jnp.where(core == 0, right_side, left_side).astype(BF16)
    rhs_sum[...] = rhs[...] + whole_of(got[half:, :])


def turn_kernel(where, placed, got, turned, across):
    half = placed.shape[0]
    core, diagonal = where[0], where[1] == 0
    mine = jnp.where(core == 0, placed[:, :half], placed[:, half:])
    other = got[...].astype(F32)
    first = jnp.where(core == 0, mine, other).T
    second = jnp.where(core == 0, other, mine).T
    turned[:, :half] = first
    turned[:, half:] = second
    across[...] = jnp.where(diagonal, placed[...], turned[...]).astype(BF16)


def finish_kernel(where, placed, turned, mirror, mirror_quad, across, out):
    half = out.shape[0]
    diagonal, opposite, same = where[1] == 0, where[1] == 2, where[4] == 1
    left = where[5] == 1
    for side, columns in enumerate((slice(0, half), slice(half, 2 * half))):
        far = across[:, columns].astype(F32)
        quad = jnp.where(left == (side == 0), mirror_quad[...].astype(F32), 0.0)
        near = jnp.where(opposite, quad, mirror[:, columns].astype(F32))
        own = turned[:, columns]
        direct = jnp.where(diagonal, jnp.where(same, placed[:, columns], far), near)
        other = jnp.where(diagonal, jnp.where(same, 0.0, own), jnp.where(same, own, far))
        out[:, columns] = direct + other


def call(kernel, outs, *args, scalars=True, scratch=(), vmem=12):
    return pl.pallas_call(
        kernel,
        out_shape=outs,
        in_specs=[SMEM if scalars and i == 0 else VMEM for i in range(len(args))],
        out_specs=jax.tree.map(lambda _: VMEM, outs),
        scratch_shapes=scratch,
        compiler_params=pltpu.CompilerParams(vmem_limit_bytes=vmem << 20),
        cost_estimate=CHEAP,
        name=kernel.__name__,
    )(*args)


def body(sizes, design, local, observed, valid, counts):
    nz, nyl, ncore, nx, nyh = sizes
    z, yl, core, x, yh = (lax.axis_index(name) for name in AXES)
    delta = (z - x) % nx
    rows, width = design.shape
    half, top = width // 2, rows // 2
    down = [(i, (i - 1) % nx) for i in range(nx)]
    up = [(i, (i + 1) % nx) for i in range(nx)]
    swap = [(0, 1), (1, 0)]
    turn = lambda k: [(i, (i + k) % nz) for i in range(nz)]
    high_x = (x >= nx // 2).astype(jnp.int32)
    same = (yl == yh).astype(jnp.int32)
    right = core ^ jnp.where(delta == 2, high_x, yh)
    where = jnp.stack([core, delta, yh, high_x, same, right]).astype(jnp.int32)

    upper, lower = design[:top], design[top:]
    above = lax.ppermute(upper, "x", down)
    below = lax.ppermute(lower, "x", up)
    flip_top = lax.ppermute(upper, "yh", swap)

    wide, sent = shape((half, width), F32), shape((half, width), BF16)
    full, sideways = shape((rows, width), BF16), shape((width, rows), BF16)

    row, low_rows = shape((1, width), F32), 16
    a_high, a_low, residual = eliminate(local, observed, valid, counts)
    own_rows, own, own_keep, own_send, rhs = call(
        own_kernel,
        (full, sideways, wide, shape((half + low_rows, width), BF16), row),
        where, a_high, a_low, residual, design,
        vmem=24,
    )
    del own_rows
    own_got = lax.ppermute(own_send, "core", swap)

    above, below, flip_top, own, lower, own_got = lax.optimization_barrier(
        (above, below, flip_top, own, lower, own_got)
    )
    flip_bottom = lax.ppermute(lower, "yh", swap)
    above2 = lax.ppermute(above, "x", down)
    below2 = lax.ppermute(below, "x", up)

    top_full, top_sideways = shape((top, width), BF16), shape((width, top), BF16)
    near_top, near_bottom, keep, send = call(
        near_kernel,
        (top_full, top_full, shape((2, half, width), F32), shape((2, half, width), BF16)),
        where, a_high, a_low, own, above, below,
        vmem=24,
    )
    got = lax.ppermute(send, "core", swap)
    mine, *ups, rhs = call(
        near_spread_kernel, (wide, sent, sent, sent, row), where, own_keep, keep, rhs, own_got, got,
        scratch=(pltpu.VMEM((nz, half, width), F32),),
    )
    flip_top, near_top, rhs = lax.optimization_barrier((flip_top, near_top, rhs))
    early_turn = lambda k: [
        (a * nx + b, (a + k) % nz * nx + b) for a in range(nz) for b in range(nx) if (a + k - b) % nx != 2
    ]
    ups = [lax.ppermute(v, ("z", "x"), early_turn(k)) for k, v in enumerate(ups, 1)]
    flip_top, flip_top_turned, up_keep, up_send = call(
        middle_kernel, (top_full, top_sideways, wide, sent), where, a_high, a_low, near_top, flip_top,
        vmem=16,
    )

    flip_bottom, above2, below2, flip_top, ups = lax.optimization_barrier(
        (flip_bottom, above2, below2, flip_top, ups)
    )
    early, send = call(near_total_kernel, (wide, sent), mine, *ups, scalars=False)
    early_got = lax.ppermute(send, ("yl", "yh"), [(1, 3), (2, 0)])
    chunks = 2
    size = half // chunks
    pieces = (shape((nz, size, width), F32), shape((nz, size, width), BF16))
    keep, send, flip_bottom, flip_bottom_turned, two = call(
        far_kernel,
        pieces + (top_full, top_sideways, full),
        where, a_high, a_low, own, near_bottom, up_keep, up_send, flip_top, flip_top_turned,
        flip_bottom, above2, below2,
        vmem=28,
    )
    keeps, gots = [keep], [lax.ppermute(send, "core", swap)]
    keep, send = call(
        far_rest_kernel, pieces,
        where, own, near_bottom, up_keep, up_send, flip_top, flip_top_turned, flip_bottom, flip_bottom_turned, two,
        vmem=24,
    )
    keep, send, gots[0] = lax.optimization_barrier((keep, send, gots[0]))
    keeps.append(keep)
    gots.append(lax.ppermute(send, "core", swap))

    late = []
    for chunk, (keep, got) in enumerate(zip(keeps, gots)):
        up = shape((size + (low_rows if chunk == 0 else 0), width), BF16)
        mine, *ups = call(far_spread_kernel, (shape((size, width), F32), up, up, up), where, keep, got, rhs)
        late += [mine] + [lax.ppermute(v, "z", turn(k)) for k, v in enumerate(ups, 1)]
    late, early_got = lax.optimization_barrier((late, early_got))
    keep, send, rhs = call(
        far_total_kernel, (wide, shape((half + low_rows, width), BF16), row), where, rhs, *late
    )
    got = lax.ppermute(send, "yl", swap)

    quad = shape((half, half), BF16)
    placed, mirror, mirror_quad, send, rhs = call(
        place_kernel, (wide, sent, quad, quad, row), where, early, early_got, keep, got, rhs
    )
    pairs = [(a * nx + b, b * nx + a) for a in range(nz) for b in range(nx) if (a - b) % 2]
    mirror = lax.ppermute(mirror, ("z", "x"), pairs)
    pairs = [(a * nx + b, b * nx + a) for a in range(nz) for b in range(nx) if (a - b) % nx == 2]
    mirror_quad = lax.ppermute(mirror_quad, ("z", "x"), pairs)
    got = lax.ppermute(send, "core", swap)
    turned, across = call(turn_kernel, (wide, sent), where, placed, got)
    across = lax.ppermute(across, ("yl", "yh"), [(1, 2), (2, 1)])
    out = call(finish_kernel, wide, where, placed, turned, mirror, mirror_quad, across)
    return out, rhs[0]


def solution(mesh):
    sizes = (4, 2, 2, 4, 2)
    grid = Mesh(mesh.devices.reshape(sizes), AXES)
    arc, col = ("z", "yl", "core"), ("x", "yh")

    def run(design, local_design, observed, valid_mask, counts):
        return jax.shard_map(
            functools.partial(body, sizes),
            mesh=grid,
            in_specs=(P(arc, col), P(None, arc), P(arc), P(arc), P(arc)),
            out_specs=(P(arc, col), P(col)),
            check_vma=False,
        )(design, local_design, observed, valid_mask, counts)

    return run
```

time: 163 us -> 143 us (0.88); the launches traced: 161 us -> 143 us
  waiting for transfers between devices: 66.5 us -> 53.4 us
  Pallas kernels: 42 us -> 34.4 us
  starting transfers between devices: 43.5 us -> 48.2 us
    ppermute x14 -> x15, waiting for transfers between devices: 53.8 us -> 29.1 us  [the longest x6 11.8 us: body(): lax.ppermute(v, 'z', turn(k))]
    pallas_call x9 -> x13, Pallas kernels: 36.4 us -> 28.7 us  [call(): pl.pallas_call(kernel, out_shape=outs, in_specs=[SMEM if scalars and i ==...]
    ppermute x14 -> x15, starting transfers between devices: 29.9 us -> 36.6 us  [the longest x3 15.4 us: body(): lax.ppermute(v, ('z', 'x'), early_turn(k))]
    ppermute x1, waiting for transfers between devices: 0.01 us -> 5.84 us  [body(): below = lax.ppermute(lower, 'x', up)]
    ppermute x1, waiting for transfers between devices: 0.01 us -> 4.24 us  [body(): flip_bottom = lax.ppermute(lower, 'yh', swap)]
    ppermute x2, waiting for transfers between devices: 3.71 us -> 0.01 us  [body(): got = lax.ppermute(send, 'core', swap)]
    ppermute x1, starting transfers between devices: 2.09 us -> 0.09 us  [body(): got = lax.ppermute(send, 'yl', swap)]
    ppermute x1, waiting for transfers between devices: 0.01 us -> 1.72 us  [body(): above = lax.ppermute(upper, 'x', down)]
  transfers between devices with their start and end apart: 24 -> 25, of which waited for: 14 -> 13; matrix products, arithmetic and copies ran while one was open for 1% -> 1% of each run, Pallas kernels for 9% -> 17%
where the time goes in v2:
time: 143 us
  waiting for transfers between devices  53.4 us (37%)
  starting transfers between devices  48.2 us (34%)
  Pallas kernels  34.4 us (24%)
  local copies, waits for them, and re-layouts  5.43 us (4%)
    pallas_call x13, Pallas kernels, call(): pl.pallas_call(kernel, out_shape=outs, in_specs=[SMEM if scalars and i ==...  28.7 us
    ppermute x3, starting transfers between devices, body(): lax.ppermute(v, ('z', 'x'), early_turn(k))  15.4 us
    ppermute x6, waiting for transfers between devices, body(): lax.ppermute(v, 'z', turn(k))  11.8 us
    ppermute x1, waiting for transfers between devices, body(): mirror = lax.ppermute(mirror, ('z', 'x'), pairs)  11.3 us
    ppermute x6, starting transfers between devices, body(): lax.ppermute(v, 'z', turn(k))  11.2 us
    ppermute x1, waiting for transfers between devices, body(): got = lax.ppermute(send, 'yl', swap)  10.6 us
    ppermute x1, waiting for transfers between devices, body(): below = lax.ppermute(lower, 'x', up)  5.84 us
    pallas_call x1, Pallas kernels, eliminate(): pl.pallas_call(eliminate_kernel, out_shape=(shape((arcs * SLOTS, SLOTS),...  5.61 us
  transfers between devices with their start and end apart: 25, of which 13 were waited for; matrix products, arithmetic and copies ran while one was open for 1% of the time, Pallas kernels for 17%

profile of v2, /device:TPU:14, one launch (start us, length us, event | category | flops | bytes accessed | tf_op | source)
XLA Modules:
  0.0 143.0 jit_solution(16415130262261895281)
XLA Ops:
  0.7 3.1 %fusion = (bf16[768,640]{1,0:T(8,128)(2,1)}, bf16[768,640]{1,0:T(8,128)(2,1)}) fusion(bf16[1536,640]{1,0:T(8,128)(2,1)} %rows.1), kind=kLoop, calls=%fused_computation.1 | loop fusion | bytes 3932160 | tf_op jit(solution)/shard_map/slice | solution.py:339
  4.3 2.3 %collective-permute-start.2 = (bf16[768,640]{1,0:T(8,128)(2,1)}, bf16[768,640]{1,0:T(8,128)(2,1)}, u32[]{:S(2)}, u32[]{:S(2)}) collective-permute-start(bf16[768,640]{1,0:T(8,128)(2,1)} %get-tuple-element.153), channel_id=1, source_target_pairs={{0,1},{1,0},{2,3},{3,2},{4,5},{5,4},{6,7},{7,6},{8,9},{9,8},{10,11... | collective-permute-start | bytes 2949128 | tf_op jit(solution)/shard_map/ppermute | solution.py:342
  6.6 1.5 %collective-permute-start = (bf16[768,640]{1,0:T(8,128)(2,1)}, bf16[768,640]{1,0:T(8,128)(2,1)}, u32[]{:S(2)}, u32[]{:S(2)}) collective-permute-start(bf16[768,640]{1,0:T(8,128)(2,1)} %get-tuple-element.153), channel_id=1, source_target_pairs={{0,6},{2,0},{4,2},{6,4},{1,7},{3,1},{5,3},{7,5},{8,14},{10,8},{12,... | collective-permute-start | bytes 2949128 | tf_op jit(solution)/shard_map/ppermute | solution.py:340
  9.1 5.6 %eliminate.1 = (bf16[1536,192]{1,0:T(8,128)(2,1)S(1)}, bf16[1536,192]{1,0:T(8,128)(2,1)S(1)}, f32[8,192]{1,0:T(8,128)S(1)}) custom-call(s32[8]{0:T(128)S(1)} %copy-done.3, f32[8,16,192]{2,1,0:T(8,128)S(1)} %bitcast.9, f32[8,192]{1,0:T(8,128)S(1)} %reshape.14.observed, s32[8,192]{1,0:T(8,128)S(1)} %reshape.15.valid), custom_call_target="tpu_custom_call" | custom-call | flops 1 | bytes 1 | tf_op jit(solution)/shard_map/eliminate/pallas_call | solution.py:68
  16.1 3.8 %own_kernel.1 = (bf16[1536,640]{1,0:T(8,128)(2,1)}, bf16[640,1536]{1,0:T(8,128)(2,1)S(1)}, f32[320,640]{1,0:T(8,128)S(1)}, bf16[336,640]{1,0:T(8,128)(2,1)S(1)}, f32[1,640]{1,0:T(1,128)S(1)}) custom-call(s32[6]{0:T(128)S(1)} %stack.31.where, bf16[1536,192]{1,0:T(8,128)(2,1)S(1)} %get-tuple-element.77.high, bf16[1536,192]{1,0:T(8,128)(2,1)S(1)} %get-tuple-element.78.low, ...), custom_call_target="tpu_custom_call" | custom-call | flops 1 | bytes 1 | tf_op jit(solution)/shard_map/own_kernel/pallas_call | solution.py:312
  20.0 1.8 %collective-permute-done.3.own_got = bf16[336,640]{1,0:T(8,128)(2,1)S(1)} collective-permute-done((bf16[336,640]{1,0:T(8,128)(2,1)S(1)}, bf16[336,640]{1,0:T(8,128)(2,1)S(1)}, u32[]{:S(2)}, u32[]{:S(2)}) %collective-permute-start.3) | collective-permute-done | bytes 430112 | tf_op jit(solution)/shard_map/ppermute | solution.py:356
  21.8 5.8 %collective-permute-done.1.below = bf16[768,640]{1,0:T(8,128)(2,1)} collective-permute-done((bf16[768,640]{1,0:T(8,128)(2,1)}, bf16[768,640]{1,0:T(8,128)(2,1)}, u32[]{:S(2)}, u32[]{:S(2)}) %collective-permute-start.1) | collective-permute-done | bytes 983072 | tf_op jit(solution)/shard_map/ppermute | solution.py:341
  27.6 1.7 %collective-permute-done.2.rows = bf16[768,640]{1,0:T(8,128)(2,1)} collective-permute-done((bf16[768,640]{1,0:T(8,128)(2,1)}, bf16[768,640]{1,0:T(8,128)(2,1)}, u32[]{:S(2)}, u32[]{:S(2)}) %collective-permute-start.2) | collective-permute-done | bytes 983072 | tf_op jit(solution)/shard_map/ppermute | solution.py:342
  29.3 1.7 %collective-permute-done.above = bf16[768,640]{1,0:T(8,128)(2,1)} collective-permute-done((bf16[768,640]{1,0:T(8,128)(2,1)}, bf16[768,640]{1,0:T(8,128)(2,1)}, u32[]{:S(2)}, u32[]{:S(2)}) %collective-permute-start) | collective-permute-done | bytes 983072 | tf_op jit(solution)/shard_map/ppermute | solution.py:340
  32.3 4.4 %near_kernel.1 = (bf16[768,640]{1,0:T(8,128)(2,1)S(1)}, bf16[768,640]{1,0:T(8,128)(2,1)S(1)}, f32[2,320,640]{2,1,0:T(8,128)S(1)}, bf16[2,320,640]{2,1,0:T(8,128)(2,1)S(1)}) custom-call(s32[6]{0:T(128)S(1)} %stack.31.where, bf16[1536,192]{1,0:T(8,128)(2,1)S(1)} %get-tuple-element.77.high, bf16[1536,192]{1,0:T(8,128)(2,1)S(1)} %get-tuple-element.78.low, ...), custom_call_target="tpu_custom_call" | custom-call | flops 1 | bytes 1 | tf_op jit(solution)/shard_map/near_kernel/pallas_call | solution.py:312
  37.7 2.3 %collective-permute-start.7 = (bf16[768,640]{1,0:T(8,128)(2,1)}, bf16[768,640]{1,0:T(8,128)(2,1)S(1)}, u32[]{:S(2)}, u32[]{:S(2)}) collective-permute-start(bf16[768,640]{1,0:T(8,128)(2,1)} %collective-permute-done.1.below), channel_id=1, source_target_pairs={{0,2},{2,4},{4,6},{6,0},{1,3},{3,5},{5,7},{7,1},{8,10},{10,12},{12... | collective-permute-start | bytes 2949128 | tf_op jit(solution)/shard_map/ppermute | solution.py:363
  42.5 8.0 %collective-permute-start.9 = (bf16[320,640]{1,0:T(8,128)(2,1)S(1)}, bf16[320,640]{1,0:T(8,128)(2,1)S(1)}, u32[]{:S(2)}, u32[]{:S(2)}) collective-permute-start(bf16[320,640]{1,0:T(8,128)(2,1)S(1)} %get-tuple-element.99), channel_id=1, source_target_pairs={{2,66},{4,68},{6,70},{32,96},{36,100},{38,102},{64,0},{66,2},{70,6... | collective-permute-start | bytes 1228808 | tf_op jit(solution)/shard_map/ppermute | solution.py:381
  50.5 4.2 %collective-permute-done.5.rows = bf16[768,640]{1,0:T(8,128)(2,1)S(1)} collective-permute-done((bf16[768,640]{1,0:T(8,128)(2,1)}, bf16[768,640]{1,0:T(8,128)(2,1)S(1)}, u32[]{:S(2)}, u32[]{:S(2)}) %collective-permute-start.5) | collective-permute-done | bytes 983072 | tf_op jit(solution)/shard_map/ppermute | solution.py:361
  54.7 6.1 %collective-permute-start.10 = (bf16[320,640]{1,0:T(8,128)(2,1)S(1)}, bf16[320,640]{1,0:T(8,128)(2,1)S(1)}, u32[]{:S(2)}, u32[]{:S(2)}) collective-permute-start(bf16[320,640]{1,0:T(8,128)(2,1)S(1)} %get-tuple-element.100), channel_id=1, source_target_pairs={{0,96},{4,100},{6,102},{32,0},{34,2},{38,6},{64,32},{66,34},{68,36... | collective-permute-start | bytes 1228808 | tf_op jit(solution)/shard_map/ppermute | solution.py:381
  60.9 2.8 %middle_kernel.1 = (bf16[768,640]{1,0:T(8,128)(2,1)S(1)}, bf16[640,768]{1,0:T(8,128)(2,1)S(1)}, f32[320,640]{1,0:T(8,128)S(1)}, bf16[320,640]{1,0:T(8,128)(2,1)S(1)}) custom-call(s32[6]{0:T(128)S(1)} %stack.31.where, bf16[1536,192]{1,0:T(8,128)(2,1)S(1)} %get-tuple-element.77.high, bf16[1536,192]{1,0:T(8,128)(2,1)S(1)} %get-tuple-element.78.low, ...), custom_call_target="tpu_custom_call" | custom-call | flops 1 | bytes 1 | tf_op jit(solution)/shard_map/middle_kernel/pallas_call | solution.py:312
  63.7 2.9 %collective-permute-done.9.two = bf16[320,640]{1,0:T(8,128)(2,1)S(1)} collective-permute-done((bf16[320,640]{1,0:T(8,128)(2,1)S(1)}, bf16[320,640]{1,0:T(8,128)(2,1)S(1)}, u32[]{:S(2)}, u32[]{:S(2)}) %collective-permute-start.9) | collective-permute-done | bytes 409632 | tf_op jit(solution)/shard_map/ppermute | solution.py:381
  67.9 5.5 %far_kernel.1 = (f32[4,160,640]{2,1,0:T(8,128)S(1)}, bf16[4,160,640]{2,1,0:T(8,128)(2,1)S(1)}, bf16[768,640]{1,0:T(8,128)(2,1)S(1)}, bf16[640,768]{1,0:T(8,128)(2,1)S(1)}, bf16[1536,640]{1,0:T(8,128)(2,1)S(1)}) custom-call(s32[6]{0:T(128)S(1)} %stack.31.where, bf16[1536,192]{1,0:T(8,128)(2,1)S(1)} %get-tuple-element.77.high, ...), custom_call_target="tpu_custom_call" | custom-call | flops 1 | bytes 1 | tf_op jit(solution)/shard_map/far_kernel/pallas_call | solution.py:312
  73.5 3.7 %far_rest_kernel.1 = (f32[4,160,640]{2,1,0:T(8,128)S(1)}, bf16[4,160,640]{2,1,0:T(8,128)(2,1)S(1)}) custom-call(s32[6]{0:T(128)S(1)} %stack.31.where, bf16[640,1536]{1,0:T(8,128)(2,1)S(1)} %get-tuple-element.83.own, bf16[768,640]{1,0:T(8,128)(2,1)S(1)} %get-tuple-element.105.near, f32[320,640]{1,0:T(8,128)S(1)} %get-tuple-element.106.done, ...), custom_call_target="tpu_custom_call" | custom-call | flops 1 | bytes 1 | tf_op jit(solution)/shard_map/far_rest_kernel/pallas_call | solution.py:312
  78.2 2.6 %collective-permute-start.19 = (bf16[320,640]{1,0:T(8,128)(2,1)S(1)}, bf16[320,640]{1,0:T(8,128)(2,1)S(1)}, u32[]{:S(2)}, u32[]{:S(2)}) collective-permute-start(bf16[320,640]{1,0:T(8,128)(2,1)S(1)} %get-tuple-element.132), channel_id=1, source_target_pairs={{1,17},{16,0},{3,19},{18,2},{5,21},{20,4},{7,23},{22,6},{9,25},{24... | collective-permute-start | bytes 1228808 | tf_op jit(solution)/shard_map/ppermute | solution.py:391
  81.7 5.0 %collective-permute-start.13 = (bf16[176,640]{1,0:T(8,128)(2,1)S(1)}, bf16[176,640]{1,0:T(8,128)(2,1)S(1)}, u32[]{:S(2)}, u32[]{:S(2)}) collective-permute-start(bf16[176,640]{1,0:T(8,128)(2,1)S(1)} %get-tuple-element.124), channel_id=1, source_target_pairs={{0,64},{32,96},{64,0},{96,32},{1,65},{33,97},{65,1},{97,33},{2,66}... | collective-permute-start | bytes 675848 | tf_op jit(solution)/shard_map/ppermute | solution.py:416
  87.4 2.1 %collective-permute-start.16 = (bf16[160,640]{1,0:T(8,128)(2,1)S(1)}, bf16[160,640]{1,0:T(8,128)(2,1)S(1)}, u32[]{:S(2)}, u32[]{:S(2)}) collective-permute-start(bf16[160,640]{1,0:T(8,128)(2,1)S(1)} %get-tuple-element.129), channel_id=1, source_target_pairs={{0,32},{32,64},{64,96},{96,0},{1,33},{33,65},{65,97},{97,1},{2,34}... | collective-permute-start | bytes 614408 | tf_op jit(solution)/shard_map/ppermute | solution.py:416
  89.7 2.1 %collective-permute-start.17 = (bf16[160,640]{1,0:T(8,128)(2,1)S(1)}, bf16[160,640]{1,0:T(8,128)(2,1)S(1)}, u32[]{:S(2)}, u32[]{:S(2)}) collective-permute-start(bf16[160,640]{1,0:T(8,128)(2,1)S(1)} %get-tuple-element.130), channel_id=1, source_target_pairs={{0,64},{32,96},{64,0},{96,32},{1,65},{33,97},{65,1},{97,33},{2,66}... | collective-permute-start | bytes 614408 | tf_op jit(solution)/shard_map/ppermute | solution.py:416
  91.8 1.9 %collective-permute-start.18 = (bf16[160,640]{1,0:T(8,128)(2,1)S(1)}, bf16[160,640]{1,0:T(8,128)(2,1)S(1)}, u32[]{:S(2)}, u32[]{:S(2)}) collective-permute-start(bf16[160,640]{1,0:T(8,128)(2,1)S(1)} %get-tuple-element.131), channel_id=1, source_target_pairs={{0,96},{32,0},{64,32},{96,64},{1,97},{33,1},{65,33},{97,65},{2,98}... | collective-permute-start | bytes 614408 | tf_op jit(solution)/shard_map/ppermute | solution.py:416
  93.7 4.3 %collective-permute-done.13.refs_2_ = bf16[176,640]{1,0:T(8,128)(2,1)S(1)} collective-permute-done((bf16[176,640]{1,0:T(8,128)(2,1)S(1)}, bf16[176,640]{1,0:T(8,128)(2,1)S(1)}, u32[]{:S(2)}, u32[]{:S(2)}) %collective-permute-start.13) | collective-permute-done | bytes 225312 | tf_op jit(solution)/shard_map/ppermute | solution.py:416
  98.0 1.9 %collective-permute-done.16.refs_5_ = bf16[160,640]{1,0:T(8,128)(2,1)S(1)} collective-permute-done((bf16[160,640]{1,0:T(8,128)(2,1)S(1)}, bf16[160,640]{1,0:T(8,128)(2,1)S(1)}, u32[]{:S(2)}, u32[]{:S(2)}) %collective-permute-start.16) | collective-permute-done | bytes 204832 | tf_op jit(solution)/shard_map/ppermute | solution.py:416
  99.9 5.6 %collective-permute-done.17.refs_6_ = bf16[160,640]{1,0:T(8,128)(2,1)S(1)} collective-permute-done((bf16[160,640]{1,0:T(8,128)(2,1)S(1)}, bf16[160,640]{1,0:T(8,128)(2,1)S(1)}, u32[]{:S(2)}, u32[]{:S(2)}) %collective-permute-start.17) | collective-permute-done | bytes 204832 | tf_op jit(solution)/shard_map/ppermute | solution.py:416
  106.5 10.6 %collective-permute-done.20.got = bf16[336,640]{1,0:T(8,128)(2,1)S(1)} collective-permute-done((bf16[336,640]{1,0:T(8,128)(2,1)S(1)}, bf16[336,640]{1,0:T(8,128)(2,1)S(1)}, u32[]{:S(2)}, u32[]{:S(2)}) %collective-permute-start.20) | collective-permute-done | bytes 430112 | tf_op jit(solution)/shard_map/ppermute | solution.py:421
  117.1 1.5 %place_kernel.1 = (f32[320,640]{1,0:T(8,128)S(1)}, bf16[320,640]{1,0:T(8,128)(2,1)S(1)}, bf16[320,320]{1,0:T(8,128)(2,1)}, bf16[320,320]{1,0:T(8,128)(2,1)S(1)}, f32[1,640]{1,0:T(1,128)S(1)}) custom-call(s32[6]{0:T(128)S(1)} %stack.31.where, f32[320,640]{1,0:T(8,128)S(1)} %get-tuple-element.104.near, bf16[320,640]{1,0:T(8,128)(2,1)S(1)} %collective-permute-done.19.near_got, ...), custom_call_target="tpu_custom_call" | custom-call | flops 1 | bytes 1 | tf_op jit(solution)/shard_map/place_kernel/pallas_call | solution.py:312
  118.7 5.0 %collective-permute-start.22 = (bf16[320,640]{1,0:T(8,128)(2,1)S(1)}, bf16[320,640]{1,0:T(8,128)(2,1)S(1)}, u32[]{:S(2)}, u32[]{:S(2)}) collective-permute-start(bf16[320,640]{1,0:T(8,128)(2,1)S(1)} %get-tuple-element.148), channel_id=1, source_target_pairs={{2,32},{6,96},{32,2},{36,66},{66,36},{70,100},{96,6},{100,70},{3,3... | collective-permute-start | bytes 1228808 | tf_op jit(solution)/shard_map/ppermute | solution.py:428
  124.9 3.5 %collective-permute-start.24 = (bf16[320,640]{1,0:T(8,128)(2,1)S(1)}, bf16[320,640]{1,0:T(8,128)(2,1)S(1)}, u32[]{:S(2)}, u32[]{:S(2)}) collective-permute-start(bf16[320,640]{1,0:T(8,128)(2,1)S(1)} %get-tuple-element.150), channel_id=1, source_target_pairs={{1,16},{16,1},{3,18},{18,3},{5,20},{20,5},{7,22},{22,7},{9,24},{24... | collective-permute-start | bytes 1228808 | tf_op jit(solution)/shard_map/ppermute | solution.py:433
  129.8 11.3 %collective-permute-done.22.mirror = bf16[320,640]{1,0:T(8,128)(2,1)S(1)} collective-permute-done((bf16[320,640]{1,0:T(8,128)(2,1)S(1)}, bf16[320,640]{1,0:T(8,128)(2,1)S(1)}, u32[]{:S(2)}, u32[]{:S(2)}) %collective-permute-start.22) | collective-permute-done | bytes 409632 | tf_op jit(solution)/shard_map/ppermute | solution.py:428
  141.0 1.9 %finish_kernel.1 = f32[320,640]{1,0:T(8,128)} custom-call(s32[6]{0:T(128)S(1)} %stack.31.where, f32[320,640]{1,0:T(8,128)S(1)} %get-tuple-element.145.placed, f32[320,640]{1,0:T(8,128)S(1)} %get-tuple-element.147.turned, bf16[320,640]{1,0:T(8,128)(2,1)S(1)} %collective-permute-done.22.mirror, bf16[320,320]{1,0:T(8,128)(2,1)S(1)} %collective-permute-done.23.mirror_quad, ...), custom_call_target="tpu_custom_call" | custom-call | flops 1 | bytes 1 | tf_op jit(solution)/shard_map/finish_kernel/pallas_call | solution.py:312
  (53 shorter events, 15.1 us)
Async XLA Ops:
  0.6 14.7 %copy-start = (bf16[1536,640]{1,0:T(8,128)(2,1)S(1)}, bf16[1536,640]{1,0:T(8,128)(2,1)}, u32[]{:S(2)}) copy-start(bf16[1536,640]{1,0:T(8,128)(2,1)} %rows.1) | copy-start | bytes 5898244
  0.6 7.5 %copy-start.5 = (f32[1536]{0:T(1024)S(1)}, f32[1536]{0:T(1024)}, u32[]{:S(2)}) copy-start(f32[1536]{0:T(1024)} %param.7) | copy-start | bytes 18436
  0.7 7.5 %copy-start.6 = (s32[1536]{0:T(1024)S(1)}, s32[1536]{0:T(1024)}, u32[]{:S(2)}) copy-start(s32[1536]{0:T(1024)} %param.8) | copy-start | bytes 18436
  0.7 7.6 %copy-start.4 = (f32[16,1536]{1,0:T(8,128)S(1)}, f32[16,1536]{1,0:T(8,128)}, u32[]{:S(2)}) copy-start(f32[16,1536]{1,0:T(8,128)} %param.6) | copy-start | bytes 294916
  3.8 23.8 %collective-permute-start.1 = (bf16[768,640]{1,0:T(8,128)(2,1)}, bf16[768,640]{1,0:T(8,128)(2,1)}, u32[]{:S(2)}, u32[]{:S(2)}) collective-permute-start(bf16[768,640]{1,0:T(8,128)(2,1)} %get-tuple-element.91), channel_id=1, source_target_pairs={{0,2},{2,4},{4,6},{6,0},{1,3},{3,5},{5,7},{7,1},{8,10},{10,12},{12... | collective-permute-start | bytes 2949128 | tf_op jit(solution)/shard_map/ppermute | solution.py:341
  4.3 25.0 %collective-permute-start.2 = (bf16[768,640]{1,0:T(8,128)(2,1)}, bf16[768,640]{1,0:T(8,128)(2,1)}, u32[]{:S(2)}, u32[]{:S(2)}) collective-permute-start(bf16[768,640]{1,0:T(8,128)(2,1)} %get-tuple-element.153), channel_id=1, source_target_pairs={{0,1},{1,0},{2,3},{3,2},{4,5},{5,4},{6,7},{7,6},{8,9},{9,8},{10,11... | collective-permute-start | bytes 2949128 | tf_op jit(solution)/shard_map/ppermute | solution.py:342
  6.6 24.5 %collective-permute-start = (bf16[768,640]{1,0:T(8,128)(2,1)}, bf16[768,640]{1,0:T(8,128)(2,1)}, u32[]{:S(2)}, u32[]{:S(2)}) collective-permute-start(bf16[768,640]{1,0:T(8,128)(2,1)} %get-tuple-element.153), channel_id=1, source_target_pairs={{0,6},{2,0},{4,2},{6,4},{1,7},{3,1},{5,3},{7,5},{8,14},{10,8},{12,... | collective-permute-start | bytes 2949128 | tf_op jit(solution)/shard_map/ppermute | solution.py:340
  8.4 0.7 copy-start.3
  14.7 0.6 copy-start.1
  15.4 0.7 copy-start.2
  19.9 1.9 %collective-permute-start.3 = (bf16[336,640]{1,0:T(8,128)(2,1)S(1)}, bf16[336,640]{1,0:T(8,128)(2,1)S(1)}, u32[]{:S(2)}, u32[]{:S(2)}) collective-permute-start(bf16[336,640]{1,0:T(8,128)(2,1)S(1)} %get-tuple-element.82), channel_id=1, source_target_pairs={{0,8},{8,0},{1,9},{9,1},{2,10},{10,2},{3,11},{11,3},{4,12},{12,4},... | collective-permute-start | bytes 1290248 | tf_op jit(solution)/shard_map/ppermute | solution.py:356
  31.0 23.7 %collective-permute-start.5 = (bf16[768,640]{1,0:T(8,128)(2,1)}, bf16[768,640]{1,0:T(8,128)(2,1)S(1)}, u32[]{:S(2)}, u32[]{:S(2)}) collective-permute-start(bf16[768,640]{1,0:T(8,128)(2,1)} %get-tuple-element.91), channel_id=1, source_target_pairs={{0,1},{1,0},{2,3},{3,2},{4,5},{5,4},{6,7},{7,6},{8,9},{9,8},{10,11... | collective-permute-start | bytes 2949128 | tf_op jit(solution)/shard_map/ppermute | solution.py:361
  36.7 3.4 %collective-permute-start.4 = (bf16[2,320,640]{2,1,0:T(8,128)(2,1)S(1)}, bf16[2,320,640]{2,1,0:T(8,128)(2,1)S(1)}, u32[]{:S(2)}, u32[]{:S(2)}) collective-permute-start(bf16[2,320,640]{2,1,0:T(8,128)(2,1)S(1)} %get-tuple-element.89), channel_id=1, source_target_pairs={{0,8},{8,0},{1,9},{9,1},{2,10},{10,2},{3,11},{11,3},{4,12},{12,4},... | collective-permute-start | bytes 2457608 | tf_op jit(solution)/shard_map/ppermute | solution.py:372
  36.8 26.9 %collective-permute-start.6 = (bf16[768,640]{1,0:T(8,128)(2,1)}, bf16[768,640]{1,0:T(8,128)(2,1)S(1)}, u32[]{:S(2)}, u32[]{:S(2)}) collective-permute-start(bf16[768,640]{1,0:T(8,128)(2,1)} %collective-permute-done.above), channel_id=1, source_target_pairs={{0,6},{2,0},{4,2},{6,4},{1,7},{3,1},{5,3},{7,5},{8,14},{10,8},{12,... | collective-permute-start | bytes 2949128 | tf_op jit(solution)/shard_map/ppermute | solution.py:362
  37.7 25.9 %collective-permute-start.7 = (bf16[768,640]{1,0:T(8,128)(2,1)}, bf16[768,640]{1,0:T(8,128)(2,1)S(1)}, u32[]{:S(2)}, u32[]{:S(2)}) collective-permute-start(bf16[768,640]{1,0:T(8,128)(2,1)} %collective-permute-done.1.below), channel_id=1, source_target_pairs={{0,2},{2,4},{4,6},{6,0},{1,3},{3,5},{5,7},{7,1},{8,10},{10,12},{12... | collective-permute-start | bytes 2949128 | tf_op jit(solution)/shard_map/ppermute | solution.py:363
  41.2 22.5 %collective-permute-start.8 = (bf16[320,640]{1,0:T(8,128)(2,1)S(1)}, bf16[320,640]{1,0:T(8,128)(2,1)S(1)}, u32[]{:S(2)}, u32[]{:S(2)}) collective-permute-start(bf16[320,640]{1,0:T(8,128)(2,1)S(1)} %get-tuple-element.98), channel_id=1, source_target_pairs={{0,32},{2,34},{4,36},{34,66},{36,68},{38,70},{64,96},{68,100},{70,... | collective-permute-start | bytes 1228808 | tf_op jit(solution)/shard_map/ppermute | solution.py:381
  42.5 24.1 %collective-permute-start.9 = (bf16[320,640]{1,0:T(8,128)(2,1)S(1)}, bf16[320,640]{1,0:T(8,128)(2,1)S(1)}, u32[]{:S(2)}, u32[]{:S(2)}) collective-permute-start(bf16[320,640]{1,0:T(8,128)(2,1)S(1)} %get-tuple-element.99), channel_id=1, source_target_pairs={{2,66},{4,68},{6,70},{32,96},{36,100},{38,102},{64,0},{66,2},{70,6... | collective-permute-start | bytes 1228808 | tf_op jit(solution)/shard_map/ppermute | solution.py:381
  54.7 13.1 %collective-permute-start.10 = (bf16[320,640]{1,0:T(8,128)(2,1)S(1)}, bf16[320,640]{1,0:T(8,128)(2,1)S(1)}, u32[]{:S(2)}, u32[]{:S(2)}) collective-permute-start(bf16[320,640]{1,0:T(8,128)(2,1)S(1)} %get-tuple-element.100), channel_id=1, source_target_pairs={{0,96},{4,100},{6,102},{32,0},{34,2},{38,6},{64,32},{66,34},{68,36... | collective-permute-start | bytes 1228808 | tf_op jit(solution)/shard_map/ppermute | solution.py:381
  73.4 3.8 %collective-permute-start.11 = (bf16[4,160,640]{2,1,0:T(8,128)(2,1)S(1)}, bf16[4,160,640]{2,1,0:T(8,128)(2,1)S(1)}, u32[]{:S(2)}, u32[]{:S(2)}) collective-permute-start(bf16[4,160,640]{2,1,0:T(8,128)(2,1)S(1)} %get-tuple-element.119), channel_id=1, source_target_pairs={{0,8},{8,0},{1,9},{9,1},{2,10},{10,2},{3,11},{11,3},{4,12},{12,4},... | collective-permute-start | bytes 2457608 | tf_op jit(solution)/shard_map/ppermute | solution.py:402
  77.3 9.5 %collective-permute-start.15 = (bf16[4,160,640]{2,1,0:T(8,128)(2,1)S(1)}, bf16[4,160,640]{2,1,0:T(8,128)(2,1)S(1)}, u32[]{:S(2)}, u32[]{:S(2)}) collective-permute-start(bf16[4,160,640]{2,1,0:T(8,128)(2,1)S(1)} %get-tuple-element.127), channel_id=1, source_target_pairs={{0,8},{8,0},{1,9},{9,1},{2,10},{10,2},{3,11},{11,3},{4,12},{12,4},... | collective-permute-start | bytes 2457608 | tf_op jit(solution)/shard_map/ppermute | solution.py:410
  78.2 11.5 %collective-permute-start.19 = (bf16[320,640]{1,0:T(8,128)(2,1)S(1)}, bf16[320,640]{1,0:T(8,128)(2,1)S(1)}, u32[]{:S(2)}, u32[]{:S(2)}) collective-permute-start(bf16[320,640]{1,0:T(8,128)(2,1)S(1)} %get-tuple-element.132), channel_id=1, source_target_pairs={{1,17},{16,0},{3,19},{18,2},{5,21},{20,4},{7,23},{22,6},{9,25},{24... | collective-permute-start | bytes 1228808 | tf_op jit(solution)/shard_map/ppermute | solution.py:391
  81.6 10.2 %collective-permute-start.12 = (bf16[176,640]{1,0:T(8,128)(2,1)S(1)}, bf16[176,640]{1,0:T(8,128)(2,1)S(1)}, u32[]{:S(2)}, u32[]{:S(2)}) collective-permute-start(bf16[176,640]{1,0:T(8,128)(2,1)S(1)} %get-tuple-element.123), channel_id=1, source_target_pairs={{0,32},{32,64},{64,96},{96,0},{1,33},{33,65},{65,97},{97,1},{2,34}... | collective-permute-start | bytes 675848 | tf_op jit(solution)/shard_map/ppermute | solution.py:416
  81.7 16.3 %collective-permute-start.13 = (bf16[176,640]{1,0:T(8,128)(2,1)S(1)}, bf16[176,640]{1,0:T(8,128)(2,1)S(1)}, u32[]{:S(2)}, u32[]{:S(2)}) collective-permute-start(bf16[176,640]{1,0:T(8,128)(2,1)S(1)} %get-tuple-element.124), channel_id=1, source_target_pairs={{0,64},{32,96},{64,0},{96,32},{1,65},{33,97},{65,1},{97,33},{2,66}... | collective-permute-start | bytes 675848 | tf_op jit(solution)/shard_map/ppermute | solution.py:416
  86.7 11.3 %collective-permute-start.14 = (bf16[176,640]{1,0:T(8,128)(2,1)S(1)}, bf16[176,640]{1,0:T(8,128)(2,1)S(1)}, u32[]{:S(2)}, u32[]{:S(2)}) collective-permute-start(bf16[176,640]{1,0:T(8,128)(2,1)S(1)} %get-tuple-element.125), channel_id=1, source_target_pairs={{0,96},{32,0},{64,32},{96,64},{1,97},{33,1},{65,33},{97,65},{2,98}... | collective-permute-start | bytes 675848 | tf_op jit(solution)/shard_map/ppermute | solution.py:416
  87.4 12.5 %collective-permute-start.16 = (bf16[160,640]{1,0:T(8,128)(2,1)S(1)}, bf16[160,640]{1,0:T(8,128)(2,1)S(1)}, u32[]{:S(2)}, u32[]{:S(2)}) collective-permute-start(bf16[160,640]{1,0:T(8,128)(2,1)S(1)} %get-tuple-element.129), channel_id=1, source_target_pairs={{0,32},{32,64},{64,96},{96,0},{1,33},{33,65},{65,97},{97,1},{2,34}... | collective-permute-start | bytes 614408 | tf_op jit(solution)/shard_map/ppermute | solution.py:416
  89.7 15.8 %collective-permute-start.17 = (bf16[160,640]{1,0:T(8,128)(2,1)S(1)}, bf16[160,640]{1,0:T(8,128)(2,1)S(1)}, u32[]{:S(2)}, u32[]{:S(2)}) collective-permute-start(bf16[160,640]{1,0:T(8,128)(2,1)S(1)} %get-tuple-element.130), channel_id=1, source_target_pairs={{0,64},{32,96},{64,0},{96,32},{1,65},{33,97},{65,1},{97,33},{2,66}... | collective-permute-start | bytes 614408 | tf_op jit(solution)/shard_map/ppermute | solution.py:416
  91.8 13.7 %collective-permute-start.18 = (bf16[160,640]{1,0:T(8,128)(2,1)S(1)}, bf16[160,640]{1,0:T(8,128)(2,1)S(1)}, u32[]{:S(2)}, u32[]{:S(2)}) collective-permute-start(bf16[160,640]{1,0:T(8,128)(2,1)S(1)} %get-tuple-element.131), channel_id=1, source_target_pairs={{0,96},{32,0},{64,32},{96,64},{1,97},{33,1},{65,33},{97,65},{2,98}... | collective-permute-start | bytes 614408 | tf_op jit(solution)/shard_map/ppermute | solution.py:416
  106.4 10.7 %collective-permute-start.20 = (bf16[336,640]{1,0:T(8,128)(2,1)S(1)}, bf16[336,640]{1,0:T(8,128)(2,1)S(1)}, u32[]{:S(2)}, u32[]{:S(2)}) collective-permute-start(bf16[336,640]{1,0:T(8,128)(2,1)S(1)} %get-tuple-element.143), channel_id=1, source_target_pairs={{0,16},{16,0},{1,17},{17,1},{2,18},{18,2},{3,19},{19,3},{4,20},{20... | collective-permute-start | bytes 1290248 | tf_op jit(solution)/shard_map/ppermute | solution.py:421
  118.7 5.0 %collective-permute-start.21 = (bf16[320,320]{1,0:T(8,128)(2,1)S(1)}, bf16[320,320]{1,0:T(8,128)(2,1)S(1)}, u32[]{:S(2)}, u32[]{:S(2)}) collective-permute-start(bf16[320,320]{1,0:T(8,128)(2,1)S(1)} %get-tuple-element.146), channel_id=1, source_target_pairs={{0,8},{8,0},{1,9},{9,1},{2,10},{10,2},{3,11},{11,3},{4,12},{12,4},... | collective-permute-start | bytes 614408 | tf_op jit(solution)/shard_map/ppermute | solution.py:431
  118.7 22.3 %collective-permute-start.22 = (bf16[320,640]{1,0:T(8,128)(2,1)S(1)}, bf16[320,640]{1,0:T(8,128)(2,1)S(1)}, u32[]{:S(2)}, u32[]{:S(2)}) collective-permute-start(bf16[320,640]{1,0:T(8,128)(2,1)S(1)} %get-tuple-element.148), channel_id=1, source_target_pairs={{2,32},{6,96},{32,2},{36,66},{66,36},{70,100},{96,6},{100,70},{3,3... | collective-permute-start | bytes 1228808 | tf_op jit(solution)/shard_map/ppermute | solution.py:428
  124.9 16.1 %collective-permute-start.24 = (bf16[320,640]{1,0:T(8,128)(2,1)S(1)}, bf16[320,640]{1,0:T(8,128)(2,1)S(1)}, u32[]{:S(2)}, u32[]{:S(2)}) collective-permute-start(bf16[320,640]{1,0:T(8,128)(2,1)S(1)} %get-tuple-element.150), channel_id=1, source_target_pairs={{1,16},{16,1},{3,18},{18,3},{5,20},{20,5},{7,22},{22,7},{9,24},{24... | collective-permute-start | bytes 1228808 | tf_op jit(solution)/shard_map/ppermute | solution.py:433
  128.5 1.3 collective-permute-start.23

commit v3 on v2

--- a/solution.py
+++ b/solution.py
@@ -16,6 +16,7 @@
 VMEM = pl.BlockSpec(memory_space=pltpu.VMEM)
 SMEM = pl.BlockSpec(memory_space=pltpu.SMEM)
 PARAMS = pltpu.CompilerParams(vmem_limit_bytes=16 << 20)
+LONG = pl.CostEstimate(flops=20_000_000_000, transcendentals=0, bytes_accessed=1)
 CHEAP = pl.CostEstimate(flops=1, transcendentals=0, bytes_accessed=1)
 
 
@@ -244,42 +245,47 @@
     send[...] = total[...].astype(BF16)
 
 
-def far_total_kernel(where, rhs, *refs):
-    keep, send, rhs_sum = refs[-3:]
-    half = keep.shape[0]
+def far_total_kernel(with_rhs, where, rhs, mine, one, two, three, keep, send, *rhs_sum):
+    size, half = keep.shape[0], keep.shape[1] // 2
     opposite, same = where[1] == 2, where[4] == 1
-    first = 0
-    for chunk in range(len(refs) // 4):
-        mine, one, two, three = refs[4 * chunk : 4 * chunk + 4]
-        size = mine.shape[0]
-        one, two, three = (up[:size, :].astype(F32) for up in (one, two, three))
-        total = ((mine[...] + one) + two) + three
-        rows = slice(first, first + size)
-        first += size
-        turned = jnp.concatenate([total[:, half:], total[:, :half]], 1)
-        send[rows, :] = jnp.where(jnp.logical_and(opposite, same), turned, total).astype(BF16)
-        keep[rows, :] = jnp.where(jnp.logical_and(opposite, jnp.logical_not(same)), turned, total)
-    one, two, three = (whole_of(up[refs[0].shape[0] :, :]) for up in refs[1:4])
-    total = (rhs[...] + two) + (one + three)
-    rhs_sum[...] = total
-    send[half:, :] = parts_of(total)
-
-
-def place_kernel(where, near, near_got, keep, got, rhs, placed, mirror, mirror_quad, quad_send, rhs_sum):
-    half = placed.shape[0]
-    core, delta, same, right = where[0], where[1], where[4] == 1, where[5] == 1
-    late = keep[...] + got[:half, :].astype(F32)
-    early = near[...] + near_got[...].astype(F32)
+    first, second, third = (up[:size, :].astype(F32) for up in (one, two, three))
+    total = ((mine[...] + first) + second) + third
+    turned = jnp.concatenate([total[:, half:], total[:, :half]], 1)
+    send[:size, :] = jnp.where(jnp.logical_and(opposite, same), turned, total).astype(BF16)
+    keep[...] = jnp.where(jnp.logical_and(opposite, jnp.logical_not(same)), turned, total)
+    if with_rhs:
+        first, second, third = (whole_of(up[size:, :]) for up in (one, two, three))
+        total = (rhs[...] + second) + (first + third)
+        rhs_sum[0][...] = total
+        send[size:, :] = parts_of(total)
+
+
+def place(where, near, near_got, keep, got, rows, placed, mirror, quads):
+    size, half = keep.shape[0], keep.shape[1] // 2
+    delta, same, right = where[1], where[4] == 1, where[5] == 1
+    late = keep[...] + got[:size, :].astype(F32)
+    early = near[rows, :] + near_got[rows, :].astype(F32)
     total = jnp.where(jnp.logical_and(same, delta != 2), early, late)
     quad = jnp.logical_or(delta == 2, jnp.logical_and(delta == 0, jnp.logical_not(same)))
-    left_side = jnp.where(jnp.logical_and(quad, right), 0.0, total[:, :half])
-    right_side = jnp.where(quad, jnp.where(right, total[:, :half], 0.0), total[:, half:])
-    placed[:, :half] = left_side
-    placed[:, half:] = right_side
-    mirror[...] = placed[...].astype(BF16)
-    mirror_quad[...] = total[:, :half].astype(BF16)
-    quad_send[...] = jnp.where(core == 0, right_side, left_side).astype(BF16)
-    rhs_sum[...] = rhs[...] + whole_of(got[half:, :])
+    placed[rows, :half] = jnp.where(jnp.logical_and(quad, right), 0.0, total[:, :half])
+    placed[rows, half:] = jnp.where(quad, jnp.where(right, total[:, :half], 0.0), total[:, half:])
+    mirror[...] = placed[rows, :].astype(BF16)
+    quads[rows, :] = total[:, :half].astype(BF16)
+
+
+def place_first_kernel(where, near, near_got, keep, got, rhs, placed, mirror, quads, rhs_sum):
+    size = keep.shape[0]
+    place(where, near, near_got, keep, got, slice(0, size), placed, mirror, quads)
+    rhs_sum[...] = rhs[...] + whole_of(got[size:, :])
+
+
+def place_last_kernel(where, near, near_got, keep, got, placed_first, quads_first, placed, mirror, quads, core_send):
+    size, half = keep.shape[0], placed.shape[0]
+    first = slice(0, half - size)
+    placed[first, :] = placed_first[first, :]
+    quads[first, :] = quads_first[first, :]
+    place(where, near, near_got, keep, got, slice(half - size, half), placed, mirror, quads)
+    core_send[...] = jnp.where(where[0] == 0, placed[:, half:], placed[:, :half]).astype(BF16)
 
 
 def turn_kernel(where, placed, got, turned, across):
@@ -294,29 +300,34 @@
     across[...] = jnp.where(diagonal, placed[...], turned[...]).astype(BF16)
 
 
-def finish_kernel(where, placed, turned, mirror, mirror_quad, across, out):
-    half = out.shape[0]
+def base_kernel(where, placed, turned, mirror_first, mirror_last, mirror_quad, base):
+    half = base.shape[0]
+    size = mirror_first.shape[0]
     diagonal, opposite, same = where[1] == 0, where[1] == 2, where[4] == 1
     left = where[5] == 1
     for side, columns in enumerate((slice(0, half), slice(half, 2 * half))):
-        far = across[:, columns].astype(F32)
-        quad = jnp.where(left == (side == 0), mirror_quad[...].astype(F32), 0.0)
-        near = jnp.where(opposite, quad, mirror[:, columns].astype(F32))
-        own = turned[:, columns]
-        direct = jnp.where(diagonal, jnp.where(same, placed[:, columns], far), near)
-        other = jnp.where(diagonal, jnp.where(same, 0.0, own), jnp.where(same, own, far))
-        out[:, columns] = direct + other
-
-
-def call(kernel, outs, *args, scalars=True, scratch=(), vmem=12):
+        for mirror, rows in ((mirror_first, slice(0, size)), (mirror_last, slice(size, half))):
+            quad = jnp.where(left == (side == 0), mirror_quad[rows, :].astype(F32), 0.0)
+            near = jnp.where(opposite, quad, mirror[:, columns].astype(F32))
+            own = jnp.where(diagonal == same, 0.0, turned[rows, columns])
+            direct = jnp.where(diagonal, jnp.where(same, placed[rows, columns], 0.0), near)
+            base[rows, columns] = direct + own
+
+
+def finish_kernel(where, base, across, out):
+    same = where[4] == 1
+    out[...] = base[...] + jnp.where(same, 0.0, across[...].astype(F32))
+
+
+def call(kernel, outs, *args, scalars=True, scratch=(), vmem=12, statics=(), cost=CHEAP):
     return pl.pallas_call(
-        kernel,
+        functools.partial(kernel, *statics),
         out_shape=outs,
         in_specs=[SMEM if scalars and i == 0 else VMEM for i in range(len(args))],
         out_specs=jax.tree.map(lambda _: VMEM, outs),
         scratch_shapes=scratch,
         compiler_params=pltpu.CompilerParams(vmem_limit_bytes=vmem << 20),
-        cost_estimate=CHEAP,
+        cost_estimate=cost,
         name=kernel.__name__,
     )(*args)
 
@@ -409,29 +420,41 @@
     keeps.append(keep)
     gots.append(lax.ppermute(send, "core", swap))
 
-    late = []
+    part = shape((size, width), F32)
+    sums = []
     for chunk, (keep, got) in enumerate(zip(keeps, gots)):
         up = shape((size + (low_rows if chunk == 0 else 0), width), BF16)
-        mine, *ups = call(far_spread_kernel, (shape((size, width), F32), up, up, up), where, keep, got, rhs)
-        late += [mine] + [lax.ppermute(v, "z", turn(k)) for k, v in enumerate(ups, 1)]
-    late, early_got = lax.optimization_barrier((late, early_got))
-    keep, send, rhs = call(
-        far_total_kernel, (wide, shape((half + low_rows, width), BF16), row), where, rhs, *late
-    )
-    got = lax.ppermute(send, "yl", swap)
-
-    quad = shape((half, half), BF16)
-    placed, mirror, mirror_quad, send, rhs = call(
-        place_kernel, (wide, sent, quad, quad, row), where, early, early_got, keep, got, rhs
-    )
-    pairs = [(a * nx + b, b * nx + a) for a in range(nz) for b in range(nx) if (a - b) % 2]
-    mirror = lax.ppermute(mirror, ("z", "x"), pairs)
-    pairs = [(a * nx + b, b * nx + a) for a in range(nz) for b in range(nx) if (a - b) % nx == 2]
-    mirror_quad = lax.ppermute(mirror_quad, ("z", "x"), pairs)
+        mine, *ups = call(far_spread_kernel, (part, up, up, up), where, keep, got, rhs)
+        sums.append((mine, [lax.ppermute(v, "z", turn(k)) for k, v in enumerate(ups, 1)]))
+    halves = []
+    for chunk, (mine, ups) in enumerate(sums):
+        extra = (row,) if chunk == 0 else ()
+        up = shape((size + (low_rows if chunk == 0 else 0), width), BF16)
+        keep, send, *rest = call(
+            far_total_kernel, (part, up) + extra, where, rhs, mine, *ups, statics=(chunk == 0,)
+        )
+        if rest:
+            (rhs_sum,) = rest
+        halves.append((keep, lax.ppermute(send, "yl", swap)))
+
+    beside = [(a * nx + b, b * nx + a) for a in range(nz) for b in range(nx) if (a - b) % 2]
+    opposite = [(a * nx + b, b * nx + a) for a in range(nz) for b in range(nx) if (a - b) % nx == 2]
+    quad, mirror = shape((half, half), BF16), shape((size, width), BF16)
+    placed, mirror_first, quads, rhs = call(
+        place_first_kernel, (wide, mirror, quad, row), where, early, early_got, *halves[0], rhs_sum
+    )
+    mirror_first = lax.ppermute(mirror_first, ("z", "x"), beside)
+    placed, mirror_last, quads, send = call(
+        place_last_kernel, (wide, mirror, quad, quad), where, early, early_got, *halves[1], placed, quads
+    )
+    mirror_last = lax.ppermute(mirror_last, ("z", "x"), beside)
+    mirror_quad = lax.ppermute(quads, ("z", "x"), opposite)
     got = lax.ppermute(send, "core", swap)
+    got, mirror_first = lax.optimization_barrier((got, mirror_first))
     turned, across = call(turn_kernel, (wide, sent), where, placed, got)
     across = lax.ppermute(across, ("yl", "yh"), [(1, 2), (2, 1)])
-    out = call(finish_kernel, wide, where, placed, turned, mirror, mirror_quad, across)
+    base = call(base_kernel, wide, where, placed, turned, mirror_first, mirror_last, mirror_quad, cost=LONG)
+    out = call(finish_kernel, wide, where, base, across)
     return out, rhs[0]
 
 

time: 143 us -> 133 us (0.930)
  waiting for transfers between devices: 53.4 us -> 40.2 us
  starting transfers between devices: 48.2 us -> 50.1 us
    ppermute x3 -> x5, waiting for transfers between devices: 21.9 us -> 7.81 us  [the longest x1 7.34 us: body(): mirror_last = lax.ppermute(mirror_last, ('z', 'x'), beside)]
    ppermute x3 -> x5, starting transfers between devices: 5.75 us -> 11.8 us  [the longest x1 4.84 us: body(): mirror_last = lax.ppermute(mirror_last, ('z', 'x'), beside)]
    ppermute x6, starting transfers between devices: 11.2 us -> 6.91 us  [body(): lax.ppermute(v, 'z', turn(k))]
    ppermute x1, waiting for transfers between devices: 0.01 us -> 2 us  [body(): across = lax.ppermute(across, ('yl', 'yh'), [(1, 2), (2, 1)])]
    pallas_call x13 -> x16, Pallas kernels: 28.7 us -> 30 us  [call(): pl.pallas_call(functools.partial(kernel, *statics), out_shape=outs, in_sp...]
  transfers between devices with their start and end apart: 25 -> 27, of which waited for: 13 -> 13; matrix products, arithmetic and copies ran while one was open for 1% -> 1% of each run, Pallas kernels for 17% -> 22%
where the time goes in v3:
time: 133 us
  starting transfers between devices  50.1 us (38%)
  waiting for transfers between devices  40.2 us (30%)
  Pallas kernels  35.6 us (27%)
  local copies, waits for them, and re-layouts  5.44 us (4%)
    pallas_call x16, Pallas kernels, call(): pl.pallas_call(functools.partial(kernel, *statics), out_shape=outs, in_sp...  30 us
    ppermute x3, starting transfers between devices, body(): lax.ppermute(v, ('z', 'x'), early_turn(k))  15.4 us
    ppermute x6, waiting for transfers between devices, body(): lax.ppermute(v, 'z', turn(k))  10.9 us
    ppermute x1, waiting for transfers between devices, body(): mirror_last = lax.ppermute(mirror_last, ('z', 'x'), beside)  7.34 us
    ppermute x6, starting transfers between devices, body(): lax.ppermute(v, 'z', turn(k))  6.91 us
    ppermute x1, waiting for transfers between devices, body(): below = lax.ppermute(lower, 'x', up)  5.84 us
    pallas_call x1, Pallas kernels, eliminate(): pl.pallas_call(eliminate_kernel, out_shape=(shape((arcs * SLOTS, SLOTS),...  5.61 us
    ppermute x1, starting transfers between devices, body(): mirror_last = lax.ppermute(mirror_last, ('z', 'x'), beside)  4.84 us
  transfers between devices with their start and end apart: 27, of which 13 were waited for; matrix products, arithmetic and copies ran while one was open for 1% of the time, Pallas kernels for 22%

profile of v3, /device:TPU:14, one launch (start us, length us, event | category | flops | bytes accessed | tf_op | source)
XLA Modules:
  0.0 132.8 jit_solution(7720749417385736697)
XLA Ops:
  0.7 3.1 %fusion = (bf16[768,640]{1,0:T(8,128)(2,1)}, bf16[768,640]{1,0:T(8,128)(2,1)}) fusion(bf16[1536,640]{1,0:T(8,128)(2,1)} %rows.1), kind=kLoop, calls=%fused_computation.1 | loop fusion | bytes 3932160 | tf_op jit(solution)/shard_map/slice | solution.py:350
  4.3 2.3 %collective-permute-start.2 = (bf16[768,640]{1,0:T(8,128)(2,1)}, bf16[768,640]{1,0:T(8,128)(2,1)}, u32[]{:S(2)}, u32[]{:S(2)}) collective-permute-start(bf16[768,640]{1,0:T(8,128)(2,1)} %get-tuple-element.149), channel_id=1, source_target_pairs={{0,1},{1,0},{2,3},{3,2},{4,5},{5,4},{6,7},{7,6},{8,9},{9,8},{10,11... | collective-permute-start | bytes 2949128 | tf_op jit(solution)/shard_map/ppermute | solution.py:353
  6.6 1.5 %collective-permute-start = (bf16[768,640]{1,0:T(8,128)(2,1)}, bf16[768,640]{1,0:T(8,128)(2,1)}, u32[]{:S(2)}, u32[]{:S(2)}) collective-permute-start(bf16[768,640]{1,0:T(8,128)(2,1)} %get-tuple-element.149), channel_id=1, source_target_pairs={{0,6},{2,0},{4,2},{6,4},{1,7},{3,1},{5,3},{7,5},{8,14},{10,8},{12,... | collective-permute-start | bytes 2949128 | tf_op jit(solution)/shard_map/ppermute | solution.py:351
  9.1 5.6 %eliminate.1 = (bf16[1536,192]{1,0:T(8,128)(2,1)S(1)}, bf16[1536,192]{1,0:T(8,128)(2,1)S(1)}, f32[8,192]{1,0:T(8,128)S(1)}) custom-call(s32[8]{0:T(128)S(1)} %copy-done.3, f32[8,16,192]{2,1,0:T(8,128)S(1)} %bitcast.9, f32[8,192]{1,0:T(8,128)S(1)} %reshape.14.observed, s32[8,192]{1,0:T(8,128)S(1)} %reshape.15.valid), custom_call_target="tpu_custom_call" | custom-call | flops 1 | bytes 1 | tf_op jit(solution)/shard_map/eliminate/pallas_call | solution.py:69
  16.1 3.8 %own_kernel.1 = (bf16[1536,640]{1,0:T(8,128)(2,1)}, bf16[640,1536]{1,0:T(8,128)(2,1)S(1)}, f32[320,640]{1,0:T(8,128)S(1)}, bf16[336,640]{1,0:T(8,128)(2,1)S(1)}, f32[1,640]{1,0:T(1,128)S(1)}) custom-call(s32[6]{0:T(128)S(1)} %stack.31.where, bf16[1536,192]{1,0:T(8,128)(2,1)S(1)} %get-tuple-element.75.high, bf16[1536,192]{1,0:T(8,128)(2,1)S(1)} %get-tuple-element.76.low, ...), custom_call_target="tpu_custom_call" | custom-call | flops 1 | bytes 1 | tf_op jit(solution)/shard_map/own_kernel/pallas_call | solution.py:323
  20.0 1.8 %collective-permute-done.3.own_got = bf16[336,640]{1,0:T(8,128)(2,1)S(1)} collective-permute-done((bf16[336,640]{1,0:T(8,128)(2,1)S(1)}, bf16[336,640]{1,0:T(8,128)(2,1)S(1)}, u32[]{:S(2)}, u32[]{:S(2)}) %collective-permute-start.3) | collective-permute-done | bytes 430112 | tf_op jit(solution)/shard_map/ppermute | solution.py:367
  21.8 5.8 %collective-permute-done.1.below = bf16[768,640]{1,0:T(8,128)(2,1)} collective-permute-done((bf16[768,640]{1,0:T(8,128)(2,1)}, bf16[768,640]{1,0:T(8,128)(2,1)}, u32[]{:S(2)}, u32[]{:S(2)}) %collective-permute-start.1) | collective-permute-done | bytes 983072 | tf_op jit(solution)/shard_map/ppermute | solution.py:352
  27.6 1.7 %collective-permute-done.2.rows = bf16[768,640]{1,0:T(8,128)(2,1)} collective-permute-done((bf16[768,640]{1,0:T(8,128)(2,1)}, bf16[768,640]{1,0:T(8,128)(2,1)}, u32[]{:S(2)}, u32[]{:S(2)}) %collective-permute-start.2) | collective-permute-done | bytes 983072 | tf_op jit(solution)/shard_map/ppermute | solution.py:353
  29.3 1.7 %collective-permute-done.above = bf16[768,640]{1,0:T(8,128)(2,1)} collective-permute-done((bf16[768,640]{1,0:T(8,128)(2,1)}, bf16[768,640]{1,0:T(8,128)(2,1)}, u32[]{:S(2)}, u32[]{:S(2)}) %collective-permute-start) | collective-permute-done | bytes 983072 | tf_op jit(solution)/shard_map/ppermute | solution.py:351
  32.3 4.4 %near_kernel.1 = (bf16[768,640]{1,0:T(8,128)(2,1)S(1)}, bf16[768,640]{1,0:T(8,128)(2,1)S(1)}, f32[2,320,640]{2,1,0:T(8,128)S(1)}, bf16[2,320,640]{2,1,0:T(8,128)(2,1)S(1)}) custom-call(s32[6]{0:T(128)S(1)} %stack.31.where, bf16[1536,192]{1,0:T(8,128)(2,1)S(1)} %get-tuple-element.75.high, bf16[1536,192]{1,0:T(8,128)(2,1)S(1)} %get-tuple-element.76.low, ...), custom_call_target="tpu_custom_call" | custom-call | flops 1 | bytes 1 | tf_op jit(solution)/shard_map/near_kernel/pallas_call | solution.py:323
  37.8 2.3 %collective-permute-start.7 = (bf16[768,640]{1,0:T(8,128)(2,1)}, bf16[768,640]{1,0:T(8,128)(2,1)S(1)}, u32[]{:S(2)}, u32[]{:S(2)}) collective-permute-start(bf16[768,640]{1,0:T(8,128)(2,1)} %collective-permute-done.1.below), channel_id=1, source_target_pairs={{0,2},{2,4},{4,6},{6,0},{1,3},{3,5},{5,7},{7,1},{8,10},{10,12},{12... | collective-permute-start | bytes 2949128 | tf_op jit(solution)/shard_map/ppermute | solution.py:374
  42.5 8.0 %collective-permute-start.9 = (bf16[320,640]{1,0:T(8,128)(2,1)S(1)}, bf16[320,640]{1,0:T(8,128)(2,1)S(1)}, u32[]{:S(2)}, u32[]{:S(2)}) collective-permute-start(bf16[320,640]{1,0:T(8,128)(2,1)S(1)} %get-tuple-element.97), channel_id=1, source_target_pairs={{2,66},{4,68},{6,70},{32,96},{36,100},{38,102},{64,0},{66,2},{70,6... | collective-permute-start | bytes 1228808 | tf_op jit(solution)/shard_map/ppermute | solution.py:392
  50.5 4.2 %collective-permute-done.5.rows = bf16[768,640]{1,0:T(8,128)(2,1)S(1)} collective-permute-done((bf16[768,640]{1,0:T(8,128)(2,1)}, bf16[768,640]{1,0:T(8,128)(2,1)S(1)}, u32[]{:S(2)}, u32[]{:S(2)}) %collective-permute-start.5) | collective-permute-done | bytes 983072 | tf_op jit(solution)/shard_map/ppermute | solution.py:372
  54.8 6.1 %collective-permute-start.10 = (bf16[320,640]{1,0:T(8,128)(2,1)S(1)}, bf16[320,640]{1,0:T(8,128)(2,1)S(1)}, u32[]{:S(2)}, u32[]{:S(2)}) collective-permute-start(bf16[320,640]{1,0:T(8,128)(2,1)S(1)} %get-tuple-element.98), channel_id=1, source_target_pairs={{0,96},{4,100},{6,102},{32,0},{34,2},{38,6},{64,32},{66,34},{68,36... | collective-permute-start | bytes 1228808 | tf_op jit(solution)/shard_map/ppermute | solution.py:392
  60.9 2.8 %middle_kernel.1 = (bf16[768,640]{1,0:T(8,128)(2,1)S(1)}, bf16[640,768]{1,0:T(8,128)(2,1)S(1)}, f32[320,640]{1,0:T(8,128)S(1)}, bf16[320,640]{1,0:T(8,128)(2,1)S(1)}) custom-call(s32[6]{0:T(128)S(1)} %stack.31.where, bf16[1536,192]{1,0:T(8,128)(2,1)S(1)} %get-tuple-element.75.high, bf16[1536,192]{1,0:T(8,128)(2,1)S(1)} %get-tuple-element.76.low, ...), custom_call_target="tpu_custom_call" | custom-call | flops 1 | bytes 1 | tf_op jit(solution)/shard_map/middle_kernel/pallas_call | solution.py:323
  63.7 2.9 %collective-permute-done.9.two = bf16[320,640]{1,0:T(8,128)(2,1)S(1)} collective-permute-done((bf16[320,640]{1,0:T(8,128)(2,1)S(1)}, bf16[320,640]{1,0:T(8,128)(2,1)S(1)}, u32[]{:S(2)}, u32[]{:S(2)}) %collective-permute-start.9) | collective-permute-done | bytes 409632 | tf_op jit(solution)/shard_map/ppermute | solution.py:392
  66.6 1.3 collective-permute-done.10.three
  67.9 5.5 %far_kernel.1 = (f32[4,160,640]{2,1,0:T(8,128)S(1)}, bf16[4,160,640]{2,1,0:T(8,128)(2,1)S(1)}, bf16[768,640]{1,0:T(8,128)(2,1)S(1)}, bf16[640,768]{1,0:T(8,128)(2,1)S(1)}, bf16[1536,640]{1,0:T(8,128)(2,1)S(1)}) custom-call(s32[6]{0:T(128)S(1)} %stack.31.where, bf16[1536,192]{1,0:T(8,128)(2,1)S(1)} %get-tuple-element.75.high, ...), custom_call_target="tpu_custom_call" | custom-call | flops 1 | bytes 1 | tf_op jit(solution)/shard_map/far_kernel/pallas_call | solution.py:323
  73.5 3.7 %far_rest_kernel.1 = (f32[4,160,640]{2,1,0:T(8,128)S(1)}, bf16[4,160,640]{2,1,0:T(8,128)(2,1)S(1)}) custom-call(s32[6]{0:T(128)S(1)} %stack.31.where, bf16[640,1536]{1,0:T(8,128)(2,1)S(1)} %get-tuple-element.81.own, bf16[768,640]{1,0:T(8,128)(2,1)S(1)} %get-tuple-element.105.near, f32[320,640]{1,0:T(8,128)S(1)} %get-tuple-element.106.done, ...), custom_call_target="tpu_custom_call" | custom-call | flops 1 | bytes 1 | tf_op jit(solution)/shard_map/far_rest_kernel/pallas_call | solution.py:323
  78.7 4.7 %collective-permute-start.19 = (bf16[176,640]{1,0:T(8,128)(2,1)S(1)}, bf16[176,640]{1,0:T(8,128)(2,1)S(1)}, u32[]{:S(2)}, u32[]{:S(2)}) collective-permute-start(bf16[176,640]{1,0:T(8,128)(2,1)S(1)} %get-tuple-element.131), channel_id=1, source_target_pairs={{0,64},{32,96},{64,0},{96,32},{1,65},{33,97},{65,1},{97,33},{2,66}... | collective-permute-start | bytes 675848 | tf_op jit(solution)/shard_map/ppermute | solution.py:428
  83.8 2.9 %collective-permute-start.11 = (bf16[320,640]{1,0:T(8,128)(2,1)S(1)}, bf16[320,640]{1,0:T(8,128)(2,1)S(1)}, u32[]{:S(2)}, u32[]{:S(2)}) collective-permute-start(bf16[320,640]{1,0:T(8,128)(2,1)S(1)} %get-tuple-element.103), channel_id=1, source_target_pairs={{1,17},{16,0},{3,19},{18,2},{5,21},{20,4},{7,23},{22,6},{9,25},{24... | collective-permute-start | bytes 1228808 | tf_op jit(solution)/shard_map/ppermute | solution.py:402
  87.5 2.1 %collective-permute-start.14 = (bf16[160,640]{1,0:T(8,128)(2,1)S(1)}, bf16[160,640]{1,0:T(8,128)(2,1)S(1)}, u32[]{:S(2)}, u32[]{:S(2)}) collective-permute-start(bf16[160,640]{1,0:T(8,128)(2,1)S(1)} %get-tuple-element.122), channel_id=1, source_target_pairs={{0,32},{32,64},{64,96},{96,0},{1,33},{33,65},{65,97},{97,1},{2,34}... | collective-permute-start | bytes 614408 | tf_op jit(solution)/shard_map/ppermute | solution.py:428
  89.6 5.1 %collective-permute-done.19.two = bf16[176,640]{1,0:T(8,128)(2,1)S(1)} collective-permute-done((bf16[176,640]{1,0:T(8,128)(2,1)S(1)}, bf16[176,640]{1,0:T(8,128)(2,1)S(1)}, u32[]{:S(2)}, u32[]{:S(2)}) %collective-permute-start.19) | collective-permute-done | bytes 225312 | tf_op jit(solution)/shard_map/ppermute | solution.py:428
  95.4 1.3 collective-permute-start.21
  96.7 2.2 %collective-permute-done.14.one = bf16[160,640]{1,0:T(8,128)(2,1)S(1)} collective-permute-done((bf16[160,640]{1,0:T(8,128)(2,1)S(1)}, bf16[160,640]{1,0:T(8,128)(2,1)S(1)}, u32[]{:S(2)}, u32[]{:S(2)}) %collective-permute-start.14) | collective-permute-done | bytes 204832 | tf_op jit(solution)/shard_map/ppermute | solution.py:428
  98.9 3.5 %collective-permute-done.15.two = bf16[160,640]{1,0:T(8,128)(2,1)S(1)} collective-permute-done((bf16[160,640]{1,0:T(8,128)(2,1)S(1)}, bf16[160,640]{1,0:T(8,128)(2,1)S(1)}, u32[]{:S(2)}, u32[]{:S(2)}) %collective-permute-start.15) | collective-permute-done | bytes 204832 | tf_op jit(solution)/shard_map/ppermute | solution.py:428
  105.1 3.9 %collective-permute-start.23 = (bf16[160,640]{1,0:T(8,128)(2,1)S(1)}, bf16[160,640]{1,0:T(8,128)(2,1)S(1)}, u32[]{:S(2)}, u32[]{:S(2)}) collective-permute-start(bf16[160,640]{1,0:T(8,128)(2,1)S(1)} %get-tuple-element.140), channel_id=1, source_target_pairs={{2,32},{6,96},{32,2},{36,66},{66,36},{70,100},{96,6},{100,70},{3,3... | collective-permute-start | bytes 614408 | tf_op jit(solution)/shard_map/ppermute | solution.py:446
  110.5 4.8 %collective-permute-start.24 = (bf16[160,640]{1,0:T(8,128)(2,1)S(1)}, bf16[160,640]{1,0:T(8,128)(2,1)S(1)}, u32[]{:S(2)}, u32[]{:S(2)}) collective-permute-start(bf16[160,640]{1,0:T(8,128)(2,1)S(1)} %get-tuple-element.144), channel_id=1, source_target_pairs={{2,32},{6,96},{32,2},{36,66},{66,36},{70,100},{96,6},{100,70},{3,3... | collective-permute-start | bytes 614408 | tf_op jit(solution)/shard_map/ppermute | solution.py:450
  117.9 3.2 %collective-permute-start.26 = (bf16[320,640]{1,0:T(8,128)(2,1)S(1)}, bf16[320,640]{1,0:T(8,128)(2,1)S(1)}, u32[]{:S(2)}, u32[]{:S(2)}) collective-permute-start(bf16[320,640]{1,0:T(8,128)(2,1)S(1)} %get-tuple-element.146), channel_id=1, source_target_pairs={{1,16},{16,1},{3,18},{18,3},{5,20},{20,5},{7,22},{22,7},{9,24},{24... | collective-permute-start | bytes 1228808 | tf_op jit(solution)/shard_map/ppermute | solution.py:455
  121.1 7.3 %collective-permute-done.24.mirror_last = bf16[160,640]{1,0:T(8,128)(2,1)S(1)} collective-permute-done((bf16[160,640]{1,0:T(8,128)(2,1)S(1)}, bf16[160,640]{1,0:T(8,128)(2,1)S(1)}, u32[]{:S(2)}, u32[]{:S(2)}) %collective-permute-start.24) | collective-permute-done | bytes 204832 | tf_op jit(solution)/shard_map/ppermute | solution.py:450
  129.3 2.0 %collective-permute-done.26.across = bf16[320,640]{1,0:T(8,128)(2,1)S(1)} collective-permute-done((bf16[320,640]{1,0:T(8,128)(2,1)S(1)}, bf16[320,640]{1,0:T(8,128)(2,1)S(1)}, u32[]{:S(2)}, u32[]{:S(2)}) %collective-permute-start.26) | collective-permute-done | bytes 409632 | tf_op jit(solution)/shard_map/ppermute | solution.py:455
  131.3 1.5 %finish_kernel.1 = f32[320,640]{1,0:T(8,128)} custom-call(s32[6]{0:T(128)S(1)} %stack.31.where, f32[320,640]{1,0:T(8,128)S(1)} %base_kernel.1.base, bf16[320,640]{1,0:T(8,128)(2,1)S(1)} %collective-permute-done.26.across), custom_call_target="tpu_custom_call" | custom-call | flops 1 | bytes 1 | tf_op jit(solution)/shard_map/finish_kernel/pallas_call | solution.py:323
  (60 shorter events, 18.3 us)
Async XLA Ops:
  0.6 14.7 %copy-start = (bf16[1536,640]{1,0:T(8,128)(2,1)S(1)}, bf16[1536,640]{1,0:T(8,128)(2,1)}, u32[]{:S(2)}) copy-start(bf16[1536,640]{1,0:T(8,128)(2,1)} %rows.1) | copy-start | bytes 5898244
  0.6 7.5 %copy-start.5 = (f32[1536]{0:T(1024)S(1)}, f32[1536]{0:T(1024)}, u32[]{:S(2)}) copy-start(f32[1536]{0:T(1024)} %param.7) | copy-start | bytes 18436
  0.7 7.5 %copy-start.6 = (s32[1536]{0:T(1024)S(1)}, s32[1536]{0:T(1024)}, u32[]{:S(2)}) copy-start(s32[1536]{0:T(1024)} %param.8) | copy-start | bytes 18436
  0.7 7.6 %copy-start.4 = (f32[16,1536]{1,0:T(8,128)S(1)}, f32[16,1536]{1,0:T(8,128)}, u32[]{:S(2)}) copy-start(f32[16,1536]{1,0:T(8,128)} %param.6) | copy-start | bytes 294916
  3.8 23.8 %collective-permute-start.1 = (bf16[768,640]{1,0:T(8,128)(2,1)}, bf16[768,640]{1,0:T(8,128)(2,1)}, u32[]{:S(2)}, u32[]{:S(2)}) collective-permute-start(bf16[768,640]{1,0:T(8,128)(2,1)} %get-tuple-element.89), channel_id=1, source_target_pairs={{0,2},{2,4},{4,6},{6,0},{1,3},{3,5},{5,7},{7,1},{8,10},{10,12},{12... | collective-permute-start | bytes 2949128 | tf_op jit(solution)/shard_map/ppermute | solution.py:352
  4.3 25.0 %collective-permute-start.2 = (bf16[768,640]{1,0:T(8,128)(2,1)}, bf16[768,640]{1,0:T(8,128)(2,1)}, u32[]{:S(2)}, u32[]{:S(2)}) collective-permute-start(bf16[768,640]{1,0:T(8,128)(2,1)} %get-tuple-element.149), channel_id=1, source_target_pairs={{0,1},{1,0},{2,3},{3,2},{4,5},{5,4},{6,7},{7,6},{8,9},{9,8},{10,11... | collective-permute-start | bytes 2949128 | tf_op jit(solution)/shard_map/ppermute | solution.py:353
  6.6 24.5 %collective-permute-start = (bf16[768,640]{1,0:T(8,128)(2,1)}, bf16[768,640]{1,0:T(8,128)(2,1)}, u32[]{:S(2)}, u32[]{:S(2)}) collective-permute-start(bf16[768,640]{1,0:T(8,128)(2,1)} %get-tuple-element.149), channel_id=1, source_target_pairs={{0,6},{2,0},{4,2},{6,4},{1,7},{3,1},{5,3},{7,5},{8,14},{10,8},{12,... | collective-permute-start | bytes 2949128 | tf_op jit(solution)/shard_map/ppermute | solution.py:351
  15.4 0.7 copy-start.2
  19.9 1.9 %collective-permute-start.3 = (bf16[336,640]{1,0:T(8,128)(2,1)S(1)}, bf16[336,640]{1,0:T(8,128)(2,1)S(1)}, u32[]{:S(2)}, u32[]{:S(2)}) collective-permute-start(bf16[336,640]{1,0:T(8,128)(2,1)S(1)} %get-tuple-element.80), channel_id=1, source_target_pairs={{0,8},{8,0},{1,9},{9,1},{2,10},{10,2},{3,11},{11,3},{4,12},{12,4},... | collective-permute-start | bytes 1290248 | tf_op jit(solution)/shard_map/ppermute | solution.py:367
  31.0 23.7 %collective-permute-start.5 = (bf16[768,640]{1,0:T(8,128)(2,1)}, bf16[768,640]{1,0:T(8,128)(2,1)S(1)}, u32[]{:S(2)}, u32[]{:S(2)}) collective-permute-start(bf16[768,640]{1,0:T(8,128)(2,1)} %get-tuple-element.89), channel_id=1, source_target_pairs={{0,1},{1,0},{2,3},{3,2},{4,5},{5,4},{6,7},{7,6},{8,9},{9,8},{10,11... | collective-permute-start | bytes 2949128 | tf_op jit(solution)/shard_map/ppermute | solution.py:372
  36.7 3.4 %collective-permute-start.4 = (bf16[2,320,640]{2,1,0:T(8,128)(2,1)S(1)}, bf16[2,320,640]{2,1,0:T(8,128)(2,1)S(1)}, u32[]{:S(2)}, u32[]{:S(2)}) collective-permute-start(bf16[2,320,640]{2,1,0:T(8,128)(2,1)S(1)} %get-tuple-element.87), channel_id=1, source_target_pairs={{0,8},{8,0},{1,9},{9,1},{2,10},{10,2},{3,11},{11,3},{4,12},{12,4},... | collective-permute-start | bytes 2457608 | tf_op jit(solution)/shard_map/ppermute | solution.py:383
  36.8 26.9 %collective-permute-start.6 = (bf16[768,640]{1,0:T(8,128)(2,1)}, bf16[768,640]{1,0:T(8,128)(2,1)S(1)}, u32[]{:S(2)}, u32[]{:S(2)}) collective-permute-start(bf16[768,640]{1,0:T(8,128)(2,1)} %collective-permute-done.above), channel_id=1, source_target_pairs={{0,6},{2,0},{4,2},{6,4},{1,7},{3,1},{5,3},{7,5},{8,14},{10,8},{12,... | collective-permute-start | bytes 2949128 | tf_op jit(solution)/shard_map/ppermute | solution.py:373
  37.8 25.9 %collective-permute-start.7 = (bf16[768,640]{1,0:T(8,128)(2,1)}, bf16[768,640]{1,0:T(8,128)(2,1)S(1)}, u32[]{:S(2)}, u32[]{:S(2)}) collective-permute-start(bf16[768,640]{1,0:T(8,128)(2,1)} %collective-permute-done.1.below), channel_id=1, source_target_pairs={{0,2},{2,4},{4,6},{6,0},{1,3},{3,5},{5,7},{7,1},{8,10},{10,12},{12... | collective-permute-start | bytes 2949128 | tf_op jit(solution)/shard_map/ppermute | solution.py:374
  41.2 22.5 %collective-permute-start.8 = (bf16[320,640]{1,0:T(8,128)(2,1)S(1)}, bf16[320,640]{1,0:T(8,128)(2,1)S(1)}, u32[]{:S(2)}, u32[]{:S(2)}) collective-permute-start(bf16[320,640]{1,0:T(8,128)(2,1)S(1)} %get-tuple-element.96), channel_id=1, source_target_pairs={{0,32},{2,34},{4,36},{34,66},{36,68},{38,70},{64,96},{68,100},{70,... | collective-permute-start | bytes 1228808 | tf_op jit(solution)/shard_map/ppermute | solution.py:392
  42.5 24.1 %collective-permute-start.9 = (bf16[320,640]{1,0:T(8,128)(2,1)S(1)}, bf16[320,640]{1,0:T(8,128)(2,1)S(1)}, u32[]{:S(2)}, u32[]{:S(2)}) collective-permute-start(bf16[320,640]{1,0:T(8,128)(2,1)S(1)} %get-tuple-element.97), channel_id=1, source_target_pairs={{2,66},{4,68},{6,70},{32,96},{36,100},{38,102},{64,0},{66,2},{70,6... | collective-permute-start | bytes 1228808 | tf_op jit(solution)/shard_map/ppermute | solution.py:392
  54.8 13.1 %collective-permute-start.10 = (bf16[320,640]{1,0:T(8,128)(2,1)S(1)}, bf16[320,640]{1,0:T(8,128)(2,1)S(1)}, u32[]{:S(2)}, u32[]{:S(2)}) collective-permute-start(bf16[320,640]{1,0:T(8,128)(2,1)S(1)} %get-tuple-element.98), channel_id=1, source_target_pairs={{0,96},{4,100},{6,102},{32,0},{34,2},{38,6},{64,32},{66,34},{68,36... | collective-permute-start | bytes 1228808 | tf_op jit(solution)/shard_map/ppermute | solution.py:392
  73.4 3.8 %collective-permute-start.12 = (bf16[4,160,640]{2,1,0:T(8,128)(2,1)S(1)}, bf16[4,160,640]{2,1,0:T(8,128)(2,1)S(1)}, u32[]{:S(2)}, u32[]{:S(2)}) collective-permute-start(bf16[4,160,640]{2,1,0:T(8,128)(2,1)S(1)} %get-tuple-element.118), channel_id=1, source_target_pairs={{0,8},{8,0},{1,9},{9,1},{2,10},{10,2},{3,11},{11,3},{4,12},{12,4},... | collective-permute-start | bytes 2457608 | tf_op jit(solution)/shard_map/ppermute | solution.py:413
  77.3 9.5 %collective-permute-start.13 = (bf16[4,160,640]{2,1,0:T(8,128)(2,1)S(1)}, bf16[4,160,640]{2,1,0:T(8,128)(2,1)S(1)}, u32[]{:S(2)}, u32[]{:S(2)}) collective-permute-start(bf16[4,160,640]{2,1,0:T(8,128)(2,1)S(1)} %get-tuple-element.120), channel_id=1, source_target_pairs={{0,8},{8,0},{1,9},{9,1},{2,10},{10,2},{3,11},{11,3},{4,12},{12,4},... | collective-permute-start | bytes 2457608 | tf_op jit(solution)/shard_map/ppermute | solution.py:421
  78.6 11.0 %collective-permute-start.18 = (bf16[176,640]{1,0:T(8,128)(2,1)S(1)}, bf16[176,640]{1,0:T(8,128)(2,1)S(1)}, u32[]{:S(2)}, u32[]{:S(2)}) collective-permute-start(bf16[176,640]{1,0:T(8,128)(2,1)S(1)} %get-tuple-element.130), channel_id=1, source_target_pairs={{0,32},{32,64},{64,96},{96,0},{1,33},{33,65},{65,97},{97,1},{2,34}... | collective-permute-start | bytes 675848 | tf_op jit(solution)/shard_map/ppermute | solution.py:428
  78.7 16.0 %collective-permute-start.19 = (bf16[176,640]{1,0:T(8,128)(2,1)S(1)}, bf16[176,640]{1,0:T(8,128)(2,1)S(1)}, u32[]{:S(2)}, u32[]{:S(2)}) collective-permute-start(bf16[176,640]{1,0:T(8,128)(2,1)S(1)} %get-tuple-element.131), channel_id=1, source_target_pairs={{0,64},{32,96},{64,0},{96,32},{1,65},{33,97},{65,1},{97,33},{2,66}... | collective-permute-start | bytes 675848 | tf_op jit(solution)/shard_map/ppermute | solution.py:428
  83.4 11.2 %collective-permute-start.20 = (bf16[176,640]{1,0:T(8,128)(2,1)S(1)}, bf16[176,640]{1,0:T(8,128)(2,1)S(1)}, u32[]{:S(2)}, u32[]{:S(2)}) collective-permute-start(bf16[176,640]{1,0:T(8,128)(2,1)S(1)} %get-tuple-element.132), channel_id=1, source_target_pairs={{0,96},{32,0},{64,32},{96,64},{1,97},{33,1},{65,33},{97,65},{2,98}... | collective-permute-start | bytes 675848 | tf_op jit(solution)/shard_map/ppermute | solution.py:428
  83.8 20.5 %collective-permute-start.11 = (bf16[320,640]{1,0:T(8,128)(2,1)S(1)}, bf16[320,640]{1,0:T(8,128)(2,1)S(1)}, u32[]{:S(2)}, u32[]{:S(2)}) collective-permute-start(bf16[320,640]{1,0:T(8,128)(2,1)S(1)} %get-tuple-element.103), channel_id=1, source_target_pairs={{1,17},{16,0},{3,19},{18,2},{5,21},{20,4},{7,23},{22,6},{9,25},{24... | collective-permute-start | bytes 1228808 | tf_op jit(solution)/shard_map/ppermute | solution.py:402
  87.5 11.5 %collective-permute-start.14 = (bf16[160,640]{1,0:T(8,128)(2,1)S(1)}, bf16[160,640]{1,0:T(8,128)(2,1)S(1)}, u32[]{:S(2)}, u32[]{:S(2)}) collective-permute-start(bf16[160,640]{1,0:T(8,128)(2,1)S(1)} %get-tuple-element.122), channel_id=1, source_target_pairs={{0,32},{32,64},{64,96},{96,0},{1,33},{33,65},{65,97},{97,1},{2,34}... | collective-permute-start | bytes 614408 | tf_op jit(solution)/shard_map/ppermute | solution.py:428
  89.6 12.9 %collective-permute-start.15 = (bf16[160,640]{1,0:T(8,128)(2,1)S(1)}, bf16[160,640]{1,0:T(8,128)(2,1)S(1)}, u32[]{:S(2)}, u32[]{:S(2)}) collective-permute-start(bf16[160,640]{1,0:T(8,128)(2,1)S(1)} %get-tuple-element.123), channel_id=1, source_target_pairs={{0,64},{32,96},{64,0},{96,32},{1,65},{33,97},{65,1},{97,33},{2,66}... | collective-permute-start | bytes 614408 | tf_op jit(solution)/shard_map/ppermute | solution.py:428
  94.6 7.8 %collective-permute-start.16 = (bf16[160,640]{1,0:T(8,128)(2,1)S(1)}, bf16[160,640]{1,0:T(8,128)(2,1)S(1)}, u32[]{:S(2)}, u32[]{:S(2)}) collective-permute-start(bf16[160,640]{1,0:T(8,128)(2,1)S(1)} %get-tuple-element.124), channel_id=1, source_target_pairs={{0,96},{32,0},{64,32},{96,64},{1,97},{33,1},{65,33},{97,65},{2,98}... | collective-permute-start | bytes 614408 | tf_op jit(solution)/shard_map/ppermute | solution.py:428
  95.4 8.9 %collective-permute-start.21 = (bf16[176,640]{1,0:T(8,128)(2,1)S(1)}, bf16[176,640]{1,0:T(8,128)(2,1)S(1)}, u32[]{:S(2)}, u32[]{:S(2)}) collective-permute-start(bf16[176,640]{1,0:T(8,128)(2,1)S(1)} %get-tuple-element.134), channel_id=1, source_target_pairs={{0,16},{16,0},{1,17},{17,1},{2,18},{18,2},{3,19},{19,3},{4,20},{20... | collective-permute-start | bytes 675848 | tf_op jit(solution)/shard_map/ppermute | solution.py:438
  103.2 6.2 %collective-permute-start.17 = (bf16[160,640]{1,0:T(8,128)(2,1)S(1)}, bf16[160,640]{1,0:T(8,128)(2,1)S(1)}, u32[]{:S(2)}, u32[]{:S(2)}) collective-permute-start(bf16[160,640]{1,0:T(8,128)(2,1)S(1)} %get-tuple-element.126), channel_id=1, source_target_pairs={{0,16},{16,0},{1,17},{17,1},{2,18},{18,2},{3,19},{19,3},{4,20},{20... | collective-permute-start | bytes 614408 | tf_op jit(solution)/shard_map/ppermute | solution.py:438
  105.1 11.5 %collective-permute-start.23 = (bf16[160,640]{1,0:T(8,128)(2,1)S(1)}, bf16[160,640]{1,0:T(8,128)(2,1)S(1)}, u32[]{:S(2)}, u32[]{:S(2)}) collective-permute-start(bf16[160,640]{1,0:T(8,128)(2,1)S(1)} %get-tuple-element.140), channel_id=1, source_target_pairs={{2,32},{6,96},{32,2},{36,66},{66,36},{70,100},{96,6},{100,70},{3,3... | collective-permute-start | bytes 614408 | tf_op jit(solution)/shard_map/ppermute | solution.py:446
  110.4 6.2 %collective-permute-start.22 = (bf16[320,320]{1,0:T(8,128)(2,1)S(1)}, bf16[320,320]{1,0:T(8,128)(2,1)S(1)}, u32[]{:S(2)}, u32[]{:S(2)}) collective-permute-start(bf16[320,320]{1,0:T(8,128)(2,1)S(1)} %get-tuple-element.139), channel_id=1, source_target_pairs={{0,8},{8,0},{1,9},{9,1},{2,10},{10,2},{3,11},{11,3},{4,12},{12,4},... | collective-permute-start | bytes 614408 | tf_op jit(solution)/shard_map/ppermute | solution.py:452
  110.5 17.9 %collective-permute-start.24 = (bf16[160,640]{1,0:T(8,128)(2,1)S(1)}, bf16[160,640]{1,0:T(8,128)(2,1)S(1)}, u32[]{:S(2)}, u32[]{:S(2)}) collective-permute-start(bf16[160,640]{1,0:T(8,128)(2,1)S(1)} %get-tuple-element.144), channel_id=1, source_target_pairs={{2,32},{6,96},{32,2},{36,66},{66,36},{70,100},{96,6},{100,70},{3,3... | collective-permute-start | bytes 614408 | tf_op jit(solution)/shard_map/ppermute | solution.py:450
  115.3 13.1 %collective-permute-start.25 = (bf16[320,320]{1,0:T(8,128)(2,1)S(1)}, bf16[320,320]{1,0:T(8,128)(2,1)S(1)}, u32[]{:S(2)}, u32[]{:S(2)}) collective-permute-start(bf16[320,320]{1,0:T(8,128)(2,1)S(1)} %get-tuple-element.145), channel_id=1, source_target_pairs={{4,64},{38,98},{64,4},{98,38},{5,65},{39,99},{65,5},{99,39},{12,72... | collective-permute-start | bytes 614408 | tf_op jit(solution)/shard_map/ppermute | solution.py:451
  117.9 13.5 %collective-permute-start.26 = (bf16[320,640]{1,0:T(8,128)(2,1)S(1)}, bf16[320,640]{1,0:T(8,128)(2,1)S(1)}, u32[]{:S(2)}, u32[]{:S(2)}) collective-permute-start(bf16[320,640]{1,0:T(8,128)(2,1)S(1)} %get-tuple-element.146), channel_id=1, source_target_pairs={{1,16},{16,1},{3,18},{18,3},{5,20},{20,5},{7,22},{22,7},{9,24},{24... | collective-permute-start | bytes 1228808 | tf_op jit(solution)/shard_map/ppermute | solution.py:455
  (2 other events, 1.3 us)

commit v4 on v3

--- a/solution.py
+++ b/solution.py
@@ -399,7 +399,7 @@
         (flip_bottom, above2, below2, flip_top, ups)
     )
     early, send = call(near_total_kernel, (wide, sent), mine, *ups, scalars=False)
-    early_got = lax.ppermute(send, ("yl", "yh"), [(1, 3), (2, 0)])
+    early_send = send
     chunks = 2
     size = half // chunks
     pieces = (shape((nz, size, width), F32), shape((nz, size, width), BF16))
@@ -425,7 +425,10 @@
     for chunk, (keep, got) in enumerate(zip(keeps, gots)):
         up = shape((size + (low_rows if chunk == 0 else 0), width), BF16)
         mine, *ups = call(far_spread_kernel, (part, up, up, up), where, keep, got, rhs)
+        if chunk:
+            ups[0], early_send = lax.optimization_barrier((ups[0], early_send))
         sums.append((mine, [lax.ppermute(v, "z", turn(k)) for k, v in enumerate(ups, 1)]))
+    early_got = lax.ppermute(early_send, ("yl", "yh"), [(1, 3), (2, 0)])
     halves = []
     for chunk, (mine, ups) in enumerate(sums):
         extra = (row,) if chunk == 0 else ()

time: 133 us -> 133 us (level)
  transfers between devices with their start and end apart: 27 -> 27, of which waited for: 13 -> 14; matrix products, arithmetic and copies ran while one was open for 1% -> 1% of each run, Pallas kernels for 22% -> 22%
where the time goes in v4:
time: 133 us
  starting transfers between devices  50.1 us (38%)
  waiting for transfers between devices  40.2 us (30%)
  Pallas kernels  35.6 us (27%)
  local copies, waits for them, and re-layouts  5.44 us (4%)
    pallas_call x16, Pallas kernels, call(): pl.pallas_call(functools.partial(kernel, *statics), out_shape=outs, in_sp...  30 us
    ppermute x3, starting transfers between devices, body(): lax.ppermute(v, ('z', 'x'), early_turn(k))  15.4 us
    ppermute x6, waiting for transfers between devices, body(): lax.ppermute(v, 'z', turn(k))  10.9 us
    ppermute x1, waiting for transfers between devices, body(): mirror_last = lax.ppermute(mirror_last, ('z', 'x'), beside)  7.35 us
    ppermute x6, starting transfers between devices, body(): lax.ppermute(v, 'z', turn(k))  6.91 us
    ppermute x1, waiting for transfers between devices, body(): below = lax.ppermute(lower, 'x', up)  5.84 us
    pallas_call x1, Pallas kernels, eliminate(): pl.pallas_call(eliminate_kernel, out_shape=(shape((arcs * SLOTS, SLOTS),...  5.61 us
    ppermute x1, starting transfers between devices, body(): mirror_last = lax.ppermute(mirror_last, ('z', 'x'), beside)  4.84 us
  transfers between devices with their start and end apart: 27, of which 14 were waited for; matrix products, arithmetic and copies ran while one was open for 1% of the time, Pallas kernels for 22%

profile of v4, /device:TPU:14, one launch (start us, length us, event | category | flops | bytes accessed | tf_op | source)
XLA Modules:
  0.0 132.8 jit_solution(13849422234664987568)
XLA Ops:
  0.7 3.1 %fusion = (bf16[768,640]{1,0:T(8,128)(2,1)}, bf16[768,640]{1,0:T(8,128)(2,1)}) fusion(bf16[1536,640]{1,0:T(8,128)(2,1)} %rows.1), kind=kLoop, calls=%fused_computation.1 | loop fusion | bytes 3932160 | tf_op jit(solution)/shard_map/slice | solution.py:350
  4.3 2.3 %collective-permute-start.2 = (bf16[768,640]{1,0:T(8,128)(2,1)}, bf16[768,640]{1,0:T(8,128)(2,1)}, u32[]{:S(2)}, u32[]{:S(2)}) collective-permute-start(bf16[768,640]{1,0:T(8,128)(2,1)} %get-tuple-element.153), channel_id=1, source_target_pairs={{0,1},{1,0},{2,3},{3,2},{4,5},{5,4},{6,7},{7,6},{8,9},{9,8},{10,11... | collective-permute-start | bytes 2949128 | tf_op jit(solution)/shard_map/ppermute | solution.py:353
  6.6 1.5 %collective-permute-start = (bf16[768,640]{1,0:T(8,128)(2,1)}, bf16[768,640]{1,0:T(8,128)(2,1)}, u32[]{:S(2)}, u32[]{:S(2)}) collective-permute-start(bf16[768,640]{1,0:T(8,128)(2,1)} %get-tuple-element.153), channel_id=1, source_target_pairs={{0,6},{2,0},{4,2},{6,4},{1,7},{3,1},{5,3},{7,5},{8,14},{10,8},{12,... | collective-permute-start | bytes 2949128 | tf_op jit(solution)/shard_map/ppermute | solution.py:351
  9.1 5.6 %eliminate.1 = (bf16[1536,192]{1,0:T(8,128)(2,1)S(1)}, bf16[1536,192]{1,0:T(8,128)(2,1)S(1)}, f32[8,192]{1,0:T(8,128)S(1)}) custom-call(s32[8]{0:T(128)S(1)} %copy-done.3, f32[8,16,192]{2,1,0:T(8,128)S(1)} %bitcast.9, f32[8,192]{1,0:T(8,128)S(1)} %reshape.14.observed, s32[8,192]{1,0:T(8,128)S(1)} %reshape.15.valid), custom_call_target="tpu_custom_call" | custom-call | flops 1 | bytes 1 | tf_op jit(solution)/shard_map/eliminate/pallas_call | solution.py:69
  16.1 3.8 %own_kernel.1 = (bf16[1536,640]{1,0:T(8,128)(2,1)}, bf16[640,1536]{1,0:T(8,128)(2,1)S(1)}, f32[320,640]{1,0:T(8,128)S(1)}, bf16[336,640]{1,0:T(8,128)(2,1)S(1)}, f32[1,640]{1,0:T(1,128)S(1)}) custom-call(s32[6]{0:T(128)S(1)} %stack.31.where, bf16[1536,192]{1,0:T(8,128)(2,1)S(1)} %get-tuple-element.77.high, bf16[1536,192]{1,0:T(8,128)(2,1)S(1)} %get-tuple-element.78.low, ...), custom_call_target="tpu_custom_call" | custom-call | flops 1 | bytes 1 | tf_op jit(solution)/shard_map/own_kernel/pallas_call | solution.py:323
  20.0 1.8 %collective-permute-done.3.own_got = bf16[336,640]{1,0:T(8,128)(2,1)S(1)} collective-permute-done((bf16[336,640]{1,0:T(8,128)(2,1)S(1)}, bf16[336,640]{1,0:T(8,128)(2,1)S(1)}, u32[]{:S(2)}, u32[]{:S(2)}) %collective-permute-start.3) | collective-permute-done | bytes 430112 | tf_op jit(solution)/shard_map/ppermute | solution.py:367
  21.8 5.8 %collective-permute-done.1.below = bf16[768,640]{1,0:T(8,128)(2,1)} collective-permute-done((bf16[768,640]{1,0:T(8,128)(2,1)}, bf16[768,640]{1,0:T(8,128)(2,1)}, u32[]{:S(2)}, u32[]{:S(2)}) %collective-permute-start.1) | collective-permute-done | bytes 983072 | tf_op jit(solution)/shard_map/ppermute | solution.py:352
  27.6 1.7 %collective-permute-done.2.rows = bf16[768,640]{1,0:T(8,128)(2,1)} collective-permute-done((bf16[768,640]{1,0:T(8,128)(2,1)}, bf16[768,640]{1,0:T(8,128)(2,1)}, u32[]{:S(2)}, u32[]{:S(2)}) %collective-permute-start.2) | collective-permute-done | bytes 983072 | tf_op jit(solution)/shard_map/ppermute | solution.py:353
  29.3 1.7 %collective-permute-done.above = bf16[768,640]{1,0:T(8,128)(2,1)} collective-permute-done((bf16[768,640]{1,0:T(8,128)(2,1)}, bf16[768,640]{1,0:T(8,128)(2,1)}, u32[]{:S(2)}, u32[]{:S(2)}) %collective-permute-start) | collective-permute-done | bytes 983072 | tf_op jit(solution)/shard_map/ppermute | solution.py:351
  32.3 4.4 %near_kernel.1 = (bf16[768,640]{1,0:T(8,128)(2,1)S(1)}, bf16[768,640]{1,0:T(8,128)(2,1)S(1)}, f32[2,320,640]{2,1,0:T(8,128)S(1)}, bf16[2,320,640]{2,1,0:T(8,128)(2,1)S(1)}) custom-call(s32[6]{0:T(128)S(1)} %stack.31.where, bf16[1536,192]{1,0:T(8,128)(2,1)S(1)} %get-tuple-element.77.high, bf16[1536,192]{1,0:T(8,128)(2,1)S(1)} %get-tuple-element.78.low, ...), custom_call_target="tpu_custom_call" | custom-call | flops 1 | bytes 1 | tf_op jit(solution)/shard_map/near_kernel/pallas_call | solution.py:323
  37.8 2.3 %collective-permute-start.7 = (bf16[768,640]{1,0:T(8,128)(2,1)}, bf16[768,640]{1,0:T(8,128)(2,1)S(1)}, u32[]{:S(2)}, u32[]{:S(2)}) collective-permute-start(bf16[768,640]{1,0:T(8,128)(2,1)} %collective-permute-done.1.below), channel_id=1, source_target_pairs={{0,2},{2,4},{4,6},{6,0},{1,3},{3,5},{5,7},{7,1},{8,10},{10,12},{12... | collective-permute-start | bytes 2949128 | tf_op jit(solution)/shard_map/ppermute | solution.py:374
  41.2 1.3 collective-permute-start.8
  42.5 8.0 %collective-permute-start.9 = (bf16[320,640]{1,0:T(8,128)(2,1)S(1)}, bf16[320,640]{1,0:T(8,128)(2,1)S(1)}, u32[]{:S(2)}, u32[]{:S(2)}) collective-permute-start(bf16[320,640]{1,0:T(8,128)(2,1)S(1)} %get-tuple-element.99), channel_id=1, source_target_pairs={{2,66},{4,68},{6,70},{32,96},{36,100},{38,102},{64,0},{66,2},{70,6... | collective-permute-start | bytes 1228808 | tf_op jit(solution)/shard_map/ppermute | solution.py:392
  50.5 4.2 %collective-permute-done.5.rows = bf16[768,640]{1,0:T(8,128)(2,1)S(1)} collective-permute-done((bf16[768,640]{1,0:T(8,128)(2,1)}, bf16[768,640]{1,0:T(8,128)(2,1)S(1)}, u32[]{:S(2)}, u32[]{:S(2)}) %collective-permute-start.5) | collective-permute-done | bytes 983072 | tf_op jit(solution)/shard_map/ppermute | solution.py:372
  54.8 6.1 %collective-permute-start.10 = (bf16[320,640]{1,0:T(8,128)(2,1)S(1)}, bf16[320,640]{1,0:T(8,128)(2,1)S(1)}, u32[]{:S(2)}, u32[]{:S(2)}) collective-permute-start(bf16[320,640]{1,0:T(8,128)(2,1)S(1)} %get-tuple-element.100), channel_id=1, source_target_pairs={{0,96},{4,100},{6,102},{32,0},{34,2},{38,6},{64,32},{66,34},{68,36... | collective-permute-start | bytes 1228808 | tf_op jit(solution)/shard_map/ppermute | solution.py:392
  60.9 2.8 %middle_kernel.1 = (bf16[768,640]{1,0:T(8,128)(2,1)S(1)}, bf16[640,768]{1,0:T(8,128)(2,1)S(1)}, f32[320,640]{1,0:T(8,128)S(1)}, bf16[320,640]{1,0:T(8,128)(2,1)S(1)}) custom-call(s32[6]{0:T(128)S(1)} %stack.31.where, bf16[1536,192]{1,0:T(8,128)(2,1)S(1)} %get-tuple-element.77.high, bf16[1536,192]{1,0:T(8,128)(2,1)S(1)} %get-tuple-element.78.low, ...), custom_call_target="tpu_custom_call" | custom-call | flops 1 | bytes 1 | tf_op jit(solution)/shard_map/middle_kernel/pallas_call | solution.py:323
  63.7 2.9 %collective-permute-done.9.two = bf16[320,640]{1,0:T(8,128)(2,1)S(1)} collective-permute-done((bf16[320,640]{1,0:T(8,128)(2,1)S(1)}, bf16[320,640]{1,0:T(8,128)(2,1)S(1)}, u32[]{:S(2)}, u32[]{:S(2)}) %collective-permute-start.9) | collective-permute-done | bytes 409632 | tf_op jit(solution)/shard_map/ppermute | solution.py:392
  66.6 1.3 collective-permute-done.10.three
  67.9 5.5 %far_kernel.1 = (f32[4,160,640]{2,1,0:T(8,128)S(1)}, bf16[4,160,640]{2,1,0:T(8,128)(2,1)S(1)}, bf16[768,640]{1,0:T(8,128)(2,1)S(1)}, bf16[640,768]{1,0:T(8,128)(2,1)S(1)}, bf16[1536,640]{1,0:T(8,128)(2,1)S(1)}) custom-call(s32[6]{0:T(128)S(1)} %stack.31.where, bf16[1536,192]{1,0:T(8,128)(2,1)S(1)} %get-tuple-element.77.high, ...), custom_call_target="tpu_custom_call" | custom-call | flops 1 | bytes 1 | tf_op jit(solution)/shard_map/far_kernel/pallas_call | solution.py:323
  73.5 3.7 %far_rest_kernel.1 = (f32[4,160,640]{2,1,0:T(8,128)S(1)}, bf16[4,160,640]{2,1,0:T(8,128)(2,1)S(1)}) custom-call(s32[6]{0:T(128)S(1)} %stack.31.where, bf16[640,1536]{1,0:T(8,128)(2,1)S(1)} %get-tuple-element.83.own, bf16[768,640]{1,0:T(8,128)(2,1)S(1)} %get-tuple-element.105.near, f32[320,640]{1,0:T(8,128)S(1)} %get-tuple-element.106.done, ...), custom_call_target="tpu_custom_call" | custom-call | flops 1 | bytes 1 | tf_op jit(solution)/shard_map/far_rest_kernel/pallas_call | solution.py:323
  78.7 4.7 %collective-permute-start.19 = (bf16[176,640]{1,0:T(8,128)(2,1)S(1)}, bf16[176,640]{1,0:T(8,128)(2,1)S(1)}, u32[]{:S(2)}, u32[]{:S(2)}) collective-permute-start(bf16[176,640]{1,0:T(8,128)(2,1)S(1)} %get-tuple-element.135), channel_id=1, source_target_pairs={{0,64},{32,96},{64,0},{96,32},{1,65},{33,97},{65,1},{97,33},{2,66}... | collective-permute-start | bytes 675848 | tf_op jit(solution)/shard_map/ppermute | solution.py:430
  84.5 2.1 %collective-permute-start.14 = (bf16[160,640]{1,0:T(8,128)(2,1)S(1)}, bf16[160,640]{1,0:T(8,128)(2,1)S(1)}, u32[]{:S(2)}, u32[]{:S(2)}) collective-permute-start(bf16[160,640]{1,0:T(8,128)(2,1)S(1)} %get-tuple-element.126), channel_id=1, source_target_pairs={{0,32},{32,64},{64,96},{96,0},{1,33},{33,65},{65,97},{97,1},{2,34}... | collective-permute-start | bytes 614408 | tf_op jit(solution)/shard_map/ppermute | solution.py:430
  87.6 2.9 %collective-permute-start.13 = (bf16[320,640]{1,0:T(8,128)(2,1)S(1)}, bf16[320,640]{1,0:T(8,128)(2,1)S(1)}, u32[]{:S(2)}, u32[]{:S(2)}) collective-permute-start(bf16[320,640]{1,0:T(8,128)(2,1)S(1)} %get-tuple-element.124), channel_id=1, source_target_pairs={{1,17},{16,0},{3,19},{18,2},{5,21},{20,4},{7,23},{22,6},{9,25},{24... | collective-permute-start | bytes 1228808 | tf_op jit(solution)/shard_map/ppermute | solution.py:431
  90.6 4.1 %collective-permute-done.19.two = bf16[176,640]{1,0:T(8,128)(2,1)S(1)} collective-permute-done((bf16[176,640]{1,0:T(8,128)(2,1)S(1)}, bf16[176,640]{1,0:T(8,128)(2,1)S(1)}, u32[]{:S(2)}, u32[]{:S(2)}) %collective-permute-start.19) | collective-permute-done | bytes 225312 | tf_op jit(solution)/shard_map/ppermute | solution.py:430
  95.4 1.3 collective-permute-start.21
  97.1 5.4 %collective-permute-done.15.two = bf16[160,640]{1,0:T(8,128)(2,1)S(1)} collective-permute-done((bf16[160,640]{1,0:T(8,128)(2,1)S(1)}, bf16[160,640]{1,0:T(8,128)(2,1)S(1)}, u32[]{:S(2)}, u32[]{:S(2)}) %collective-permute-start.15) | collective-permute-done | bytes 204832 | tf_op jit(solution)/shard_map/ppermute | solution.py:430
  105.1 3.9 %collective-permute-start.23 = (bf16[160,640]{1,0:T(8,128)(2,1)S(1)}, bf16[160,640]{1,0:T(8,128)(2,1)S(1)}, u32[]{:S(2)}, u32[]{:S(2)}) collective-permute-start(bf16[160,640]{1,0:T(8,128)(2,1)S(1)} %get-tuple-element.144), channel_id=1, source_target_pairs={{2,32},{6,96},{32,2},{36,66},{66,36},{70,100},{96,6},{100,70},{3,3... | collective-permute-start | bytes 614408 | tf_op jit(solution)/shard_map/ppermute | solution.py:449
  110.5 4.8 %collective-permute-start.24 = (bf16[160,640]{1,0:T(8,128)(2,1)S(1)}, bf16[160,640]{1,0:T(8,128)(2,1)S(1)}, u32[]{:S(2)}, u32[]{:S(2)}) collective-permute-start(bf16[160,640]{1,0:T(8,128)(2,1)S(1)} %get-tuple-element.148), channel_id=1, source_target_pairs={{2,32},{6,96},{32,2},{36,66},{66,36},{70,100},{96,6},{100,70},{3,3... | collective-permute-start | bytes 614408 | tf_op jit(solution)/shard_map/ppermute | solution.py:453
  117.9 3.2 %collective-permute-start.26 = (bf16[320,640]{1,0:T(8,128)(2,1)S(1)}, bf16[320,640]{1,0:T(8,128)(2,1)S(1)}, u32[]{:S(2)}, u32[]{:S(2)}) collective-permute-start(bf16[320,640]{1,0:T(8,128)(2,1)S(1)} %get-tuple-element.150), channel_id=1, source_target_pairs={{1,16},{16,1},{3,18},{18,3},{5,20},{20,5},{7,22},{22,7},{9,24},{24... | collective-permute-start | bytes 1228808 | tf_op jit(solution)/shard_map/ppermute | solution.py:458
  121.1 7.3 %collective-permute-done.24.mirror_last = bf16[160,640]{1,0:T(8,128)(2,1)S(1)} collective-permute-done((bf16[160,640]{1,0:T(8,128)(2,1)S(1)}, bf16[160,640]{1,0:T(8,128)(2,1)S(1)}, u32[]{:S(2)}, u32[]{:S(2)}) %collective-permute-start.24) | collective-permute-done | bytes 204832 | tf_op jit(solution)/shard_map/ppermute | solution.py:453
  129.3 2.0 %collective-permute-done.26.across = bf16[320,640]{1,0:T(8,128)(2,1)S(1)} collective-permute-done((bf16[320,640]{1,0:T(8,128)(2,1)S(1)}, bf16[320,640]{1,0:T(8,128)(2,1)S(1)}, u32[]{:S(2)}, u32[]{:S(2)}) %collective-permute-start.26) | collective-permute-done | bytes 409632 | tf_op jit(solution)/shard_map/ppermute | solution.py:458
  131.3 1.5 %finish_kernel.1 = f32[320,640]{1,0:T(8,128)} custom-call(s32[6]{0:T(128)S(1)} %stack.31.where, f32[320,640]{1,0:T(8,128)S(1)} %base_kernel.1.base, bf16[320,640]{1,0:T(8,128)(2,1)S(1)} %collective-permute-done.26.across), custom_call_target="tpu_custom_call" | custom-call | flops 1 | bytes 1 | tf_op jit(solution)/shard_map/finish_kernel/pallas_call | solution.py:323
  (60 shorter events, 18.4 us)
Async XLA Ops:
  0.6 14.7 %copy-start = (bf16[1536,640]{1,0:T(8,128)(2,1)S(1)}, bf16[1536,640]{1,0:T(8,128)(2,1)}, u32[]{:S(2)}) copy-start(bf16[1536,640]{1,0:T(8,128)(2,1)} %rows.1) | copy-start | bytes 5898244
  0.6 7.5 %copy-start.5 = (f32[1536]{0:T(1024)S(1)}, f32[1536]{0:T(1024)}, u32[]{:S(2)}) copy-start(f32[1536]{0:T(1024)} %param.7) | copy-start | bytes 18436
  0.7 7.5 %copy-start.6 = (s32[1536]{0:T(1024)S(1)}, s32[1536]{0:T(1024)}, u32[]{:S(2)}) copy-start(s32[1536]{0:T(1024)} %param.8) | copy-start | bytes 18436
  0.7 7.6 %copy-start.4 = (f32[16,1536]{1,0:T(8,128)S(1)}, f32[16,1536]{1,0:T(8,128)}, u32[]{:S(2)}) copy-start(f32[16,1536]{1,0:T(8,128)} %param.6) | copy-start | bytes 294916
  3.8 23.8 %collective-permute-start.1 = (bf16[768,640]{1,0:T(8,128)(2,1)}, bf16[768,640]{1,0:T(8,128)(2,1)}, u32[]{:S(2)}, u32[]{:S(2)}) collective-permute-start(bf16[768,640]{1,0:T(8,128)(2,1)} %get-tuple-element.91), channel_id=1, source_target_pairs={{0,2},{2,4},{4,6},{6,0},{1,3},{3,5},{5,7},{7,1},{8,10},{10,12},{12... | collective-permute-start | bytes 2949128 | tf_op jit(solution)/shard_map/ppermute | solution.py:352
  4.3 25.0 %collective-permute-start.2 = (bf16[768,640]{1,0:T(8,128)(2,1)}, bf16[768,640]{1,0:T(8,128)(2,1)}, u32[]{:S(2)}, u32[]{:S(2)}) collective-permute-start(bf16[768,640]{1,0:T(8,128)(2,1)} %get-tuple-element.153), channel_id=1, source_target_pairs={{0,1},{1,0},{2,3},{3,2},{4,5},{5,4},{6,7},{7,6},{8,9},{9,8},{10,11... | collective-permute-start | bytes 2949128 | tf_op jit(solution)/shard_map/ppermute | solution.py:353
  6.6 24.5 %collective-permute-start = (bf16[768,640]{1,0:T(8,128)(2,1)}, bf16[768,640]{1,0:T(8,128)(2,1)}, u32[]{:S(2)}, u32[]{:S(2)}) collective-permute-start(bf16[768,640]{1,0:T(8,128)(2,1)} %get-tuple-element.153), channel_id=1, source_target_pairs={{0,6},{2,0},{4,2},{6,4},{1,7},{3,1},{5,3},{7,5},{8,14},{10,8},{12,... | collective-permute-start | bytes 2949128 | tf_op jit(solution)/shard_map/ppermute | solution.py:351
  15.4 0.7 copy-start.2
  19.9 1.9 %collective-permute-start.3 = (bf16[336,640]{1,0:T(8,128)(2,1)S(1)}, bf16[336,640]{1,0:T(8,128)(2,1)S(1)}, u32[]{:S(2)}, u32[]{:S(2)}) collective-permute-start(bf16[336,640]{1,0:T(8,128)(2,1)S(1)} %get-tuple-element.82), channel_id=1, source_target_pairs={{0,8},{8,0},{1,9},{9,1},{2,10},{10,2},{3,11},{11,3},{4,12},{12,4},... | collective-permute-start | bytes 1290248 | tf_op jit(solution)/shard_map/ppermute | solution.py:367
  31.0 23.7 %collective-permute-start.5 = (bf16[768,640]{1,0:T(8,128)(2,1)}, bf16[768,640]{1,0:T(8,128)(2,1)S(1)}, u32[]{:S(2)}, u32[]{:S(2)}) collective-permute-start(bf16[768,640]{1,0:T(8,128)(2,1)} %get-tuple-element.91), channel_id=1, source_target_pairs={{0,1},{1,0},{2,3},{3,2},{4,5},{5,4},{6,7},{7,6},{8,9},{9,8},{10,11... | collective-permute-start | bytes 2949128 | tf_op jit(solution)/shard_map/ppermute | solution.py:372
  36.7 3.4 %collective-permute-start.4 = (bf16[2,320,640]{2,1,0:T(8,128)(2,1)S(1)}, bf16[2,320,640]{2,1,0:T(8,128)(2,1)S(1)}, u32[]{:S(2)}, u32[]{:S(2)}) collective-permute-start(bf16[2,320,640]{2,1,0:T(8,128)(2,1)S(1)} %get-tuple-element.89), channel_id=1, source_target_pairs={{0,8},{8,0},{1,9},{9,1},{2,10},{10,2},{3,11},{11,3},{4,12},{12,4},... | collective-permute-start | bytes 2457608 | tf_op jit(solution)/shard_map/ppermute | solution.py:383
  36.8 26.9 %collective-permute-start.6 = (bf16[768,640]{1,0:T(8,128)(2,1)}, bf16[768,640]{1,0:T(8,128)(2,1)S(1)}, u32[]{:S(2)}, u32[]{:S(2)}) collective-permute-start(bf16[768,640]{1,0:T(8,128)(2,1)} %collective-permute-done.above), channel_id=1, source_target_pairs={{0,6},{2,0},{4,2},{6,4},{1,7},{3,1},{5,3},{7,5},{8,14},{10,8},{12,... | collective-permute-start | bytes 2949128 | tf_op jit(solution)/shard_map/ppermute | solution.py:373
  37.8 25.9 %collective-permute-start.7 = (bf16[768,640]{1,0:T(8,128)(2,1)}, bf16[768,640]{1,0:T(8,128)(2,1)S(1)}, u32[]{:S(2)}, u32[]{:S(2)}) collective-permute-start(bf16[768,640]{1,0:T(8,128)(2,1)} %collective-permute-done.1.below), channel_id=1, source_target_pairs={{0,2},{2,4},{4,6},{6,0},{1,3},{3,5},{5,7},{7,1},{8,10},{10,12},{12... | collective-permute-start | bytes 2949128 | tf_op jit(solution)/shard_map/ppermute | solution.py:374
  41.2 22.5 %collective-permute-start.8 = (bf16[320,640]{1,0:T(8,128)(2,1)S(1)}, bf16[320,640]{1,0:T(8,128)(2,1)S(1)}, u32[]{:S(2)}, u32[]{:S(2)}) collective-permute-start(bf16[320,640]{1,0:T(8,128)(2,1)S(1)} %get-tuple-element.98), channel_id=1, source_target_pairs={{0,32},{2,34},{4,36},{34,66},{36,68},{38,70},{64,96},{68,100},{70,... | collective-permute-start | bytes 1228808 | tf_op jit(solution)/shard_map/ppermute | solution.py:392
  42.5 24.1 %collective-permute-start.9 = (bf16[320,640]{1,0:T(8,128)(2,1)S(1)}, bf16[320,640]{1,0:T(8,128)(2,1)S(1)}, u32[]{:S(2)}, u32[]{:S(2)}) collective-permute-start(bf16[320,640]{1,0:T(8,128)(2,1)S(1)} %get-tuple-element.99), channel_id=1, source_target_pairs={{2,66},{4,68},{6,70},{32,96},{36,100},{38,102},{64,0},{66,2},{70,6... | collective-permute-start | bytes 1228808 | tf_op jit(solution)/shard_map/ppermute | solution.py:392
  54.8 13.1 %collective-permute-start.10 = (bf16[320,640]{1,0:T(8,128)(2,1)S(1)}, bf16[320,640]{1,0:T(8,128)(2,1)S(1)}, u32[]{:S(2)}, u32[]{:S(2)}) collective-permute-start(bf16[320,640]{1,0:T(8,128)(2,1)S(1)} %get-tuple-element.100), channel_id=1, source_target_pairs={{0,96},{4,100},{6,102},{32,0},{34,2},{38,6},{64,32},{66,34},{68,36... | collective-permute-start | bytes 1228808 | tf_op jit(solution)/shard_map/ppermute | solution.py:392
  73.4 3.8 %collective-permute-start.11 = (bf16[4,160,640]{2,1,0:T(8,128)(2,1)S(1)}, bf16[4,160,640]{2,1,0:T(8,128)(2,1)S(1)}, u32[]{:S(2)}, u32[]{:S(2)}) collective-permute-start(bf16[4,160,640]{2,1,0:T(8,128)(2,1)S(1)} %get-tuple-element.118), channel_id=1, source_target_pairs={{0,8},{8,0},{1,9},{9,1},{2,10},{10,2},{3,11},{11,3},{4,12},{12,4},... | collective-permute-start | bytes 2457608 | tf_op jit(solution)/shard_map/ppermute | solution.py:413
  77.3 6.5 %collective-permute-start.12 = (bf16[4,160,640]{2,1,0:T(8,128)(2,1)S(1)}, bf16[4,160,640]{2,1,0:T(8,128)(2,1)S(1)}, u32[]{:S(2)}, u32[]{:S(2)}) collective-permute-start(bf16[4,160,640]{2,1,0:T(8,128)(2,1)S(1)} %get-tuple-element.120), channel_id=1, source_target_pairs={{0,8},{8,0},{1,9},{9,1},{2,10},{10,2},{3,11},{11,3},{4,12},{12,4},... | collective-permute-start | bytes 2457608 | tf_op jit(solution)/shard_map/ppermute | solution.py:421
  78.6 9.1 %collective-permute-start.18 = (bf16[176,640]{1,0:T(8,128)(2,1)S(1)}, bf16[176,640]{1,0:T(8,128)(2,1)S(1)}, u32[]{:S(2)}, u32[]{:S(2)}) collective-permute-start(bf16[176,640]{1,0:T(8,128)(2,1)S(1)} %get-tuple-element.134), channel_id=1, source_target_pairs={{0,32},{32,64},{64,96},{96,0},{1,33},{33,65},{65,97},{97,1},{2,34}... | collective-permute-start | bytes 675848 | tf_op jit(solution)/shard_map/ppermute | solution.py:430
  78.7 16.0 %collective-permute-start.19 = (bf16[176,640]{1,0:T(8,128)(2,1)S(1)}, bf16[176,640]{1,0:T(8,128)(2,1)S(1)}, u32[]{:S(2)}, u32[]{:S(2)}) collective-permute-start(bf16[176,640]{1,0:T(8,128)(2,1)S(1)} %get-tuple-element.135), channel_id=1, source_target_pairs={{0,64},{32,96},{64,0},{96,32},{1,65},{33,97},{65,1},{97,33},{2,66}... | collective-permute-start | bytes 675848 | tf_op jit(solution)/shard_map/ppermute | solution.py:430
  83.4 11.2 %collective-permute-start.20 = (bf16[176,640]{1,0:T(8,128)(2,1)S(1)}, bf16[176,640]{1,0:T(8,128)(2,1)S(1)}, u32[]{:S(2)}, u32[]{:S(2)}) collective-permute-start(bf16[176,640]{1,0:T(8,128)(2,1)S(1)} %get-tuple-element.136), channel_id=1, source_target_pairs={{0,96},{32,0},{64,32},{96,64},{1,97},{33,1},{65,33},{97,65},{2,98}... | collective-permute-start | bytes 675848 | tf_op jit(solution)/shard_map/ppermute | solution.py:430
  84.5 12.5 %collective-permute-start.14 = (bf16[160,640]{1,0:T(8,128)(2,1)S(1)}, bf16[160,640]{1,0:T(8,128)(2,1)S(1)}, u32[]{:S(2)}, u32[]{:S(2)}) collective-permute-start(bf16[160,640]{1,0:T(8,128)(2,1)S(1)} %get-tuple-element.126), channel_id=1, source_target_pairs={{0,32},{32,64},{64,96},{96,0},{1,33},{33,65},{65,97},{97,1},{2,34}... | collective-permute-start | bytes 614408 | tf_op jit(solution)/shard_map/ppermute | solution.py:430
  86.6 15.9 %collective-permute-start.15 = (bf16[160,640]{1,0:T(8,128)(2,1)S(1)}, bf16[160,640]{1,0:T(8,128)(2,1)S(1)}, u32[]{:S(2)}, u32[]{:S(2)}) collective-permute-start(bf16[160,640]{1,0:T(8,128)(2,1)S(1)} %get-tuple-element.127), channel_id=1, source_target_pairs={{0,64},{32,96},{64,0},{96,32},{1,65},{33,97},{65,1},{97,33},{2,66}... | collective-permute-start | bytes 614408 | tf_op jit(solution)/shard_map/ppermute | solution.py:430
  87.6 16.7 %collective-permute-start.13 = (bf16[320,640]{1,0:T(8,128)(2,1)S(1)}, bf16[320,640]{1,0:T(8,128)(2,1)S(1)}, u32[]{:S(2)}, u32[]{:S(2)}) collective-permute-start(bf16[320,640]{1,0:T(8,128)(2,1)S(1)} %get-tuple-element.124), channel_id=1, source_target_pairs={{1,17},{16,0},{3,19},{18,2},{5,21},{20,4},{7,23},{22,6},{9,25},{24... | collective-permute-start | bytes 1228808 | tf_op jit(solution)/shard_map/ppermute | solution.py:431
  94.6 7.8 %collective-permute-start.16 = (bf16[160,640]{1,0:T(8,128)(2,1)S(1)}, bf16[160,640]{1,0:T(8,128)(2,1)S(1)}, u32[]{:S(2)}, u32[]{:S(2)}) collective-permute-start(bf16[160,640]{1,0:T(8,128)(2,1)S(1)} %get-tuple-element.128), channel_id=1, source_target_pairs={{0,96},{32,0},{64,32},{96,64},{1,97},{33,1},{65,33},{97,65},{2,98}... | collective-permute-start | bytes 614408 | tf_op jit(solution)/shard_map/ppermute | solution.py:430
  95.4 8.9 %collective-permute-start.21 = (bf16[176,640]{1,0:T(8,128)(2,1)S(1)}, bf16[176,640]{1,0:T(8,128)(2,1)S(1)}, u32[]{:S(2)}, u32[]{:S(2)}) collective-permute-start(bf16[176,640]{1,0:T(8,128)(2,1)S(1)} %get-tuple-element.138), channel_id=1, source_target_pairs={{0,16},{16,0},{1,17},{17,1},{2,18},{18,2},{3,19},{19,3},{4,20},{20... | collective-permute-start | bytes 675848 | tf_op jit(solution)/shard_map/ppermute | solution.py:441
  103.2 6.2 %collective-permute-start.17 = (bf16[160,640]{1,0:T(8,128)(2,1)S(1)}, bf16[160,640]{1,0:T(8,128)(2,1)S(1)}, u32[]{:S(2)}, u32[]{:S(2)}) collective-permute-start(bf16[160,640]{1,0:T(8,128)(2,1)S(1)} %get-tuple-element.130), channel_id=1, source_target_pairs={{0,16},{16,0},{1,17},{17,1},{2,18},{18,2},{3,19},{19,3},{4,20},{20... | collective-permute-start | bytes 614408 | tf_op jit(solution)/shard_map/ppermute | solution.py:441
  105.1 11.5 %collective-permute-start.23 = (bf16[160,640]{1,0:T(8,128)(2,1)S(1)}, bf16[160,640]{1,0:T(8,128)(2,1)S(1)}, u32[]{:S(2)}, u32[]{:S(2)}) collective-permute-start(bf16[160,640]{1,0:T(8,128)(2,1)S(1)} %get-tuple-element.144), channel_id=1, source_target_pairs={{2,32},{6,96},{32,2},{36,66},{66,36},{70,100},{96,6},{100,70},{3,3... | collective-permute-start | bytes 614408 | tf_op jit(solution)/shard_map/ppermute | solution.py:449
  110.4 6.2 %collective-permute-start.22 = (bf16[320,320]{1,0:T(8,128)(2,1)S(1)}, bf16[320,320]{1,0:T(8,128)(2,1)S(1)}, u32[]{:S(2)}, u32[]{:S(2)}) collective-permute-start(bf16[320,320]{1,0:T(8,128)(2,1)S(1)} %get-tuple-element.143), channel_id=1, source_target_pairs={{0,8},{8,0},{1,9},{9,1},{2,10},{10,2},{3,11},{11,3},{4,12},{12,4},... | collective-permute-start | bytes 614408 | tf_op jit(solution)/shard_map/ppermute | solution.py:455
  110.5 17.9 %collective-permute-start.24 = (bf16[160,640]{1,0:T(8,128)(2,1)S(1)}, bf16[160,640]{1,0:T(8,128)(2,1)S(1)}, u32[]{:S(2)}, u32[]{:S(2)}) collective-permute-start(bf16[160,640]{1,0:T(8,128)(2,1)S(1)} %get-tuple-element.148), channel_id=1, source_target_pairs={{2,32},{6,96},{32,2},{36,66},{66,36},{70,100},{96,6},{100,70},{3,3... | collective-permute-start | bytes 614408 | tf_op jit(solution)/shard_map/ppermute | solution.py:453
  115.3 13.1 %collective-permute-start.25 = (bf16[320,320]{1,0:T(8,128)(2,1)S(1)}, bf16[320,320]{1,0:T(8,128)(2,1)S(1)}, u32[]{:S(2)}, u32[]{:S(2)}) collective-permute-start(bf16[320,320]{1,0:T(8,128)(2,1)S(1)} %get-tuple-element.149), channel_id=1, source_target_pairs={{4,64},{38,98},{64,4},{98,38},{5,65},{39,99},{65,5},{99,39},{12,72... | collective-permute-start | bytes 614408 | tf_op jit(solution)/shard_map/ppermute | solution.py:454
  117.9 13.5 %collective-permute-start.26 = (bf16[320,640]{1,0:T(8,128)(2,1)S(1)}, bf16[320,640]{1,0:T(8,128)(2,1)S(1)}, u32[]{:S(2)}, u32[]{:S(2)}) collective-permute-start(bf16[320,640]{1,0:T(8,128)(2,1)S(1)} %get-tuple-element.150), channel_id=1, source_target_pairs={{1,16},{16,1},{3,18},{18,3},{5,20},{20,5},{7,22},{22,7},{9,24},{24... | collective-permute-start | bytes 1228808 | tf_op jit(solution)/shard_map/ppermute | solution.py:458
  (2 other events, 1.3 us)
